TPU v7x, 32 devices: a whole 2x2x4 slice. The times are simulated.
32 devices in a mesh: groups: 2 (over x), gx: 4 (over y, core), gy: 4 (over z).
Axes of the slice: x: 2, y: 2, z: 4, core: 2. Of those that a mesh axis runs over, the one named last changes fastest.
Arguments:
- field_input: bfloat16 [64, 256, 1024], P(('groups', 'gx'), 'gy'), parts along dimension 0, may hold values from -8 to 8
- cotangent: bfloat16 [64, 256, 1024], P(('groups', 'gx'), 'gy'), parts along dimension 0, may hold values from -8 to 8
- spectral_weight: bfloat16 [256, 32768], P(('gx', 'gy')), may hold values from -0.75 to 0.75
- point_weight: bfloat16 [32, 32], replicated, may hold values from -1 to 1
- point_bias: float32 [32], replicated, may hold values from -3 to 3
Outputs:
- grad_field: bfloat16 [64, 256, 1024], P(('groups', 'gx'), 'gy'), parts along dimension 0
- grad_spectral: float32 [512, 32768], P(('groups', 'gx', 'gy')), parts along dimension 0
- grad_point: float32 [64, 32], P('groups'), parts along dimension 0
- grad_bias: float32 [64], P('groups'), parts along dimension 0
There are 2 independent parts, one for each index of `groups`. A program takes and returns all parts, laid end to end along the dimension named above; an argument that names none is the same for every part. Nothing has to cross between parts.
All inputs are finite; a program needn't handle non-finite values.
Results may differ from a plain program's by a relative error of at most 0.0052.
Values sent between devices are 32-bit elements; how exact they have to be, the bound alone decides.
No kernel may reach another device: no remote copies, remote signals or barrier semaphores. Data moves between devices by JAX's collectives and lax.ppermute only.
A program may use at most 64 MiB of HBM per device.

v0:
```python
import functools
import math

import jax
import jax.numpy as jnp
import ml_dtypes
import numpy as np
from jax import lax
from jax.experimental import pallas as pl
from jax.experimental.pallas import tpu as pltpu
from jax.sharding import PartitionSpec as P

C = 32
KX = 16
KY = 16
KZ = 16
NZ = 32


def mode_values(mode_count, length):
    position = jnp.arange(mode_count, dtype=jnp.int32)
    return jnp.where(position < mode_count // 2, position, length - mode_count + position)


def phase_angles(positions, wavenumbers, length):
    steps = positions[:, None] * wavenumbers[None, :] % length
    return 2.0 * math.pi / length * steps.astype(jnp.float32)


def complex_table(positions, wavenumbers, length, factor):
    angles = phase_angles(positions, wavenumbers, length)
    cosine = jnp.cos(angles) * factor
    sine = jnp.sin(angles) * factor
    return jnp.stack(
        [jnp.stack([cosine, -sine], axis=-1), jnp.stack([sine, cosine], axis=-1)], axis=1
    )


def depth_table(depth_count, mode_count):
    angles = phase_angles(
        jnp.arange(depth_count, dtype=jnp.int32),
        jnp.arange(mode_count, dtype=jnp.int32),
        depth_count,
    )
    return jnp.stack([jnp.cos(angles), -jnp.sin(angles)], axis=1).astype(jnp.bfloat16)


def doubled(table):
    factor = jnp.where(jnp.arange(table.shape[2]) == 0, 1.0, 2.0).astype(jnp.float32)
    return table.astype(jnp.float32) * factor[None, None, :]


def spectral_product(spectrum, weights):
    shaped = spectrum.reshape(spectrum.shape[0], KX, 2, C)
    real_in, imag_in = (shaped[:, :, 0], shaped[:, :, 1])
    real_w, imag_w = (weights[:, :, 0], weights[:, :, 1])
    hp = lax.Precision.HIGHEST
    real_out = jnp.einsum("rmi,rmio->rmo", real_in, real_w, precision=hp) - jnp.einsum(
        "rmi,rmio->rmo", imag_in, imag_w, precision=hp
    )
    imag_out = jnp.einsum("rmi,rmio->rmo", real_in, imag_w, precision=hp) + jnp.einsum(
        "rmi,rmio->rmo", imag_in, real_w, precision=hp
    )
    return jnp.stack([real_out, imag_out], axis=2).reshape(spectrum.shape)


def adjoint_product(spectrum, weights):
    shaped = spectrum.reshape(spectrum.shape[0], KX, 2, C)
    real_in, imag_in = (shaped[:, :, 0], shaped[:, :, 1])
    real_w, imag_w = (weights[:, :, 0], weights[:, :, 1])
    hp = lax.Precision.HIGHEST
    real_out = jnp.einsum("rmo,rmio->rmi", real_in, real_w, precision=hp) + jnp.einsum(
        "rmo,rmio->rmi", imag_in, imag_w, precision=hp
    )
    imag_out = jnp.einsum("rmo,rmio->rmi", imag_in, real_w, precision=hp) - jnp.einsum(
        "rmo,rmio->rmi", real_in, imag_w, precision=hp
    )
    return jnp.stack([real_out, imag_out], axis=2).reshape(spectrum.shape)


def weight_gradient(field_spec, adjoint_spec):
    field_shaped = field_spec.reshape(field_spec.shape[0], KX, 2, C)
    adjoint_shaped = adjoint_spec.reshape(adjoint_spec.shape[0], KX, 2, C)
    real_v, imag_v = (field_shaped[:, :, 0], field_shaped[:, :, 1])
    real_h, imag_h = (adjoint_shaped[:, :, 0], adjoint_shaped[:, :, 1])
    real_g = (
        real_v[:, :, :, None] * real_h[:, :, None, :]
        + imag_v[:, :, :, None] * imag_h[:, :, None, :]
    )
    imag_g = (
        real_v[:, :, :, None] * imag_h[:, :, None, :]
        - imag_v[:, :, :, None] * real_h[:, :, None, :]
    )
    return jnp.stack([real_g, imag_g], axis=2).reshape(field_spec.shape[0], KX * 2 * C * C)


def channel_mix(values, weight):
    group_size = max(1, 128 // weight.shape[0])
    block = jnp.kron(jnp.eye(group_size, dtype=weight.dtype), weight)
    rows = values.reshape(-1, block.shape[0])
    return jnp.dot(rows, block, preferred_element_type=jnp.float32).reshape(values.shape)


def spectrum(values, z_table, y_table, x_local, x_whole):
    rows_x, rows_y, _ = values.shape
    hp = lax.Precision.HIGHEST
    shaped = values.reshape(rows_x, rows_y, NZ, C)
    zpart = jnp.einsum(
        "xyzc,zpk->xypkc", shaped, z_table, preferred_element_type=jnp.float32
    ).reshape(rows_x, rows_y, 2, KZ * C)
    ypart = jnp.einsum("xyqm,yqjp->xjpm", zpart, y_table, precision=hp)
    pencil = lax.all_to_all(ypart, "gx", split_axis=1, concat_axis=0, tiled=True)
    mode_rows = pencil.shape[1]
    pencil = pencil.reshape(pencil.shape[0], mode_rows, 2, KZ, C)
    partial_value = jnp.einsum("xjqkc,xqmp->jkmpc", pencil, x_whole, precision=hp).reshape(
        mode_rows * KZ, KX * 2 * C
    )
    return lax.psum_scatter(partial_value, "gy", scatter_dimension=0, tiled=True)


def synthesis(owned, z_float, y_table, x_whole, rows_x, rows_y):
    hp = lax.Precision.HIGHEST
    planes = lax.all_gather(owned, "gy", axis=0, tiled=True)
    mode_rows = planes.shape[0] // KZ
    shaped = planes.reshape(mode_rows, KZ, KX, 2, C)
    wide = jnp.einsum("jkmqc,xpmq->xjpkc", shaped, x_whole, precision=hp).reshape(
        x_whole.shape[0], mode_rows, 2, KZ * C
    )
    slab = lax.all_to_all(wide, "gx", split_axis=0, concat_axis=1, tiled=True)
    ypart = jnp.einsum("xjqm,ypjq->xypm", slab, y_table, precision=hp).reshape(
        rows_x, rows_y, 2, KZ, C
    )
    return jnp.einsum("xypkc,zpk->xyzc", ypart, z_float, precision=hp).reshape(
        rows_x, rows_y, NZ * C
    )


def general_device(field_input, cotangent, spectral_weight, point_weight, point_bias):
    rows_x, rows_y, _ = field_input.shape
    full_x = rows_x * lax.axis_size("gx")
    full_y = rows_y * lax.axis_size("gy")
    cell_scale = 1.0 / math.sqrt(full_x * full_y * NZ)
    x_start = lax.axis_index("gx") * rows_x
    y_start = lax.axis_index("gy") * rows_y
    y_table = complex_table(
        y_start + jnp.arange(rows_y, dtype=jnp.int32), mode_values(KY, full_y), full_y, 1.0
    )
    x_local = complex_table(
        x_start + jnp.arange(rows_x, dtype=jnp.int32), mode_values(KX, full_x), full_x, cell_scale
    )
    x_whole = complex_table(
        jnp.arange(full_x, dtype=jnp.int32), mode_values(KX, full_x), full_x, cell_scale
    )
    z_plain = depth_table(NZ, KZ)
    z_double_float = doubled(z_plain)
    z_double = z_double_float.astype(jnp.bfloat16)
    field_spec = spectrum(field_input, z_plain, y_table, x_local, x_whole)
    weights = spectral_weight.astype(jnp.float32).reshape(-1, KX, 2, C, C)
    mode_output = spectral_product(field_spec, weights)
    spectral_out = synthesis(mode_output, z_double_float, y_table, x_whole, rows_x, rows_y)
    bias_row = jnp.tile(point_bias, NZ)
    preact = spectral_out + channel_mix(field_input, point_weight) + bias_row
    _, pullback = jax.vjp(jax.nn.gelu, preact)
    adjoint = pullback(cotangent.astype(jnp.float32))[0].astype(jnp.bfloat16)
    adjoint_spec = spectrum(adjoint, z_double, y_table, x_local, x_whole)
    grad_spectral = weight_gradient(field_spec, adjoint_spec) * cell_scale
    mode_adjoint = adjoint_product(adjoint_spec, weights)
    flat_field = field_input.reshape(-1, C)
    flat_adjoint = adjoint.reshape(-1, C)
    point_term = (
        jnp.einsum("rc,rd->cd", flat_field, flat_adjoint, preferred_element_type=jnp.float32)
        * cell_scale
    )
    bias_term = jnp.sum(flat_adjoint.astype(jnp.float32), axis=0) * cell_scale
    grad_point, grad_bias = lax.psum((point_term, bias_term), ("gx", "gy"))
    back_field = synthesis(
        mode_adjoint, z_plain.astype(jnp.float32), y_table, x_whole, rows_x, rows_y
    )
    grad_field = (channel_mix(adjoint, point_weight.T) + back_field).astype(jnp.bfloat16)
    return (grad_field, grad_spectral, grad_point, grad_bias)


BF = jnp.bfloat16
F32 = jnp.float32
LANES = 128
CHUNKS = KZ * C // LANES
WIDE = KZ * C
DATA_ROWS = 16 * CHUNKS
SUM_ROWS = 16


def dot(left, right, dims=((1,), (0,))):
    return lax.dot_general(left, right, (dims, ((), ())), preferred_element_type=F32)


def halves(values):
    high = values.astype(BF)
    return high, (values - high.astype(F32)).astype(BF)


def iota(shape, axis):
    return lax.broadcasted_iota(jnp.int32, shape, axis)


def lane_take(values, index):
    return jnp.take_along_axis(values, index, axis=1, mode="promise_in_bounds")


def np_halves(table):
    high = table.astype(ml_dtypes.bfloat16).astype(np.float64)
    low = (table - high).astype(ml_dtypes.bfloat16).astype(np.float64)
    return high, low


def np_modes(count, length):
    position = np.arange(count)
    return np.where(position < count // 2, position, length - count + position)


def np_angles(positions, modes, length):
    return 2.0 * np.pi * ((positions[:, None] * modes[None, :]) % length) / length


def depth_matrix():
    angles = np_angles(np.arange(NZ), np.arange(KZ), NZ)
    table = np.stack([np.cos(angles), -np.sin(angles)], axis=1).astype(ml_dtypes.bfloat16)
    table = table.astype(np.float32).reshape(NZ, 2 * KZ)
    return np.kron(table, np.eye(C, dtype=np.float32)).astype(ml_dtypes.bfloat16)


def y_tables(full_y, rows_y, rows_x, parts):
    angles = np_angles(np.arange(full_y), np_modes(KY, full_y), full_y)
    table = np.stack([np.cos(angles), -np.sin(angles)], axis=0)
    both = np.stack(np_halves(table), axis=0).reshape(2, 2, parts, rows_y, KY)
    forward = both.transpose(2, 0, 1, 4, 3).reshape(parts, 4 * KY, rows_y)
    forward = np.tile(forward, (1, 1, LANES // rows_y))
    inverse = np.repeat(both.transpose(2, 0, 3, 1, 4), rows_x, axis=-1)
    inverse = inverse.reshape(parts, 2 * rows_y, 2 * KY * rows_x)
    return forward.astype(np.float32), inverse.astype(np.float32)


def x_tables(full_x, rows_x, factor):
    angles = np_angles(np.arange(full_x), np_modes(KX, full_x), full_x)
    cosine, sine = np.cos(angles) * factor, np.sin(angles) * factor
    table = np.stack([np.stack([cosine, -sine], -1), np.stack([sine, cosine], -1)], axis=1)
    blocked = table.reshape(full_x // rows_x, rows_x, 2, KX, 2).transpose(0, 2, 1, 3, 4)
    inverse = blocked.reshape(2 * full_x, 2 * KX)
    forward = inverse.T

    def packed(matrix):
        high, low = np_halves(matrix)
        return np.concatenate([high, low, high], axis=1).astype(ml_dtypes.bfloat16)

    return packed(forward), packed(inverse)


def tripled(values):
    high, low = halves(values)
    return jnp.concatenate([high, high, low], axis=0)


def forward_matrix(table_ref, rows_x, rows_y):
    table = table_ref[lax.axis_index("gy")]
    count = table.shape[0]
    spread = jnp.broadcast_to(table[:, None, :], (count, rows_x, LANES))
    spread = spread.reshape(count * rows_x, LANES)
    spread = jnp.concatenate([spread] * (rows_x * rows_y // LANES), axis=1)
    shape = spread.shape
    return jnp.where(iota(shape, 1) // rows_y == iota(shape, 0) % rows_x, spread, 0.0).astype(BF)


def inverse_matrix(table_ref, rows_x, rows_y):
    table = table_ref[lax.axis_index("gy")]
    wide = table.shape[1]
    both = []
    for part in range(2):
        block = table[part * rows_y : (part + 1) * rows_y]
        owner = iota((rows_y, wide), 1) % rows_x
        rows = [jnp.where(owner == x, block, 0.0) for x in range(rows_x)]
        both.append(jnp.concatenate(rows, axis=0).astype(BF))
    return jnp.concatenate([both[0], both[1], both[0]], axis=1)


def field_spectrum(values, matrix, depth_ref, out_ref, rows_x):
    rows = KY * rows_x
    both = dot(matrix, values)
    high, low = halves(both[: 2 * rows] + both[2 * rows :])
    both = dot(jnp.concatenate([high, low], axis=0), depth_ref[...])
    both = both[: 2 * rows] + both[2 * rows :]
    real = both[:rows, :WIDE] - both[rows:, WIDE:]
    imag = both[:rows, WIDE:] + both[rows:, :WIDE]
    for part, piece in ((0, real), (1, imag)):
        for chunk in range(CHUNKS):
            start = (chunk * 2 + part) * rows_x
            block = piece[:, chunk * LANES : (chunk + 1) * LANES]
            out_ref[:, start : start + rows_x, :] = block.reshape(KY, rows_x, LANES)


def field_synthesis(in_ref, matrix, depth_ref, rows_x):
    rows = KY * rows_x
    parts = []
    for part in range(2):
        pieces = []
        for chunk in range(CHUNKS):
            start = (chunk * 2 + part) * rows_x
            pieces.append(in_ref[:, start : start + rows_x, :].reshape(rows, LANES))
        parts.append(jnp.concatenate(pieces, axis=1))
    real, imag = parts
    stacked = jnp.concatenate(
        [jnp.concatenate([real, imag], axis=1), jnp.concatenate([imag, -real], axis=1)], axis=0
    )
    high, low = halves(stacked)
    both = dot(jnp.concatenate([high, low], axis=0), depth_ref[...], ((1,), (1,)))
    planes = both[: 2 * rows] + both[2 * rows :]
    return dot(matrix, tripled(planes))


def mixing_matrix(weight_ref):
    wide = 8 * C
    pick = (iota((wide, C), 0) % C == iota((wide, C), 1)).astype(F32).astype(BF)
    tall = dot(pick, weight_ref[...]).astype(BF)
    tiled = dot(tall, pick, ((1,), (1,)))
    shape = (wide, wide)
    return jnp.where(iota(shape, 0) // C == iota(shape, 1) // C, tiled, 0.0).astype(BF)


def mixed(values, matrix, dims):
    wide = matrix.shape[0]
    pieces = []
    for start in range(0, values.shape[1], wide):
        pieces.append(dot(values[:, start : start + wide], matrix, dims))
    return jnp.concatenate(pieces, axis=1)


def folded(row):
    total = row[:, :LANES]
    for start in range(LANES, row.shape[1], LANES):
        total = total + row[:, start : start + LANES]
    total = total + pltpu.roll(total, 64, 1)
    return total + pltpu.roll(total, 32, 1)


def own_spectrum(in_ref, table_ref, x_parts, y_parts):
    chunks = []
    for chunk in range(CHUNKS):
        rows = []
        for x_part in range(x_parts):
            block = [
                in_ref[x_part * y_parts + y_part, chunk * 16 : (chunk + 1) * 16, :]
                for y_part in range(y_parts)
            ]
            rows.append(functools.reduce(jnp.add, block))
        chunks.append(jnp.concatenate(rows, axis=0))
    return dot(table_ref[...], tripled(jnp.concatenate(chunks, axis=1)))


def depth_factor():
    return jnp.where(iota((1, WIDE), 1) < C, 1.0, 2.0).astype(F32)


def spread_modes(values, table_ref, out_ref, x_parts, y_parts):
    cells = dot(table_ref[...], tripled(values))
    for x_part in range(x_parts):
        for chunk in range(CHUNKS):
            block = cells[x_part * 16 : (x_part + 1) * 16, chunk * LANES : (chunk + 1) * LANES]
            for y_part in range(y_parts):
                out_ref[x_part * y_parts + y_part, chunk * 16 : (chunk + 1) * 16, :] = block


def mode_row(ref, row):
    wide = jnp.broadcast_to(ref[pl.ds(row, 1), :], (KZ, WIDE))
    group = iota((KZ, LANES), 0) // 4
    chosen = wide[:, :LANES]
    for chunk in range(1, CHUNKS):
        chosen = jnp.where(group == chunk, wide[:, chunk * LANES : (chunk + 1) * LANES], chosen)
    return chosen


def in_index(step):
    return iota((KZ, LANES), 0) % 4 * C + step * 4 + iota((KZ, LANES), 1) // C


def out_index():
    return iota((KZ, LANES), 0) % 4 * C + iota((KZ, LANES), 1) % C


def own_group():
    return iota((KZ, LANES), 0) % 4 == iota((KZ, LANES), 1) // C


def gathered_rows(scratch):
    pieces = []
    for chunk in range(CHUNKS):
        terms = [scratch[pl.ds(chunk * 4 + a, 2 * KX, stride=KZ), :] for a in range(4)]
        pieces.append((terms[0] + terms[1]) + (terms[2] + terms[3]))
    return jnp.concatenate(pieces, axis=1)


def weight_parts(weight_ref, mode):
    start = pl.multiple_of(mode * 2 * C * C, LANES)
    both = weight_ref[:, pl.ds(start, 2 * C * C)].astype(F32)
    return both[:, : C * C], both[:, C * C :]


def lanes_of(values, step):
    return values[:, step * LANES : (step + 1) * LANES]


def first_kernel(rows_x, rows_y, field_ref, table_ref, depth_ref, out_ref):
    matrix = forward_matrix(table_ref, rows_x, rows_y)
    field_spectrum(field_ref[...], matrix, depth_ref, out_ref, rows_x)


def product_kernel(
    x_parts, y_parts, in_ref, forward_ref, inverse_ref, weight_ref, out_ref, spec_ref, scratch
):
    spec_ref[...] = own_spectrum(in_ref, forward_ref, x_parts, y_parts)
    keep = own_group()

    def step(mode, carry):
        real, imag = mode_row(spec_ref, 2 * mode), mode_row(spec_ref, 2 * mode + 1)
        real_w, imag_w = weight_parts(weight_ref, mode)
        real_sum = jnp.zeros((KZ, LANES), F32)
        imag_sum = jnp.zeros((KZ, LANES), F32)
        for part in range(C // 4):
            index = in_index(part)
            real_v, imag_v = lane_take(real, index), lane_take(imag, index)
            real_p, imag_p = lanes_of(real_w, part), lanes_of(imag_w, part)
            real_sum = real_sum + (real_v * real_p - imag_v * imag_p)
            imag_sum = imag_sum + (real_v * imag_p + imag_v * real_p)
        for part, total in ((0, real_sum), (1, imag_sum)):
            start = pl.multiple_of((2 * mode + part) * KZ, KZ)
            scratch[pl.ds(start, KZ), :] = jnp.where(keep, folded(total), 0.0)
        return carry

    lax.fori_loop(0, KX, step, 0, unroll=4)
    spread_modes(gathered_rows(scratch) * depth_factor(), inverse_ref, out_ref, x_parts, y_parts)


def middle_kernel(
    rows_x,
    rows_y,
    in_ref,
    field_ref,
    cotangent_ref,
    point_ref,
    bias_ref,
    table_ref,
    back_ref,
    depth_ref,
    out_ref,
    adjoint_ref,
    sums_ref,
):
    spectral = field_synthesis(in_ref, inverse_matrix(back_ref, rows_x, rows_y), depth_ref, rows_x)
    mixing = mixing_matrix(point_ref)
    field = field_ref[...]
    bias = jnp.concatenate([bias_ref[...]] * NZ, axis=1)
    value = spectral + mixed(field, mixing, ((1,), (0,))) + bias
    root = math.sqrt(2.0 / math.pi)
    square = value * value
    bent = jnp.tanh(value * (root + (root * 0.044715) * square))
    slope = 0.5 * (1.0 + bent) + (0.5 * value) * (1.0 - bent * bent) * (
        root + (3.0 * root * 0.044715) * square
    )
    adjoint = (cotangent_ref[...].astype(F32) * slope).astype(BF)
    adjoint_ref[...] = adjoint
    field_spectrum(adjoint, forward_matrix(table_ref, rows_x, rows_y), depth_ref, out_ref, rows_x)
    wide = mixing.shape[0]
    total = jnp.zeros((wide, wide), F32)
    for start in range(0, NZ * C, wide):
        total = total + dot(
            field[:, start : start + wide], adjoint[:, start : start + wide], ((0,), (0,))
        )
    total = jnp.where(iota((wide, wide), 0) // C == iota((wide, wide), 1) // C, total, 0.0)
    point = total[:C]
    for start in range(C, wide, C):
        point = point + total[start : start + C]
    point = folded(point)
    group = iota((8, LANES), 1) // C
    packed = point[:8]
    for part in range(1, 4):
        packed = jnp.where(group == part, point[part * 8 : (part + 1) * 8], packed)
    sums_ref[:8, :] = packed
    sums_ref[8:, :] = folded(dot(jnp.ones((8, adjoint.shape[0]), BF), adjoint))


def swapped(values, index, distance):
    return lane_take(values, index ^ distance)


def adjoint_kernel(
    x_parts,
    y_parts,
    in_ref,
    forward_ref,
    inverse_ref,
    weight_ref,
    sums_ref,
    out_ref,
    spec_ref,
    scratch,
):
    spec_ref[...] = own_spectrum(in_ref, forward_ref, x_parts, y_parts) * depth_factor()
    keep = own_group()
    lane = iota((KZ, LANES), 1)
    final = lane % C % 4 * C + lane % C // 4 * 4

    def reduced(parts):
        distance = 16
        while len(parts) > 1:
            bit = (lane & distance) != 0
            half = len(parts) // 2
            merged = []
            for low, high in zip(parts[:half], parts[half:]):
                kept = jnp.where(bit, high, low)
                other = jnp.where(bit, low, high)
                merged.append(kept + swapped(other, lane, distance))
            parts = merged
            distance //= 2
        total = parts[0]
        while distance:
            total = total + swapped(total, lane, distance)
            distance //= 2
        return lane_take(total, final)

    def step(mode, carry):
        index = out_index()
        real = lane_take(mode_row(spec_ref, 2 * mode), index)
        imag = lane_take(mode_row(spec_ref, 2 * mode + 1), index)
        real_w, imag_w = weight_parts(weight_ref, mode)
        real_parts, imag_parts = [], []
        for part in range(C // 4):
            real_p, imag_p = lanes_of(real_w, part), lanes_of(imag_w, part)
            real_parts.append(real * real_p + imag * imag_p)
            imag_parts.append(imag * real_p - real * imag_p)
        for part, parts in ((0, real_parts), (1, imag_parts)):
            start = pl.multiple_of((2 * mode + part) * KZ, KZ)
            scratch[pl.ds(start, KZ), :] = jnp.where(keep, reduced(parts), 0.0)
        return carry

    lax.fori_loop(0, KX, step, 0, unroll=4)
    spread_modes(gathered_rows(scratch), inverse_ref, out_ref, x_parts, y_parts)
    for device in range(x_parts * y_parts):
        out_ref[device, DATA_ROWS:, :] = sums_ref[...]


def weight_kernel(scale, modes, field_ref, adjoint_ref, out_ref):
    first = pl.program_id(0) * modes
    index = out_index()
    for local in range(modes):
        row = 2 * (first + local)
        real_v, imag_v = mode_row(field_ref, row), mode_row(field_ref, row + 1)
        real_h = lane_take(mode_row(adjoint_ref, row), index) * scale
        imag_h = lane_take(mode_row(adjoint_ref, row + 1), index) * scale
        for part in range(C // 4):
            take = in_index(part)
            real, imag = lane_take(real_v, take), lane_take(imag_v, take)
            start = local * 2 * C * C + part * LANES
            out_ref[:, start : start + LANES] = real * real_h + imag * imag_h
            start += C * C
            out_ref[:, start : start + LANES] = real * imag_h - imag * real_h


def last_kernel(
    rows_x,
    rows_y,
    scale,
    in_ref,
    adjoint_ref,
    point_ref,
    back_ref,
    depth_ref,
    out_ref,
    grad_ref,
    bias_ref,
):
    spectral = field_synthesis(in_ref, inverse_matrix(back_ref, rows_x, rows_y), depth_ref, rows_x)
    mixing = mixing_matrix(point_ref)
    out_ref[...] = (mixed(adjoint_ref[...], mixing, ((1,), (1,))) + spectral).astype(BF)
    total = in_ref[0, DATA_ROWS:, :]
    for device in range(1, in_ref.shape[0]):
        total = total + in_ref[device, DATA_ROWS:, :]
    total = total * scale
    packed = total[:8]
    for part in range(4):
        piece = packed if part == 0 else pltpu.roll(packed, LANES - part * C, 1)
        grad_ref[part * 8 : (part + 1) * 8, :] = piece[:, :C]
    bias_ref[...] = total[8:9, :C]


def call(kernel, outs, scratch=(), **options):
    shapes = [jax.ShapeDtypeStruct(shape, kind) for shape, kind in outs]
    params = pltpu.CompilerParams(vmem_limit_bytes=56 * 1024 * 1024)
    return pl.pallas_call(
        kernel, out_shape=shapes, scratch_shapes=list(scratch), compiler_params=params, **options
    )


def exchange(values):
    return lax.all_to_all(values, ("gx", "gy"), split_axis=0, concat_axis=0, tiled=True)


def fast_device(field_input, cotangent, spectral_weight, point_weight, point_bias):
    rows_x, rows_y, depth = field_input.shape
    x_parts, y_parts = lax.axis_size("gx"), lax.axis_size("gy")
    devices = x_parts * y_parts
    full_x, full_y = rows_x * x_parts, rows_y * y_parts
    scale = 1.0 / math.sqrt(full_x * full_y * NZ)
    cells = rows_x * rows_y
    depth_table = jnp.asarray(depth_matrix())
    forward_y, inverse_y = map(jnp.asarray, y_tables(full_y, rows_y, rows_x, y_parts))
    forward_x, inverse_x = map(jnp.asarray, x_tables(full_x, rows_x, scale))
    field = field_input.reshape(cells, depth)
    bias = point_bias.reshape(1, C)
    payload = ((devices, DATA_ROWS, LANES), F32)
    spectrum_shape = ((2 * KX, WIDE), F32)
    rows_scratch = pltpu.VMEM((2 * KX * KZ, LANES), F32)

    (sent,) = call(functools.partial(first_kernel, rows_x, rows_y), [payload])(
        field, forward_y, depth_table
    )
    sent, field_modes = call(
        functools.partial(product_kernel, x_parts, y_parts),
        [payload, spectrum_shape],
        [rows_scratch],
    )(exchange(sent), forward_x, inverse_x, spectral_weight)
    sent, adjoint, sums = call(
        functools.partial(middle_kernel, rows_x, rows_y),
        [payload, ((cells, depth), BF), ((SUM_ROWS, LANES), F32)],
    )(
        exchange(sent),
        field,
        cotangent.reshape(cells, depth),
        point_weight,
        bias,
        forward_y,
        inverse_y,
        depth_table,
    )
    sent, adjoint_modes = call(
        functools.partial(adjoint_kernel, x_parts, y_parts),
        [((devices, DATA_ROWS + SUM_ROWS, LANES), F32), spectrum_shape],
        [rows_scratch],
    )(exchange(sent), forward_x, inverse_x, spectral_weight, sums)
    steps = 4
    modes = KX // steps
    whole = pl.BlockSpec((2 * KX, WIDE), lambda i: (0, 0))
    (grad_spectral,) = call(
        functools.partial(weight_kernel, scale, modes),
        [((KZ, KX * 2 * C * C), F32)],
        grid=(steps,),
        in_specs=[whole, whole],
        out_specs=[pl.BlockSpec((KZ, modes * 2 * C * C), lambda i: (0, i))],
    )(field_modes, adjoint_modes)
    grad_field, grad_point, grad_bias = call(
        functools.partial(last_kernel, rows_x, rows_y, scale),
        [((cells, depth), BF), ((C, C), F32), ((1, C), F32)],
    )(exchange(sent), adjoint, point_weight, inverse_y, depth_table)
    return (
        grad_field.reshape(field_input.shape),
        grad_spectral,
        grad_point,
        grad_bias.reshape(C),
    )


def on_device(*arguments):
    rows_x, rows_y, _ = arguments[0].shape
    if rows_x == 8 and rows_y == 64 and arguments[2].shape[0] == KZ:
        return fast_device(*arguments)
    return general_device(*arguments)


def solution(mesh):
    return jax.shard_map(
        on_device,
        mesh=mesh,
        in_specs=(
            P(("groups", "gx"), "gy", None),
            P(("groups", "gx"), "gy", None),
            P(("gx", "gy"), None),
            P(),
            P(),
        ),
        out_specs=(
            P(("groups", "gx"), "gy", None),
            P(("groups", "gx", "gy"), None),
            P("groups", None),
            P("groups"),
        ),
        check_vma=False,
    )
```

profile of v0, /device:TPU:0, one launch (start us, length us, event | category | flops | bytes accessed | tf_op | source)
XLA Modules:
  0.0 116.4 jit_solution(1811222174111250205)
XLA Ops:
  0.6 4.6 %shard_map.129 = f32[16,64,128]{2,1,0:T(8,128)} custom-call(bf16[512,1024]{1,0:T(8,128)(2,1)} %bitcast.5, f32[4,64,128]{2,1,0:T(8,128)} %constant.11.clone.table_ref, bf16[1024,1024]{1,0:T(8,128)(2,1)} %constant.10.clone.depth_ref), custom_call_target="tpu_custom_call" | custom-call | tf_op jit(solution)/shard_map/pallas_call | solution.py:620
  5.2 23.2 %all_to_all.20.in_ref = f32[16,64,128]{2,1,0:T(8,128)} all-to-all(f32[16,64,128]{2,1,0:T(8,128)} %shard_map.129), channel_id=1, replica_groups=mesh['groups'=2,'gx'=4,'gy'=4] {'gx','gy'}, dimensions={0} | all-to-all | bytes 1048576 | tf_op jit(solution)/shard_map/all_to_all | solution.py:601
  28.4 5.0 %shard_map.130 = (f32[16,64,128]{2,1,0:T(8,128)}, f32[32,512]{1,0:T(8,128)}) custom-call(f32[16,64,128]{2,1,0:T(8,128)} %all_to_all.20.in_ref, bf16[32,192]{1,0:T(8,128)(2,1)} %constant.13.clone.forward_ref, bf16[64,96]{1,0:T(8,128)(2,1)} %constant.14.clone.inverse_ref, bf16[16,32768]{1,0:T(8,128)(2,1)} %weight_ref.3), custom_call_target="tpu_custom_call" | custom-call | tf_op jit(solution)/shard_map/pallas_call | solution.py:623
  33.4 19.9 %all_to_all.21.in_ref = f32[16,64,128]{2,1,0:T(8,128)} all-to-all(f32[16,64,128]{2,1,0:T(8,128)} %get-tuple-element.14), channel_id=1, replica_groups=mesh['groups'=2,'gx'=4,'gy'=4] {'gx','gy'}, dimensions={0} | all-to-all | bytes 1048576 | tf_op jit(solution)/shard_map/all_to_all | solution.py:601
  53.4 9.2 %shard_map.131 = (f32[16,64,128]{2,1,0:T(8,128)}, bf16[512,1024]{1,0:T(8,128)(2,1)}, f32[16,128]{1,0:T(8,128)}) custom-call(f32[16,64,128]{2,1,0:T(8,128)} %all_to_all.21.in_ref, bf16[512,1024]{1,0:T(8,128)(2,1)} %bitcast.6, bf16[512,1024]{1,0:T(8,128)(2,1)} %bitcast.7, bf16[32,32]{1,0:T(8,128)(2,1)} %point_ref.3, f32[1,32]{1,0:T(1,128)} %bitcast.8, ...), custom_call_target="tpu_custom_call" | custom-call | tf_op jit(solution)/shard_map/pallas_call | solution.py:628
  62.6 19.9 %all_to_all.22.in_ref = f32[16,64,128]{2,1,0:T(8,128)} all-to-all(f32[16,64,128]{2,1,0:T(8,128)} %get-tuple-element.15), channel_id=1, replica_groups=mesh['groups'=2,'gx'=4,'gy'=4] {'gx','gy'}, dimensions={0} | all-to-all | bytes 1048576 | tf_op jit(solution)/shard_map/all_to_all | solution.py:601
  82.5 5.0 %shard_map.132 = (f32[16,80,128]{2,1,0:T(8,128)}, f32[32,512]{1,0:T(8,128)}) custom-call(f32[16,64,128]{2,1,0:T(8,128)} %all_to_all.22.in_ref, bf16[32,192]{1,0:T(8,128)(2,1)} %constant.13.clone.forward_ref, bf16[64,96]{1,0:T(8,128)(2,1)} %constant.14.clone.inverse_ref, bf16[16,32768]{1,0:T(8,128)(2,1)} %weight_ref.3, f32[16,128]{1,0:T(8,128)} %get-tuple-element.16.sums_ref), custom_call_target="tpu_custom_call" | custom-call | tf_op jit(solution)/shard_map/pallas_call | solution.py:641
  87.5 3.6 %all-to-all-start.3 = ((f32[16,80,128]{2,1,0:T(8,128)}), f32[16,80,128]{2,1,0:T(8,128)S(1)}, u32[]{:S(2)}, u32[]{:S(2)}) async-start(f32[16,80,128]{2,1,0:T(8,128)} %get-tuple-element.17), calls=%async_computation.3 | async-start | bytes 1310720 | tf_op jit(solution)/shard_map/all_to_all | solution.py:601
  91.1 3.8 %shard_map.134 = f32[16,32768]{1,0:T(8,128)} custom-call(f32[32,512]{1,0:T(8,128)} %get-tuple-element.20.field_ref, f32[32,512]{1,0:T(8,128)} %get-tuple-element.21.adjoint_ref), custom_call_target="tpu_custom_call" | custom-call | tf_op jit(solution)/shard_map/pallas_call | solution.py:649
  94.9 14.7 %all-to-all-done.3.in_ref = f32[16,80,128]{2,1,0:T(8,128)S(1)} async-done(((f32[16,80,128]{2,1,0:T(8,128)}), f32[16,80,128]{2,1,0:T(8,128)S(1)}, u32[]{:S(2)}, u32[]{:S(2)}) %all-to-all-start.3) | async-done | bytes 655392 | tf_op jit(solution)/shard_map/all_to_all | solution.py:601
  109.5 0.0 copy-start
  109.5 0.9 copy-done
  110.4 6.0 %shard_map.133 = (bf16[512,1024]{1,0:T(8,128)(2,1)}, f32[32,32]{1,0:T(8,128)}, f32[1,32]{1,0:T(1,128)}) custom-call(f32[16,80,128]{2,1,0:T(8,128)} %copy-done, bf16[512,1024]{1,0:T(8,128)(2,1)} %get-tuple-element.18.adjoint_ref, bf16[32,32]{1,0:T(8,128)(2,1)} %point_ref.3, f32[4,128,256]{2,1,0:T(8,128)} %constant.12.clone.back_ref, ...), custom_call_target="tpu_custom_call" | custom-call | tf_op jit(solution)/shard_map/pallas_call | solution.py:656
Async XLA Ops:
  87.5 22.0 %all-to-all-start.3 = ((f32[16,80,128]{2,1,0:T(8,128)}), f32[16,80,128]{2,1,0:T(8,128)S(1)}, u32[]{:S(2)}, u32[]{:S(2)}) async-start(f32[16,80,128]{2,1,0:T(8,128)} %get-tuple-element.17), calls=%async_computation.3 | async-start | bytes 1310720 | tf_op jit(solution)/shard_map/all_to_all | solution.py:601
  109.5 0.9 copy-start
where the time goes:
time: 117 us; the launch traced here: 116 us
  blocking collectives  63 us (54%)
  Pallas kernels  33.6 us (29%)
  waiting for transfers between devices  14.7 us (13%)
  starting transfers between devices  3.59 us (3%)
    all_to_all x3, blocking collectives, exchange(): lax.all_to_all(values, ('gx', 'gy'), split_axis=0, concat_axis=0, tiled=T...  63 us
    all_to_all x1, waiting for transfers between devices, exchange(): lax.all_to_all(values, ('gx', 'gy'), split_axis=0, concat_axis=0, tiled=T...  14.7 us
    pallas_call x1, Pallas kernels, fast_device(): call(functools.partial(middle_kernel, rows_x, rows_y), [payload, ((cells,...  9.22 us
    pallas_call x1, Pallas kernels, fast_device(): call(functools.partial(last_kernel, rows_x, rows_y, scale), [((cells, dep...  5.96 us
    pallas_call x1, Pallas kernels, fast_device(): call(functools.partial(product_kernel, x_parts, y_parts), [payload, spect...  5.04 us
    pallas_call x1, Pallas kernels, fast_device(): call(functools.partial(adjoint_kernel, x_parts, y_parts), [((devices, DAT...  4.99 us
    pallas_call x1, Pallas kernels, fast_device(): call(functools.partial(first_kernel, rows_x, rows_y), [payload])  4.58 us
    pallas_call x1, Pallas kernels, fast_device(): call(functools.partial(weight_kernel, scale, modes), [((KZ, KX * 2 * C *...  3.77 us
  transfers between devices with their start and end apart: 1, of which 1 were waited for; matrix products, arithmetic and copies ran while one was open for 0% of the time, Pallas kernels for 3%

commit v1 on v0

--- a/solution.py
+++ b/solution.py
@@ -198,6 +198,12 @@
     return high, (values - high.astype(F32)).astype(BF)
 
 
+def halved(values, table, dims):
+    high, low = halves(values)
+    both = dot(jnp.concatenate([high, low], axis=0), table, ((dims[0],), (dims[1],)))
+    return both[: values.shape[0]] + both[values.shape[0] :]
+
+
 def iota(shape, axis):
     return lax.broadcasted_iota(jnp.int32, shape, axis)
 
@@ -259,8 +265,7 @@
     return jnp.concatenate([high, high, low], axis=0)
 
 
-def forward_matrix(table_ref, rows_x, rows_y):
-    table = table_ref[lax.axis_index("gy")]
+def forward_matrix(table, rows_x, rows_y):
     count = table.shape[0]
     spread = jnp.broadcast_to(table[:, None, :], (count, rows_x, LANES))
     spread = spread.reshape(count * rows_x, LANES)
@@ -281,12 +286,15 @@
     return jnp.concatenate([both[0], both[1], both[0]], axis=1)
 
 
-def field_spectrum(values, matrix, depth_ref, out_ref, rows_x):
+def y_spectrum(values, matrix):
+    rows = matrix.shape[0] // 2
+    both = dot(matrix, values)
+    return both[:rows] + both[rows:]
+
+
+def z_spectrum(planes, depth_ref, out_ref, rows_x):
     rows = KY * rows_x
-    both = dot(matrix, values)
-    high, low = halves(both[: 2 * rows] + both[2 * rows :])
-    both = dot(jnp.concatenate([high, low], axis=0), depth_ref[...])
-    both = both[: 2 * rows] + both[2 * rows :]
+    both = halved(planes, depth_ref[...], (1, 0))
     real = both[:rows, :WIDE] - both[rows:, WIDE:]
     imag = both[:rows, WIDE:] + both[rows:, :WIDE]
     for part, piece in ((0, real), (1, imag)):
@@ -296,7 +304,7 @@
             out_ref[:, start : start + rows_x, :] = block.reshape(KY, rows_x, LANES)
 
 
-def field_synthesis(in_ref, matrix, depth_ref, rows_x):
+def z_synthesis(in_ref, depth_ref, rows_x):
     rows = KY * rows_x
     parts = []
     for part in range(2):
@@ -309,10 +317,8 @@
     stacked = jnp.concatenate(
         [jnp.concatenate([real, imag], axis=1), jnp.concatenate([imag, -real], axis=1)], axis=0
     )
-    high, low = halves(stacked)
-    both = dot(jnp.concatenate([high, low], axis=0), depth_ref[...], ((1,), (1,)))
-    planes = both[: 2 * rows] + both[2 * rows :]
-    return dot(matrix, tripled(planes))
+    planes = halved(stacked, depth_ref[...], (1, 1))
+    return tripled(planes)
 
 
 def mixing_matrix(weight_ref):
@@ -358,13 +364,14 @@
     return jnp.where(iota((1, WIDE), 1) < C, 1.0, 2.0).astype(F32)
 
 
-def spread_modes(values, table_ref, out_ref, x_parts, y_parts):
+def spread_modes(values, table_ref, out_ref, x_parts, y_parts, done=lambda x_part: None):
     cells = dot(table_ref[...], tripled(values))
     for x_part in range(x_parts):
         for chunk in range(CHUNKS):
             block = cells[x_part * 16 : (x_part + 1) * 16, chunk * LANES : (chunk + 1) * LANES]
             for y_part in range(y_parts):
                 out_ref[x_part * y_parts + y_part, chunk * 16 : (chunk + 1) * 16, :] = block
+        done(x_part)
 
 
 def mode_row(ref, row):
@@ -406,9 +413,30 @@
     return values[:, step * LANES : (step + 1) * LANES]
 
 
-def first_kernel(rows_x, rows_y, field_ref, table_ref, depth_ref, out_ref):
-    matrix = forward_matrix(table_ref, rows_x, rows_y)
-    field_spectrum(field_ref[...], matrix, depth_ref, out_ref, rows_x)
+def first_kernel(
+    rows_x, rows_y, field_ref, table_ref, depth_ref, out_ref, field, table, depth, gates
+):
+    copies = [pltpu.make_async_copy(table_ref.at[lax.axis_index("gy")], table, gates.at[0])]
+    for part in range(2):
+        rows = pl.ds(part * field.shape[0] // 2, field.shape[0] // 2)
+        copies.append(
+            pltpu.make_async_copy(field_ref.at[rows], field.at[rows], gates.at[1 + part])
+        )
+    for part in range(4):
+        rows = pl.ds(part * depth.shape[0] // 4, depth.shape[0] // 4)
+        copies.append(
+            pltpu.make_async_copy(depth_ref.at[rows], depth.at[rows], gates.at[3 + part])
+        )
+    for copy in copies:
+        copy.start()
+    copies[0].wait()
+    matrix = forward_matrix(table[...], rows_x, rows_y)
+    copies[1].wait()
+    copies[2].wait()
+    planes = y_spectrum(field[...], matrix)
+    for copy in copies[3:]:
+        copy.wait()
+    z_spectrum(planes, depth, out_ref, rows_x)
 
 
 def product_kernel(
@@ -451,8 +479,11 @@
     out_ref,
     adjoint_ref,
     sums_ref,
+    held,
+    gate,
 ):
-    spectral = field_synthesis(in_ref, inverse_matrix(back_ref, rows_x, rows_y), depth_ref, rows_x)
+    matrix = inverse_matrix(back_ref, rows_x, rows_y)
+    spectral = dot(matrix, z_synthesis(in_ref, depth_ref, rows_x))
     mixing = mixing_matrix(point_ref)
     field = field_ref[...]
     bias = jnp.concatenate([bias_ref[...]] * NZ, axis=1)
@@ -464,8 +495,11 @@
         root + (3.0 * root * 0.044715) * square
     )
     adjoint = (cotangent_ref[...].astype(F32) * slope).astype(BF)
-    adjoint_ref[...] = adjoint
-    field_spectrum(adjoint, forward_matrix(table_ref, rows_x, rows_y), depth_ref, out_ref, rows_x)
+    held[...] = adjoint
+    copy = pltpu.make_async_copy(held, adjoint_ref, gate)
+    copy.start()
+    matrix = forward_matrix(table_ref[lax.axis_index("gy")], rows_x, rows_y)
+    z_spectrum(y_spectrum(adjoint, matrix), depth_ref, out_ref, rows_x)
     wide = mixing.shape[0]
     total = jnp.zeros((wide, wide), F32)
     for start in range(0, NZ * C, wide):
@@ -483,6 +517,7 @@
         packed = jnp.where(group == part, point[part * 8 : (part + 1) * 8], packed)
     sums_ref[:8, :] = packed
     sums_ref[8:, :] = folded(dot(jnp.ones((8, adjoint.shape[0]), BF), adjoint))
+    copy.wait()
 
 
 def swapped(values, index, distance):
@@ -500,6 +535,8 @@
     out_ref,
     spec_ref,
     scratch,
+    staged,
+    gates,
 ):
     spec_ref[...] = own_spectrum(in_ref, forward_ref, x_parts, y_parts) * depth_factor()
     keep = own_group()
@@ -540,26 +577,52 @@
         return carry
 
     lax.fori_loop(0, KX, step, 0, unroll=4)
-    spread_modes(gathered_rows(scratch), inverse_ref, out_ref, x_parts, y_parts)
     for device in range(x_parts * y_parts):
-        out_ref[device, DATA_ROWS:, :] = sums_ref[...]
-
-
-def weight_kernel(scale, modes, field_ref, adjoint_ref, out_ref):
-    first = pl.program_id(0) * modes
+        staged[device, DATA_ROWS:, :] = sums_ref[...]
+    stores = []
+
+    def send(x_part):
+        block = pl.ds(x_part * y_parts, y_parts)
+        stores.append(
+            pltpu.make_async_copy(staged.at[block], out_ref.at[block], gates.at[x_part])
+        )
+        stores[-1].start()
+
+    spread_modes(gathered_rows(scratch), inverse_ref, staged, x_parts, y_parts, send)
+    for store in stores:
+        store.wait()
+
+
+def weight_kernel(scale, field_ref, adjoint_ref, out_ref, staged, gates):
     index = out_index()
-    for local in range(modes):
-        row = 2 * (first + local)
+    stores = []
+    turns = gates.shape[0]
+    modes = KX // turns
+
+    def step(mode, carry):
+        row = 2 * mode
         real_v, imag_v = mode_row(field_ref, row), mode_row(field_ref, row + 1)
         real_h = lane_take(mode_row(adjoint_ref, row), index) * scale
         imag_h = lane_take(mode_row(adjoint_ref, row + 1), index) * scale
+        real_g, imag_g = [], []
         for part in range(C // 4):
             take = in_index(part)
             real, imag = lane_take(real_v, take), lane_take(imag_v, take)
-            start = local * 2 * C * C + part * LANES
-            out_ref[:, start : start + LANES] = real * real_h + imag * imag_h
-            start += C * C
-            out_ref[:, start : start + LANES] = real * imag_h - imag * real_h
+            real_g.append(real * real_h + imag * imag_h)
+            imag_g.append(real * imag_h - imag * real_h)
+        start = pl.multiple_of(mode * 2 * C * C, LANES)
+        staged[:, pl.ds(start, 2 * C * C)] = jnp.concatenate(real_g + imag_g, axis=1)
+        return carry
+
+    for turn in range(turns):
+        lax.fori_loop(turn * modes, (turn + 1) * modes, step, 0, unroll=2)
+        block = pl.ds(turn * modes * 2 * C * C, modes * 2 * C * C)
+        stores.append(
+            pltpu.make_async_copy(staged.at[:, block], out_ref.at[:, block], gates.at[turn])
+        )
+        stores[-1].start()
+    for store in stores:
+        store.wait()
 
 
 def last_kernel(
@@ -574,10 +637,13 @@
     out_ref,
     grad_ref,
     bias_ref,
+    adjoint,
+    result,
+    gate,
+    gates,
 ):
-    spectral = field_synthesis(in_ref, inverse_matrix(back_ref, rows_x, rows_y), depth_ref, rows_x)
-    mixing = mixing_matrix(point_ref)
-    out_ref[...] = (mixed(adjoint_ref[...], mixing, ((1,), (1,))) + spectral).astype(BF)
+    fetch = pltpu.make_async_copy(adjoint_ref, adjoint, gate)
+    fetch.start()
     total = in_ref[0, DATA_ROWS:, :]
     for device in range(1, in_ref.shape[0]):
         total = total + in_ref[device, DATA_ROWS:, :]
@@ -587,14 +653,50 @@
         piece = packed if part == 0 else pltpu.roll(packed, LANES - part * C, 1)
         grad_ref[part * 8 : (part + 1) * 8, :] = piece[:, :C]
     bias_ref[...] = total[8:9, :C]
-
-
-def call(kernel, outs, scratch=(), **options):
-    shapes = [jax.ShapeDtypeStruct(shape, kind) for shape, kind in outs]
-    params = pltpu.CompilerParams(vmem_limit_bytes=56 * 1024 * 1024)
-    return pl.pallas_call(
-        kernel, out_shape=shapes, scratch_shapes=list(scratch), compiler_params=params, **options
-    )
+    matrix = inverse_matrix(back_ref, rows_x, rows_y)
+    planes = z_synthesis(in_ref, depth_ref, rows_x)
+    mixing = mixing_matrix(point_ref)
+    fetch.wait()
+    stores = []
+    rows = result.shape[0] // gates.shape[0]
+    for part in range(gates.shape[0]):
+        block = pl.ds(part * rows, rows)
+        mix = mixed(adjoint[block, :], mixing, ((1,), (1,)))
+        spectral = dot(matrix[part * rows : (part + 1) * rows], planes)
+        result[block, :] = (mix + spectral).astype(BF)
+        stores.append(
+            pltpu.make_async_copy(result.at[block], out_ref.at[block], gates.at[part])
+        )
+        stores[-1].start()
+    for store in stores:
+        store.wait()
+
+
+NEAR = pl.BlockSpec(memory_space=pltpu.VMEM)
+FAR = pl.BlockSpec(memory_space=pltpu.HBM)
+
+
+def call(kernel, ins, outs, scratch=()):
+    shapes = []
+    for shape, kind, inner in outs:
+        if inner is None:
+            shapes.append(jax.ShapeDtypeStruct(shape, kind))
+        else:
+            shapes.append((pltpu.VMEM if inner else pltpu.HBM)(shape, kind))
+    function = pl.pallas_call(
+        kernel,
+        out_shape=shapes,
+        in_specs=[NEAR if inner else FAR for inner in ins],
+        out_specs=[FAR if inner is False else NEAR for _, _, inner in outs],
+        scratch_shapes=list(scratch),
+        compiler_params=pltpu.CompilerParams(vmem_limit_bytes=40 * 1024 * 1024),
+    )
+
+    def run(*arguments):
+        spaces = [pltpu.VMEM if inner else pltpu.HBM for inner in ins]
+        return function(*map(pltpu.with_memory_space_constraint, arguments, spaces))
+
+    return run
 
 
 def exchange(values):
@@ -613,21 +715,34 @@
     forward_x, inverse_x = map(jnp.asarray, x_tables(full_x, rows_x, scale))
     field = field_input.reshape(cells, depth)
     bias = point_bias.reshape(1, C)
-    payload = ((devices, DATA_ROWS, LANES), F32)
-    spectrum_shape = ((2 * KX, WIDE), F32)
+    payload = ((devices, DATA_ROWS, LANES), F32, True)
+    spectrum_shape = ((2 * KX, WIDE), F32, True)
     rows_scratch = pltpu.VMEM((2 * KX * KZ, LANES), F32)
-
-    (sent,) = call(functools.partial(first_kernel, rows_x, rows_y), [payload])(
-        field, forward_y, depth_table
-    )
+    plane = pltpu.VMEM((cells, depth), BF)
+    gate = pltpu.SemaphoreType.DMA(())
+
+    (sent,) = call(
+        functools.partial(first_kernel, rows_x, rows_y),
+        [False] * 3,
+        [payload],
+        [
+            plane,
+            pltpu.VMEM(forward_y.shape[1:], F32),
+            pltpu.VMEM(depth_table.shape, BF),
+            pltpu.SemaphoreType.DMA((7,)),
+        ],
+    )(field, forward_y, depth_table)
     sent, field_modes = call(
         functools.partial(product_kernel, x_parts, y_parts),
+        [True] * 4,
         [payload, spectrum_shape],
         [rows_scratch],
     )(exchange(sent), forward_x, inverse_x, spectral_weight)
     sent, adjoint, sums = call(
         functools.partial(middle_kernel, rows_x, rows_y),
-        [payload, ((cells, depth), BF), ((SUM_ROWS, LANES), F32)],
+        [True] * 8,
+        [payload, ((cells, depth), BF, False), ((SUM_ROWS, LANES), F32, True)],
+        [plane, gate],
     )(
         exchange(sent),
         field,
@@ -640,22 +755,27 @@
     )
     sent, adjoint_modes = call(
         functools.partial(adjoint_kernel, x_parts, y_parts),
-        [((devices, DATA_ROWS + SUM_ROWS, LANES), F32), spectrum_shape],
-        [rows_scratch],
+        [True] * 5,
+        [((devices, DATA_ROWS + SUM_ROWS, LANES), F32, False), spectrum_shape],
+        [
+            rows_scratch,
+            pltpu.VMEM((devices, DATA_ROWS + SUM_ROWS, LANES), F32),
+            pltpu.SemaphoreType.DMA((x_parts,)),
+        ],
     )(exchange(sent), forward_x, inverse_x, spectral_weight, sums)
-    steps = 4
-    modes = KX // steps
-    whole = pl.BlockSpec((2 * KX, WIDE), lambda i: (0, 0))
+    wide = (KZ, KX * 2 * C * C)
     (grad_spectral,) = call(
-        functools.partial(weight_kernel, scale, modes),
-        [((KZ, KX * 2 * C * C), F32)],
-        grid=(steps,),
-        in_specs=[whole, whole],
-        out_specs=[pl.BlockSpec((KZ, modes * 2 * C * C), lambda i: (0, i))],
+        functools.partial(weight_kernel, scale),
+        [True, True],
+        [(wide, F32, False)],
+        [pltpu.VMEM(wide, F32), pltpu.SemaphoreType.DMA((4,))],
     )(field_modes, adjoint_modes)
+    chunks = 4
     grad_field, grad_point, grad_bias = call(
         functools.partial(last_kernel, rows_x, rows_y, scale),
-        [((cells, depth), BF), ((C, C), F32), ((1, C), F32)],
+        [True, False, True, True, True],
+        [((cells, depth), BF, False), ((C, C), F32, None), ((1, C), F32, None)],
+        [plane, plane, gate, pltpu.SemaphoreType.DMA((chunks,))],
     )(exchange(sent), adjoint, point_weight, inverse_y, depth_table)
     return (
         grad_field.reshape(field_input.shape),

time: 117 us -> 105 us (0.90)
  Pallas kernels: 33.6 us -> 23.8 us
  blocking collectives: 63 us -> 60.9 us
    pallas_call x6, Pallas kernels: 33.6 us -> 23.8 us  [run(): return function(*map(pltpu.with_memory_space_constraint, arguments, spaces))]
    all_to_all x3, blocking collectives: 63 us -> 60.9 us  [exchange(): lax.all_to_all(values, ('gx', 'gy'), split_axis=0, concat_axis=0, tiled=T...]
where the time goes in v1:
time: 105 us
  blocking collectives  60.9 us (58%)
  Pallas kernels  23.8 us (23%)
  waiting for transfers between devices  15.6 us (15%)
  starting transfers between devices  3.61 us (3%)
    all_to_all x3, blocking collectives, exchange(): lax.all_to_all(values, ('gx', 'gy'), split_axis=0, concat_axis=0, tiled=T...  60.9 us
    pallas_call x6, Pallas kernels, run(): return function(*map(pltpu.with_memory_space_constraint, arguments, spaces))  23.8 us
    all_to_all x1, waiting for transfers between devices, exchange(): lax.all_to_all(values, ('gx', 'gy'), split_axis=0, concat_axis=0, tiled=T...  15.6 us
    all_to_all x1, starting transfers between devices, exchange(): lax.all_to_all(values, ('gx', 'gy'), split_axis=0, concat_axis=0, tiled=T...  3.61 us
  transfers between devices with their start and end apart: 1, of which 1 were waited for; matrix products, arithmetic and copies ran while one was open for 0% of the time, Pallas kernels for 3%

profile of v1, /device:TPU:0, one launch (start us, length us, event | category | flops | bytes accessed | tf_op | source)
XLA Modules:
  0.0 104.7 jit_solution(10797582765655838483)
XLA Ops:
  0.6 0.0 copy-start.1
  0.6 0.0 copy-start.6
  0.7 0.0 copy-start.7
  0.7 0.0 copy-start.4
  0.7 0.0 copy-start.5
  0.7 3.4 %shard_map.129 = f32[16,64,128]{2,1,0:T(8,128)S(1)} custom-call(bf16[512,1024]{1,0:T(8,128)(2,1)} %bitcast.5, f32[4,64,128]{2,1,0:T(8,128)} %constant.11.clone.table_ref, bf16[1024,1024]{1,0:T(8,128)(2,1)} %constant.10.clone.depth_ref), custom_call_target="tpu_custom_call" | custom-call | tf_op jit(solution)/shard_map/pallas_call | solution.py:697
  4.1 0.0 copy-start
  4.1 0.0 copy-start.2
  4.1 0.0 copy-start.3
  4.1 0.0 copy-start.8
  4.1 0.0 copy-start.9
  4.2 23.1 %all_to_all.20.in_ref = f32[16,64,128]{2,1,0:T(8,128)S(1)} all-to-all(f32[16,64,128]{2,1,0:T(8,128)S(1)} %shard_map.129), channel_id=1, replica_groups=mesh['groups'=2,'gx'=4,'gy'=4] {'gx','gy'}, dimensions={0} | all-to-all | bytes 1048576 | tf_op jit(solution)/shard_map/all_to_all | solution.py:703
  27.3 0.0 copy-done.1
  27.3 0.0 copy-done.7
  27.3 2.8 %shard_map.130 = (f32[16,64,128]{2,1,0:T(8,128)S(1)}, f32[32,512]{1,0:T(8,128)S(1)}) custom-call(f32[16,64,128]{2,1,0:T(8,128)S(1)} %all_to_all.20.in_ref, bf16[32,192]{1,0:T(8,128)(2,1)S(1)} %copy-done.7, bf16[64,96]{1,0:T(8,128)(2,1)S(1)} %copy-done.6, bf16[16,32768]{1,0:T(8,128)(2,1)S(1)} %copy-done.1), custom_call_target="tpu_custom_call" | custom-call | tf_op jit(solution)/shard_map/pallas_call | solution.py:697
  30.1 18.9 %all_to_all.21.in_ref = f32[16,64,128]{2,1,0:T(8,128)S(1)} all-to-all(f32[16,64,128]{2,1,0:T(8,128)S(1)} %get-tuple-element.14), channel_id=1, replica_groups=mesh['groups'=2,'gx'=4,'gy'=4] {'gx','gy'}, dimensions={0} | all-to-all | bytes 1048576 | tf_op jit(solution)/shard_map/all_to_all | solution.py:703
  49.0 0.0 copy-done
  49.0 6.6 %shard_map.131 = (f32[16,64,128]{2,1,0:T(8,128)S(1)}, bf16[512,1024]{1,0:T(8,128)(2,1)}, f32[16,128]{1,0:T(8,128)S(1)}) custom-call(f32[16,64,128]{2,1,0:T(8,128)S(1)} %all_to_all.21.in_ref, bf16[512,1024]{1,0:T(8,128)(2,1)S(1)} %bitcast.6, bf16[512,1024]{1,0:T(8,128)(2,1)S(1)} %bitcast.7, bf16[32,32]{1,0:T(8,128)(2,1)S(1)} %copy-done.8, ...), custom_call_target="tpu_custom_call" | custom-call | tf_op jit(solution)/shard_map/pallas_call | solution.py:697
  55.6 18.9 %all_to_all.22.in_ref = f32[16,64,128]{2,1,0:T(8,128)S(1)} all-to-all(f32[16,64,128]{2,1,0:T(8,128)S(1)} %get-tuple-element.15), channel_id=1, replica_groups=mesh['groups'=2,'gx'=4,'gy'=4] {'gx','gy'}, dimensions={0} | all-to-all | bytes 1048576 | tf_op jit(solution)/shard_map/all_to_all | solution.py:703
  74.5 3.6 %shard_map.132 = (f32[16,80,128]{2,1,0:T(8,128)}, f32[32,512]{1,0:T(8,128)S(1)}) custom-call(f32[16,64,128]{2,1,0:T(8,128)S(1)} %all_to_all.22.in_ref, bf16[32,192]{1,0:T(8,128)(2,1)S(1)} %copy-done.7, bf16[64,96]{1,0:T(8,128)(2,1)S(1)} %copy-done.6, bf16[16,32768]{1,0:T(8,128)(2,1)S(1)} %copy-done.1, f32[16,128]{1,0:T(8,128)S(1)} %get-tuple-element.16.sums_ref), custom_call_target="tpu_custom_call" | custom-call | tf_op jit(solution)/shard_map/pallas_call | solution.py:697
  78.1 3.6 %all-to-all-start.3 = ((f32[16,80,128]{2,1,0:T(8,128)}), f32[16,80,128]{2,1,0:T(8,128)S(1)}, u32[]{:S(2)}, u32[]{:S(2)}) async-start(f32[16,80,128]{2,1,0:T(8,128)} %get-tuple-element.17), calls=%async_computation.3 | async-start | bytes 1310720 | tf_op jit(solution)/shard_map/all_to_all | solution.py:703
  81.8 2.8 %shard_map.134 = f32[16,32768]{1,0:T(8,128)} custom-call(f32[32,512]{1,0:T(8,128)S(1)} %get-tuple-element.20.field_ref, f32[32,512]{1,0:T(8,128)S(1)} %get-tuple-element.21.adjoint_ref), custom_call_target="tpu_custom_call" | custom-call | tf_op jit(solution)/shard_map/pallas_call | solution.py:697
  84.6 15.6 %all-to-all-done.3.in_ref = f32[16,80,128]{2,1,0:T(8,128)S(1)} async-done(((f32[16,80,128]{2,1,0:T(8,128)}), f32[16,80,128]{2,1,0:T(8,128)S(1)}, u32[]{:S(2)}, u32[]{:S(2)}) %all-to-all-start.3) | async-done | bytes 655392 | tf_op jit(solution)/shard_map/all_to_all | solution.py:703
  100.2 4.5 %shard_map.133 = (bf16[512,1024]{1,0:T(8,128)(2,1)}, f32[32,32]{1,0:T(8,128)}, f32[1,32]{1,0:T(1,128)}) custom-call(f32[16,80,128]{2,1,0:T(8,128)S(1)} %all-to-all-done.3.in_ref, bf16[512,1024]{1,0:T(8,128)(2,1)} %get-tuple-element.18.adjoint_ref, bf16[32,32]{1,0:T(8,128)(2,1)S(1)} %copy-done.8, f32[4,128,256]{2,1,0:T(8,128)S(1)} %copy-done.3, ...), custom_call_target="tpu_custom_call" | custom-call | tf_op jit(solution)/shard_map/pallas_call | solution.py:697
  (7 shorter events, 0.0 us)
Async XLA Ops:
  0.6 26.7 %copy-start.1 = (bf16[16,32768]{1,0:T(8,128)(2,1)S(1)}, bf16[16,32768]{1,0:T(8,128)(2,1)}, u32[]{:S(2)}) copy-start(bf16[16,32768]{1,0:T(8,128)(2,1)} %weight_ref.3) | copy-start | bytes 3145732
  0.6 26.7 %copy-start.6 = (bf16[64,96]{1,0:T(8,128)(2,1)S(1)}, bf16[64,96]{1,0:T(8,128)(2,1)}, u32[]{:S(2)}) copy-start(bf16[64,96]{1,0:T(8,128)(2,1)} %constant.14.clone.inverse_ref) | copy-start | bytes 36868
  0.7 26.6 %copy-start.7 = (bf16[32,192]{1,0:T(8,128)(2,1)S(1)}, bf16[32,192]{1,0:T(8,128)(2,1)}, u32[]{:S(2)}) copy-start(bf16[32,192]{1,0:T(8,128)(2,1)} %constant.13.clone.forward_ref) | copy-start | bytes 36868
  0.7 48.3 %copy-start.4 = (bf16[8,64,1024]{2,1,0:T(8,128)(2,1)S(1)}, bf16[8,64,1024]{2,1,0:T(8,128)(2,1)}, u32[]{:S(2)}) copy-start(bf16[8,64,1024]{2,1,0:T(8,128)(2,1)} %param.11) | copy-start | bytes 3145732
  0.7 48.3 %copy-start.5 = (f32[4,64,128]{2,1,0:T(8,128)S(1)}, f32[4,64,128]{2,1,0:T(8,128)}, u32[]{:S(2)}) copy-start(f32[4,64,128]{2,1,0:T(8,128)} %constant.11.clone.table_ref) | copy-start | bytes 393220
  4.1 44.9 %copy-start = (bf16[1024,1024]{1,0:T(8,128)(2,1)S(1)}, bf16[1024,1024]{1,0:T(8,128)(2,1)}, u32[]{:S(2)}) copy-start(bf16[1024,1024]{1,0:T(8,128)(2,1)} %constant.10.clone.depth_ref) | copy-start | bytes 6291460
  4.1 44.9 %copy-start.2 = (bf16[8,64,1024]{2,1,0:T(8,128)(2,1)S(1)}, bf16[8,64,1024]{2,1,0:T(8,128)(2,1)}, u32[]{:S(2)}) copy-start(bf16[8,64,1024]{2,1,0:T(8,128)(2,1)} %param.10) | copy-start | bytes 3145732
  4.1 44.9 %copy-start.3 = (f32[4,128,256]{2,1,0:T(8,128)S(1)}, f32[4,128,256]{2,1,0:T(8,128)}, u32[]{:S(2)}) copy-start(f32[4,128,256]{2,1,0:T(8,128)} %constant.12.clone.back_ref) | copy-start | bytes 1572868
  4.1 44.9 %copy-start.8 = (bf16[32,32]{1,0:T(8,128)(2,1)S(1)}, bf16[32,32]{1,0:T(8,128)(2,1)}, u32[]{:S(2)}) copy-start(bf16[32,32]{1,0:T(8,128)(2,1)} %point_ref.3) | copy-start | bytes 6148
  4.1 44.9 %copy-start.9 = (f32[32]{0:T(128)S(1)}, f32[32]{0:T(128)}, u32[]{:S(2)}) copy-start(f32[32]{0:T(128)} %param.14) | copy-start | bytes 388
  78.1 22.1 %all-to-all-start.3 = ((f32[16,80,128]{2,1,0:T(8,128)}), f32[16,80,128]{2,1,0:T(8,128)S(1)}, u32[]{:S(2)}, u32[]{:S(2)}) async-start(f32[16,80,128]{2,1,0:T(8,128)} %get-tuple-element.17), calls=%async_computation.3 | async-start | bytes 1310720 | tf_op jit(solution)/shard_map/all_to_all | solution.py:703

commit v2 on v1

--- a/solution.py
+++ b/solution.py
@@ -185,7 +185,6 @@
 LANES = 128
 CHUNKS = KZ * C // LANES
 WIDE = KZ * C
-DATA_ROWS = 16 * CHUNKS
 SUM_ROWS = 16
 
 
@@ -227,37 +226,53 @@
     return 2.0 * np.pi * ((positions[:, None] * modes[None, :]) % length) / length
 
 
-def depth_matrix():
+def depth_rows():
     angles = np_angles(np.arange(NZ), np.arange(KZ), NZ)
     table = np.stack([np.cos(angles), -np.sin(angles)], axis=1).astype(ml_dtypes.bfloat16)
-    table = table.astype(np.float32).reshape(NZ, 2 * KZ)
-    return np.kron(table, np.eye(C, dtype=np.float32)).astype(ml_dtypes.bfloat16)
-
-
-def y_tables(full_y, rows_y, rows_x, parts):
+    return np.repeat(table.astype(np.float32).reshape(NZ, 2 * KZ), C, axis=1)
+
+
+def y_tables(full_y, rows_y, x_parts, y_parts):
     angles = np_angles(np.arange(full_y), np_modes(KY, full_y), full_y)
-    table = np.stack([np.cos(angles), -np.sin(angles)], axis=0)
-    both = np.stack(np_halves(table), axis=0).reshape(2, 2, parts, rows_y, KY)
-    forward = both.transpose(2, 0, 1, 4, 3).reshape(parts, 4 * KY, rows_y)
-    forward = np.tile(forward, (1, 1, LANES // rows_y))
-    inverse = np.repeat(both.transpose(2, 0, 3, 1, 4), rows_x, axis=-1)
-    inverse = inverse.reshape(parts, 2 * rows_y, 2 * KY * rows_x)
-    return forward.astype(np.float32), inverse.astype(np.float32)
-
-
-def x_tables(full_x, rows_x, factor):
+    table = np.stack([np.cos(angles), -np.sin(angles)], axis=-1)
+    high, low = np_halves(table)
+    forward, inverse = [], []
+    for device in range(x_parts * y_parts):
+        own_x, own_y = device // y_parts, device % y_parts
+        order = [
+            (own_x ^ turn) * y_parts + (own_y ^ step)
+            for turn in range(x_parts)
+            for step in range(y_parts)
+        ]
+        rows = slice(own_y * rows_y, (own_y + 1) * rows_y)
+
+        def picked(values):
+            block = values[rows][:, order].reshape(rows_y, x_parts, y_parts, 2)
+            return block.transpose(0, 1, 3, 2).reshape(rows_y, 2 * KY)
+
+        forward.append(np.concatenate([picked(high), picked(low)], axis=1).T)
+        inverse.append(np.concatenate([picked(high), picked(low), picked(high)], axis=1))
+    return tuple(np.stack(part).astype(ml_dtypes.bfloat16) for part in (forward, inverse))
+
+
+def x_tables(full_x, rows_x, factor, y_parts):
     angles = np_angles(np.arange(full_x), np_modes(KX, full_x), full_x)
     cosine, sine = np.cos(angles) * factor, np.sin(angles) * factor
     table = np.stack([np.stack([cosine, -sine], -1), np.stack([sine, cosine], -1)], axis=1)
-    blocked = table.reshape(full_x // rows_x, rows_x, 2, KX, 2).transpose(0, 2, 1, 3, 4)
-    inverse = blocked.reshape(2 * full_x, 2 * KX)
-    forward = inverse.T
-
-    def packed(matrix):
-        high, low = np_halves(matrix)
-        return np.concatenate([high, low, high], axis=1).astype(ml_dtypes.bfloat16)
-
-    return packed(forward), packed(inverse)
+    blocked = table.reshape(full_x // rows_x, rows_x * 2, KX * 2)
+    same = np.eye(y_parts)
+
+    def packed(spread):
+        high, low = np_halves(spread)
+        return np.concatenate([high, low, high], axis=2).astype(ml_dtypes.bfloat16)
+
+    forward = np.einsum("grm,de->gdmre", blocked, same)
+    inverse = np.einsum("grm,de->grdem", blocked, same)
+    parts, rows, modes = blocked.shape
+    return (
+        packed(forward.reshape(parts, y_parts * modes, rows * y_parts)),
+        packed(inverse.reshape(parts, rows * y_parts, y_parts * modes)),
+    )
 
 
 def tripled(values):
@@ -265,60 +280,60 @@
     return jnp.concatenate([high, high, low], axis=0)
 
 
-def forward_matrix(table, rows_x, rows_y):
-    count = table.shape[0]
-    spread = jnp.broadcast_to(table[:, None, :], (count, rows_x, LANES))
-    spread = spread.reshape(count * rows_x, LANES)
-    spread = jnp.concatenate([spread] * (rows_x * rows_y // LANES), axis=1)
-    shape = spread.shape
-    return jnp.where(iota(shape, 1) // rows_y == iota(shape, 0) % rows_x, spread, 0.0).astype(BF)
-
-
-def inverse_matrix(table_ref, rows_x, rows_y):
-    table = table_ref[lax.axis_index("gy")]
-    wide = table.shape[1]
-    both = []
-    for part in range(2):
-        block = table[part * rows_y : (part + 1) * rows_y]
-        owner = iota((rows_y, wide), 1) % rows_x
-        rows = [jnp.where(owner == x, block, 0.0) for x in range(rows_x)]
-        both.append(jnp.concatenate(rows, axis=0).astype(BF))
-    return jnp.concatenate([both[0], both[1], both[0]], axis=1)
-
-
-def y_spectrum(values, matrix):
-    rows = matrix.shape[0] // 2
-    both = dot(matrix, values)
-    return both[:rows] + both[rows:]
-
-
-def z_spectrum(planes, depth_ref, out_ref, rows_x):
-    rows = KY * rows_x
+def lanes_of(values, step):
+    return values[:, step * LANES : (step + 1) * LANES]
+
+
+def read_lanes(ref, rows):
+    pieces = [ref[i * rows : (i + 1) * rows, :] for i in range(CHUNKS)]
+    return jnp.concatenate(pieces, axis=1)
+
+
+def write_lanes(ref, values, rows, start=0):
+    for chunk in range(CHUNKS):
+        first = chunk * rows + start
+        ref[first : first + values.shape[0], :] = lanes_of(values, chunk)
+
+
+def turned(values):
+    tiles = values.reshape(values.shape[0] // 8, 8, values.shape[1])
+    return pltpu.roll(tiles, 4, 1).reshape(values.shape)
+
+
+def part_sign(rows):
+    return jnp.where(iota((rows, 1), 0) % 8 < 4, -1.0, 1.0).astype(F32)
+
+
+def y_spectrum(values, table, rows_x, rows_y):
+    planes = []
+    half = table.shape[0] // 2
+    for x in range(rows_x):
+        both = dot(table, values[x * rows_y : (x + 1) * rows_y])
+        planes.append(both[:half] + both[half:])
+    return jnp.concatenate(planes, axis=0)
+
+
+def z_spectrum(planes, depth_ref, out_refs, rows_x):
     both = halved(planes, depth_ref[...], (1, 0))
-    real = both[:rows, :WIDE] - both[rows:, WIDE:]
-    imag = both[:rows, WIDE:] + both[rows:, :WIDE]
-    for part, piece in ((0, real), (1, imag)):
-        for chunk in range(CHUNKS):
-            start = (chunk * 2 + part) * rows_x
-            block = piece[:, chunk * LANES : (chunk + 1) * LANES]
-            out_ref[:, start : start + rows_x, :] = block.reshape(KY, rows_x, LANES)
-
-
-def z_synthesis(in_ref, depth_ref, rows_x):
-    rows = KY * rows_x
-    parts = []
-    for part in range(2):
-        pieces = []
-        for chunk in range(CHUNKS):
-            start = (chunk * 2 + part) * rows_x
-            pieces.append(in_ref[:, start : start + rows_x, :].reshape(rows, LANES))
-        parts.append(jnp.concatenate(pieces, axis=1))
-    real, imag = parts
-    stacked = jnp.concatenate(
-        [jnp.concatenate([real, imag], axis=1), jnp.concatenate([imag, -real], axis=1)], axis=0
-    )
-    planes = halved(stacked, depth_ref[...], (1, 1))
-    return tripled(planes)
+    whole = both[:, :WIDE] + part_sign(planes.shape[0]) * turned(both[:, WIDE:])
+    turns = len(out_refs)
+    for x in range(rows_x):
+        for turn in range(turns):
+            block = whole[(x * turns + turn) * 8 : (x * turns + turn + 1) * 8]
+            write_lanes(out_refs[turn], block, rows_x * 8, x * 8)
+
+
+def z_synthesis(in_refs, depth_ref, rows_x):
+    blocks = [read_lanes(ref, rows_x * 8) for ref in in_refs]
+    modes = jnp.concatenate(blocks, axis=0)
+    other = -part_sign(modes.shape[0]) * turned(modes)
+    return halved(jnp.concatenate([modes, other], axis=1), depth_ref[...], (1, 1))
+
+
+def y_synthesis(planes, table, x, rows_x):
+    turns = planes.shape[0] // (8 * rows_x)
+    rows = [(turn * rows_x + x) * 8 for turn in range(turns)]
+    return dot(table, tripled(jnp.concatenate([planes[r : r + 8] for r in rows], axis=0)))
 
 
 def mixing_matrix(weight_ref):
@@ -346,32 +361,8 @@
     return total + pltpu.roll(total, 32, 1)
 
 
-def own_spectrum(in_ref, table_ref, x_parts, y_parts):
-    chunks = []
-    for chunk in range(CHUNKS):
-        rows = []
-        for x_part in range(x_parts):
-            block = [
-                in_ref[x_part * y_parts + y_part, chunk * 16 : (chunk + 1) * 16, :]
-                for y_part in range(y_parts)
-            ]
-            rows.append(functools.reduce(jnp.add, block))
-        chunks.append(jnp.concatenate(rows, axis=0))
-    return dot(table_ref[...], tripled(jnp.concatenate(chunks, axis=1)))
-
-
 def depth_factor():
     return jnp.where(iota((1, WIDE), 1) < C, 1.0, 2.0).astype(F32)
-
-
-def spread_modes(values, table_ref, out_ref, x_parts, y_parts, done=lambda x_part: None):
-    cells = dot(table_ref[...], tripled(values))
-    for x_part in range(x_parts):
-        for chunk in range(CHUNKS):
-            block = cells[x_part * 16 : (x_part + 1) * 16, chunk * LANES : (chunk + 1) * LANES]
-            for y_part in range(y_parts):
-                out_ref[x_part * y_parts + y_part, chunk * 16 : (chunk + 1) * 16, :] = block
-        done(x_part)
 
 
 def mode_row(ref, row):
@@ -409,40 +400,90 @@
     return both[:, : C * C], both[:, C * C :]
 
 
-def lanes_of(values, step):
-    return values[:, step * LANES : (step + 1) * LANES]
+def device_index():
+    return lax.axis_index("gx") * lax.axis_size("gy") + lax.axis_index("gy")
+
+
+def fill_depth(rows_ref, depth_ref):
+    count, wide = rows_ref.shape
+    same = iota((C, wide), 0) == iota((C, wide), 1) % C
+    for z in range(count):
+        row = jnp.broadcast_to(rows_ref[z : z + 1, :], (C, wide))
+        depth_ref[z * C : (z + 1) * C, :] = jnp.where(same, row, 0.0).astype(BF)
 
 
 def first_kernel(
-    rows_x, rows_y, field_ref, table_ref, depth_ref, out_ref, field, table, depth, gates
+    rows_x,
+    rows_y,
+    field_ref,
+    table_ref,
+    rows_ref,
+    point_ref,
+    back_ref,
+    modes_ref,
+    cells_ref,
+    *refs,
 ):
-    copies = [pltpu.make_async_copy(table_ref.at[lax.axis_index("gy")], table, gates.at[0])]
+    out_refs, refs = refs[:-10], refs[-10:]
+    depth, mixing_ref, table, back, to_modes, to_cells, field, rows, point, gates = refs
+    device = device_index()
+    half = field.shape[0] // 2
+    pairs = [(rows_ref, rows), (point_ref, point), (table_ref.at[device], table)]
     for part in range(2):
-        rows = pl.ds(part * field.shape[0] // 2, field.shape[0] // 2)
-        copies.append(
-            pltpu.make_async_copy(field_ref.at[rows], field.at[rows], gates.at[1 + part])
-        )
-    for part in range(4):
-        rows = pl.ds(part * depth.shape[0] // 4, depth.shape[0] // 4)
-        copies.append(
-            pltpu.make_async_copy(depth_ref.at[rows], depth.at[rows], gates.at[3 + part])
-        )
+        block = pl.ds(part * half, half)
+        pairs.append((field_ref.at[block], field.at[block]))
+    pairs += [(back_ref.at[device], back), (modes_ref, to_modes), (cells_ref, to_cells)]
+    copies = [
+        pltpu.make_async_copy(source, target, gates.at[turn])
+        for turn, (source, target) in enumerate(pairs)
+    ]
     for copy in copies:
         copy.start()
     copies[0].wait()
-    matrix = forward_matrix(table[...], rows_x, rows_y)
+    fill_depth(rows, depth)
     copies[1].wait()
-    copies[2].wait()
-    planes = y_spectrum(field[...], matrix)
-    for copy in copies[3:]:
+    mixing_ref[...] = mixing_matrix(point)
+    for copy in copies[2:5]:
         copy.wait()
-    z_spectrum(planes, depth, out_ref, rows_x)
-
-
-def product_kernel(
-    x_parts, y_parts, in_ref, forward_ref, inverse_ref, weight_ref, out_ref, spec_ref, scratch
-):
-    spec_ref[...] = own_spectrum(in_ref, forward_ref, x_parts, y_parts)
+    z_spectrum(y_spectrum(field[...], table[...], rows_x, rows_y), depth, out_refs, rows_x)
+    for copy in copies[5:]:
+        copy.wait()
+
+
+def x_forward_kernel(turns, table_ref, *refs):
+    in_refs, refs = refs[:turns], refs[turns:]
+    rows = table_ref.shape[2] // 3
+    own = lax.axis_index("gx")
+    total = None
+    for turn in range(turns):
+        term = dot(table_ref[own ^ turn], tripled(read_lanes(in_refs[turn], rows)))
+        total = term if total is None else total + term
+    modes = 2 * KX
+    steps = total.shape[0] // modes
+    for step, ref in enumerate(refs[-steps:]):
+        write_lanes(ref, total[step * modes : (step + 1) * modes], modes)
+        if len(refs) > steps:
+            ref[CHUNKS * modes :, :] = refs[0][...]
+
+
+def x_inverse_kernel(steps, turns, table_ref, *refs):
+    in_refs, refs = refs[:steps], refs[steps:]
+    values = tripled(jnp.concatenate([read_lanes(ref, 2 * KX) for ref in in_refs], axis=0))
+    own = lax.axis_index("gx")
+    rows = table_ref.shape[1]
+    for turn, ref in enumerate(refs[-turns:]):
+        write_lanes(ref, dot(table_ref[own ^ turn], values), rows)
+        if len(refs) > turns:
+            ref[CHUNKS * rows :, :] = refs[0][...]
+
+
+def summed_modes(in_refs):
+    return functools.reduce(jnp.add, [read_lanes(ref, 2 * KX) for ref in in_refs])
+
+
+def product_kernel(steps, weight_ref, *refs):
+    in_refs, (out_ref, spec_ref, scratch) = refs[:steps], refs[steps:]
+    spec_ref[...] = summed_modes(in_refs)
     keep = own_group()
 
     def step(mode, carry):
@@ -462,44 +503,45 @@
         return carry
 
     lax.fori_loop(0, KX, step, 0, unroll=4)
-    spread_modes(gathered_rows(scratch) * depth_factor(), inverse_ref, out_ref, x_parts, y_parts)
+    write_lanes(out_ref, gathered_rows(scratch) * depth_factor(), 2 * KX)
+
+
+def point_kernel(field_ref, mixing_ref, bias_ref, out_ref):
+    bias = jnp.concatenate([bias_ref[...]] * NZ, axis=1)
+    out_ref[...] = mixed(field_ref[...], mixing_ref[...], ((1,), (0,))) + bias
 
 
 def middle_kernel(
     rows_x,
     rows_y,
-    in_ref,
-    field_ref,
+    turns,
+    base_ref,
     cotangent_ref,
-    point_ref,
-    bias_ref,
     table_ref,
     back_ref,
     depth_ref,
-    out_ref,
-    adjoint_ref,
-    sums_ref,
-    held,
-    gate,
+    *refs,
 ):
-    matrix = inverse_matrix(back_ref, rows_x, rows_y)
-    spectral = dot(matrix, z_synthesis(in_ref, depth_ref, rows_x))
-    mixing = mixing_matrix(point_ref)
-    field = field_ref[...]
-    bias = jnp.concatenate([bias_ref[...]] * NZ, axis=1)
-    value = spectral + mixed(field, mixing, ((1,), (0,))) + bias
+    in_refs, out_refs, (adjoint_ref, value_ref) = refs[:turns], refs[turns:-2], refs[-2:]
+    planes = z_synthesis(in_refs, depth_ref, rows_x)
+    for x in range(rows_x):
+        block = slice(x * rows_y, (x + 1) * rows_y)
+        spectral = y_synthesis(planes, back_ref[...], x, rows_x)
+        value_ref[block, :] = spectral + base_ref[block, :]
+    value = value_ref[...]
     root = math.sqrt(2.0 / math.pi)
     square = value * value
     bent = jnp.tanh(value * (root + (root * 0.044715) * square))
-    slope = 0.5 * (1.0 + bent) + (0.5 * value) * (1.0 - bent * bent) * (
-        root + (3.0 * root * 0.044715) * square
-    )
+    tail = value * (root + (3.0 * root * 0.044715) * square)
+    slope = (0.5 + 0.5 * bent) * (1.0 + (1.0 - bent) * tail)
     adjoint = (cotangent_ref[...].astype(F32) * slope).astype(BF)
-    held[...] = adjoint
-    copy = pltpu.make_async_copy(held, adjoint_ref, gate)
-    copy.start()
-    matrix = forward_matrix(table_ref[lax.axis_index("gy")], rows_x, rows_y)
-    z_spectrum(y_spectrum(adjoint, matrix), depth_ref, out_ref, rows_x)
+    adjoint_ref[...] = adjoint
+    z_spectrum(y_spectrum(adjoint, table_ref[...], rows_x, rows_y), depth_ref, out_refs, rows_x)
+
+
+def sums_kernel(field_ref, adjoint_ref, mixing_ref, out_ref, sums_ref):
+    field, adjoint, mixing = field_ref[...], adjoint_ref[...], mixing_ref[...]
+    out_ref[...] = mixed(adjoint, mixing, ((1,), (1,)))
     wide = mixing.shape[0]
     total = jnp.zeros((wide, wide), F32)
     for start in range(0, NZ * C, wide):
@@ -517,28 +559,16 @@
         packed = jnp.where(group == part, point[part * 8 : (part + 1) * 8], packed)
     sums_ref[:8, :] = packed
     sums_ref[8:, :] = folded(dot(jnp.ones((8, adjoint.shape[0]), BF), adjoint))
-    copy.wait()
 
 
 def swapped(values, index, distance):
     return lane_take(values, index ^ distance)
 
 
-def adjoint_kernel(
-    x_parts,
-    y_parts,
-    in_ref,
-    forward_ref,
-    inverse_ref,
-    weight_ref,
-    sums_ref,
-    out_ref,
-    spec_ref,
-    scratch,
-    staged,
-    gates,
-):
-    spec_ref[...] = own_spectrum(in_ref, forward_ref, x_parts, y_parts) * depth_factor()
+def adjoint_kernel(steps, weight_ref, *refs):
+    in_refs, (out_ref, spec_ref, sums_ref, scratch) = refs[:steps], refs[steps:]
+    spec_ref[...] = summed_modes(in_refs) * depth_factor()
+    sums_ref[...] = functools.reduce(jnp.add, [ref[CHUNKS * 2 * KX :, :] for ref in in_refs])
     keep = own_group()
     lane = iota((KZ, LANES), 1)
     final = lane % C % 4 * C + lane % C // 4 * 4
@@ -577,20 +607,7 @@
         return carry
 
     lax.fori_loop(0, KX, step, 0, unroll=4)
-    for device in range(x_parts * y_parts):
-        staged[device, DATA_ROWS:, :] = sums_ref[...]
-    stores = []
-
-    def send(x_part):
-        block = pl.ds(x_part * y_parts, y_parts)
-        stores.append(
-            pltpu.make_async_copy(staged.at[block], out_ref.at[block], gates.at[x_part])
-        )
-        stores[-1].start()
-
-    spread_modes(gathered_rows(scratch), inverse_ref, staged, x_parts, y_parts, send)
-    for store in stores:
-        store.wait()
+    write_lanes(out_ref, gathered_rows(scratch), 2 * KX)
 
 
 def weight_kernel(scale, field_ref, adjoint_ref, out_ref, staged, gates):
@@ -625,49 +642,30 @@
         store.wait()
 
 
-def last_kernel(
-    rows_x,
-    rows_y,
-    scale,
-    in_ref,
-    adjoint_ref,
-    point_ref,
-    back_ref,
-    depth_ref,
-    out_ref,
-    grad_ref,
-    bias_ref,
-    adjoint,
-    result,
-    gate,
-    gates,
-):
-    fetch = pltpu.make_async_copy(adjoint_ref, adjoint, gate)
-    fetch.start()
-    total = in_ref[0, DATA_ROWS:, :]
-    for device in range(1, in_ref.shape[0]):
-        total = total + in_ref[device, DATA_ROWS:, :]
+def last_kernel(rows_x, rows_y, turns, scale, mixed_ref, back_ref, depth_ref, *refs):
+    in_refs, (out_ref, point_ref, bias_ref, result, gates) = refs[:turns], refs[turns:]
+    total = functools.reduce(jnp.add, [ref[ref.shape[0] - SUM_ROWS :, :] for ref in in_refs])
     total = total * scale
     packed = total[:8]
     for part in range(4):
         piece = packed if part == 0 else pltpu.roll(packed, LANES - part * C, 1)
-        grad_ref[part * 8 : (part + 1) * 8, :] = piece[:, :C]
+        point_ref[part * 8 : (part + 1) * 8, :] = piece[:, :C]
     bias_ref[...] = total[8:9, :C]
-    matrix = inverse_matrix(back_ref, rows_x, rows_y)
-    planes = z_synthesis(in_ref, depth_ref, rows_x)
-    mixing = mixing_matrix(point_ref)
-    fetch.wait()
+    planes = z_synthesis(in_refs, depth_ref, rows_x)
     stores = []
-    rows = result.shape[0] // gates.shape[0]
-    for part in range(gates.shape[0]):
-        block = pl.ds(part * rows, rows)
-        mix = mixed(adjoint[block, :], mixing, ((1,), (1,)))
-        spectral = dot(matrix[part * rows : (part + 1) * rows], planes)
-        result[block, :] = (mix + spectral).astype(BF)
-        stores.append(
-            pltpu.make_async_copy(result.at[block], out_ref.at[block], gates.at[part])
-        )
-        stores[-1].start()
+    parts = gates.shape[0]
+    for x in range(rows_x):
+        block = slice(x * rows_y, (x + 1) * rows_y)
+        spectral = y_synthesis(planes, back_ref[...], x, rows_x)
+        result[block, :] = (mixed_ref[block, :] + spectral).astype(BF)
+        if (x + 1) % (rows_x // parts) == 0:
+            part = (x + 1) // (rows_x // parts) - 1
+            rows = result.shape[0] // parts
+            span = pl.ds(part * rows, rows)
+            stores.append(
+                pltpu.make_async_copy(result.at[span], out_ref.at[span], gates.at[part])
+            )
+            stores[-1].start()
     for store in stores:
         store.wait()
 
@@ -699,84 +697,110 @@
     return run
 
 
-def exchange(values):
-    return lax.all_to_all(values, ("gx", "gy"), split_axis=0, concat_axis=0, tiled=True)
+def exchange(blocks, axis):
+    count = lax.axis_size(axis)
+    order = [2, 3, 1] if count == 4 else list(range(1, count))
+    received = list(blocks)
+    for turn in order:
+        pairs = [(device, device ^ turn) for device in range(count)]
+        received[turn] = lax.ppermute(blocks[turn], axis, pairs)
+    return received
 
 
 def fast_device(field_input, cotangent, spectral_weight, point_weight, point_bias):
     rows_x, rows_y, depth = field_input.shape
     x_parts, y_parts = lax.axis_size("gx"), lax.axis_size("gy")
-    devices = x_parts * y_parts
     full_x, full_y = rows_x * x_parts, rows_y * y_parts
     scale = 1.0 / math.sqrt(full_x * full_y * NZ)
     cells = rows_x * rows_y
-    depth_table = jnp.asarray(depth_matrix())
-    forward_y, inverse_y = map(jnp.asarray, y_tables(full_y, rows_y, rows_x, y_parts))
-    forward_x, inverse_x = map(jnp.asarray, x_tables(full_x, rows_x, scale))
+    z_rows = jnp.asarray(depth_rows())
+    forward_y, inverse_y = map(jnp.asarray, y_tables(full_y, rows_y, x_parts, y_parts))
+    forward_x, inverse_x = map(jnp.asarray, x_tables(full_x, rows_x, scale, y_parts))
     field = field_input.reshape(cells, depth)
     bias = point_bias.reshape(1, C)
-    payload = ((devices, DATA_ROWS, LANES), F32, True)
+    cell_rows, mode_rows = CHUNKS * rows_x * 8, CHUNKS * 2 * KX
+    cell_block, mode_block = ((cell_rows, LANES), F32, True), ((mode_rows, LANES), F32, True)
+    cell_sums = ((cell_rows + SUM_ROWS, LANES), F32, True)
+    mode_sums = ((mode_rows + SUM_ROWS, LANES), F32, True)
     spectrum_shape = ((2 * KX, WIDE), F32, True)
     rows_scratch = pltpu.VMEM((2 * KX * KZ, LANES), F32)
-    plane = pltpu.VMEM((cells, depth), BF)
-    gate = pltpu.SemaphoreType.DMA(())
-
-    (sent,) = call(
+    sums_shape = ((SUM_ROWS, LANES), F32, True)
+    cell_shape = ((cells, depth), F32, True)
+    wide = (KZ, KX * 2 * C * C)
+
+    def forward(blocks, extra, mode_shape):
+        received = exchange(blocks, "gx")
+        sent = call(
+            functools.partial(x_forward_kernel, x_parts),
+            [True] * (1 + x_parts + len(extra)),
+            [mode_shape] * y_parts,
+        )(to_modes, *received, *extra)
+        return exchange(sent, "gy")
+
+    def inverse(block, extra, cell_shape):
+        received = exchange([block] * y_parts, "gy")
+        sent = call(
+            functools.partial(x_inverse_kernel, y_parts, x_parts),
+            [True] * (1 + y_parts + len(extra)),
+            [cell_shape] * x_parts,
+        )(to_cells, *received, *extra)
+        return exchange(sent, "gx")
+
+    *blocks, depth_table, mixing, table, back, to_modes, to_cells = call(
         functools.partial(first_kernel, rows_x, rows_y),
-        [False] * 3,
-        [payload],
+        [False] * 7,
+        [cell_block] * x_parts
+        + [((depth, 2 * WIDE), BF, True), ((8 * C, 8 * C), BF, True)]
+        + [(part.shape[1:], BF, True) for part in (forward_y, inverse_y)]
+        + [(part.shape, BF, True) for part in (forward_x, inverse_x)],
         [
-            plane,
-            pltpu.VMEM(forward_y.shape[1:], F32),
-            pltpu.VMEM(depth_table.shape, BF),
-            pltpu.SemaphoreType.DMA((7,)),
+            pltpu.VMEM((cells, depth), BF),
+            pltpu.VMEM(z_rows.shape, F32),
+            pltpu.VMEM((C, C), BF),
+            pltpu.SemaphoreType.DMA((8,)),
         ],
-    )(field, forward_y, depth_table)
-    sent, field_modes = call(
-        functools.partial(product_kernel, x_parts, y_parts),
-        [True] * 4,
-        [payload, spectrum_shape],
+    )(field, forward_y, z_rows, point_weight, inverse_y, forward_x, inverse_x)
+    (base,) = call(point_kernel, [True] * 3, [cell_shape])(field, mixing, bias)
+    block, field_modes = call(
+        functools.partial(product_kernel, y_parts),
+        [True] * (1 + y_parts),
+        [mode_block, spectrum_shape],
         [rows_scratch],
-    )(exchange(sent), forward_x, inverse_x, spectral_weight)
-    sent, adjoint, sums = call(
-        functools.partial(middle_kernel, rows_x, rows_y),
-        [True] * 8,
-        [payload, ((cells, depth), BF, False), ((SUM_ROWS, LANES), F32, True)],
-        [plane, gate],
+    )(spectral_weight, *forward(blocks, [], mode_block))
+    *blocks, adjoint = call(
+        functools.partial(middle_kernel, rows_x, rows_y, x_parts),
+        [True] * (5 + x_parts),
+        [cell_block] * x_parts + [((cells, depth), BF, True)],
+        [pltpu.VMEM((cells, depth), F32)],
     )(
-        exchange(sent),
-        field,
+        base,
         cotangent.reshape(cells, depth),
-        point_weight,
-        bias,
-        forward_y,
-        inverse_y,
+        table,
+        back,
         depth_table,
-    )
-    sent, adjoint_modes = call(
-        functools.partial(adjoint_kernel, x_parts, y_parts),
-        [True] * 5,
-        [((devices, DATA_ROWS + SUM_ROWS, LANES), F32, False), spectrum_shape],
-        [
-            rows_scratch,
-            pltpu.VMEM((devices, DATA_ROWS + SUM_ROWS, LANES), F32),
-            pltpu.SemaphoreType.DMA((x_parts,)),
-        ],
-    )(exchange(sent), forward_x, inverse_x, spectral_weight, sums)
-    wide = (KZ, KX * 2 * C * C)
+        *inverse(block, [], cell_block),
+    )
+    mixed_adjoint, sums = call(sums_kernel, [True] * 3, [cell_shape, sums_shape])(
+        field, adjoint, mixing
+    )
+    block, adjoint_modes, sums = call(
+        functools.partial(adjoint_kernel, y_parts),
+        [True] * (1 + y_parts),
+        [mode_block, spectrum_shape, sums_shape],
+        [rows_scratch],
+    )(spectral_weight, *forward(blocks, [sums], mode_sums))
     (grad_spectral,) = call(
         functools.partial(weight_kernel, scale),
-        [True, True],
+        [True] * 2,
         [(wide, F32, False)],
         [pltpu.VMEM(wide, F32), pltpu.SemaphoreType.DMA((4,))],
     )(field_modes, adjoint_modes)
-    chunks = 4
     grad_field, grad_point, grad_bias = call(
-        functools.partial(last_kernel, rows_x, rows_y, scale),
-        [True, False, True, True, True],
+        functools.partial(last_kernel, rows_x, rows_y, x_parts, scale),
+        [True] * (3 + x_parts),
         [((cells, depth), BF, False), ((C, C), F32, None), ((1, C), F32, None)],
-        [plane, plane, gate, pltpu.SemaphoreType.DMA((chunks,))],
-    )(exchange(sent), adjoint, point_weight, inverse_y, depth_table)
+        [pltpu.VMEM((cells, depth), BF), pltpu.SemaphoreType.DMA((4,))],
+    )(mixed_adjoint, back, depth_table, *inverse(block, [sums], cell_sums))
     return (
         grad_field.reshape(field_input.shape),
         grad_spectral,
@@ -787,7 +811,9 @@
 
 def on_device(*arguments):
     rows_x, rows_y, _ = arguments[0].shape
-    if rows_x == 8 and rows_y == 64 and arguments[2].shape[0] == KZ:
+    x_parts, y_parts = lax.axis_size("gx"), lax.axis_size("gy")
+    whole_modes = arguments[2].shape[0] == KZ and y_parts == 4 and x_parts == 4
+    if whole_modes and rows_x == 8 and rows_y == 64:
         return fast_device(*arguments)
     return general_device(*arguments)
 

time: 105 us -> 89.5 us (0.85)
  blocking collectives: 60.9 us -> 0 us
  waiting for transfers between devices: 15.6 us -> 40.6 us
  starting transfers between devices: 3.61 us -> 26.8 us
  Pallas kernels: 23.8 us -> 21.2 us
    all_to_all x3 -> x0, blocking collectives: 60.9 us -> none  [exchange(): lax.all_to_all(values, ('gx', 'gy'), split_axis=0, concat_axis=0, tiled=T...]
    ppermute x0 -> x24, waiting for transfers between devices: none -> 40.6 us  [exchange(): received[turn] = lax.ppermute(blocks[turn], axis, pairs)]
    ppermute x0 -> x24, starting transfers between devices: none -> 26.8 us  [exchange(): received[turn] = lax.ppermute(blocks[turn], axis, pairs)]
    all_to_all x1 -> x0, waiting for transfers between devices: 15.6 us -> none  [exchange(): lax.all_to_all(values, ('gx', 'gy'), split_axis=0, concat_axis=0, tiled=T...]
    all_to_all x1 -> x0, starting transfers between devices: 3.61 us -> none  [exchange(): lax.all_to_all(values, ('gx', 'gy'), split_axis=0, concat_axis=0, tiled=T...]
    pallas_call x6 -> x12, Pallas kernels: 23.8 us -> 21.2 us  [run(): return function(*map(pltpu.with_memory_space_constraint, arguments, spaces))]
  transfers between devices with their start and end apart: 1 -> 24, of which waited for: 1 -> 16; matrix products, arithmetic and copies ran while one was open for 0% -> 0% of each run, Pallas kernels for 3% -> 5%
where the time goes in v2:
time: 89.5 us; the launch traced here: 89.4 us
  waiting for transfers between devices  40.6 us (45%)
  starting transfers between devices  26.8 us (30%)
  Pallas kernels  21.2 us (24%)
    ppermute x24, waiting for transfers between devices, exchange(): received[turn] = lax.ppermute(blocks[turn], axis, pairs)  40.6 us
    ppermute x24, starting transfers between devices, exchange(): received[turn] = lax.ppermute(blocks[turn], axis, pairs)  26.8 us
    pallas_call x12, Pallas kernels, run(): return function(*map(pltpu.with_memory_space_constraint, arguments, spaces))  21.2 us
  transfers between devices with their start and end apart: 24, of which 16 were waited for; matrix products, arithmetic and copies ran while one was open for 0% of the time, Pallas kernels for 5%

profile of v2, /device:TPU:0, one launch (start us, length us, event | category | flops | bytes accessed | tf_op | source)
XLA Modules:
  0.0 89.4 jit_solution(16823165287225483661)
XLA Ops:
  0.7 3.3 %shard_map.129 = (f32[256,128]{1,0:T(8,128)S(1)}, f32[256,128]{1,0:T(8,128)S(1)}, f32[256,128]{1,0:T(8,128)S(1)}, f32[256,128]{1,0:T(8,128)S(1)}, bf16[1024,1024...) custom-call(bf16[512,1024]{1,0:T(8,128)(2,1)} %bitcast.5, ...), custom_call_target="tpu_custom_call" | custom-call | tf_op jit(solution)/shard_map/pallas_call | solution.py:695
  4.5 2.6 %collective-permute-start.1 = (f32[256,128]{1,0:T(8,128)S(1)}, f32[256,128]{1,0:T(8,128)S(1)}, u32[]{:S(2)}, u32[]{:S(2)}) collective-permute-start(f32[256,128]{1,0:T(8,128)S(1)} %get-tuple-element.53), channel_id=1, source_target_pairs={{0,8},{4,12},{8,0},{12,4},{1,9},{5,13},{9,1},{13,5},{2,10},{6,14},... | collective-permute-start | bytes 393224 | tf_op jit(solution)/shard_map/ppermute | solution.py:706
  7.2 4.3 %collective-permute-done.1.refs_2_ = f32[256,128]{1,0:T(8,128)S(1)} collective-permute-done((f32[256,128]{1,0:T(8,128)S(1)}, f32[256,128]{1,0:T(8,128)S(1)}, u32[]{:S(2)}, u32[]{:S(2)}) %collective-permute-start.1) | collective-permute-done | bytes 131104 | tf_op jit(solution)/shard_map/ppermute | solution.py:706
  11.5 2.3 %collective-permute-done.2.refs_3_ = f32[256,128]{1,0:T(8,128)S(1)} collective-permute-done((f32[256,128]{1,0:T(8,128)S(1)}, f32[256,128]{1,0:T(8,128)S(1)}, u32[]{:S(2)}, u32[]{:S(2)}) %collective-permute-start.2) | collective-permute-done | bytes 131104 | tf_op jit(solution)/shard_map/ppermute | solution.py:706
  15.7 2.6 %collective-permute-start.4 = (f32[128,128]{1,0:T(8,128)S(1)}, f32[128,128]{1,0:T(8,128)S(1)}, u32[]{:S(2)}, u32[]{:S(2)}) collective-permute-start(f32[128,128]{1,0:T(8,128)S(1)} %get-tuple-element.57), channel_id=1, source_target_pairs={{0,2},{1,3},{2,0},{3,1},{4,6},{5,7},{6,4},{7,5},{8,10},{9,11},{10,... | collective-permute-start | bytes 196616 | tf_op jit(solution)/shard_map/ppermute | solution.py:706
  18.5 4.8 %collective-permute-done.4.refs_2_ = f32[128,128]{1,0:T(8,128)S(1)} collective-permute-done((f32[128,128]{1,0:T(8,128)S(1)}, f32[128,128]{1,0:T(8,128)S(1)}, u32[]{:S(2)}, u32[]{:S(2)}) %collective-permute-start.4) | collective-permute-done | bytes 65568 | tf_op jit(solution)/shard_map/ppermute | solution.py:706
  24.5 2.5 %shard_map.132 = (f32[128,128]{1,0:T(8,128)S(1)}, f32[32,512]{1,0:T(8,128)S(1)}) custom-call(bf16[16,32768]{1,0:T(8,128)(2,1)S(1)} %copy-done.1, f32[128,128]{1,0:T(8,128)S(1)} %get-tuple-element.55.refs_0_, f32[128,128]{1,0:T(8,128)S(1)} %collective-permute-done.3.refs_1_, f32[128,128]{1,0:T(8,128)S(1)} %collective-permute-done.4.refs_2_, ...), custom_call_target="tpu_custom_call" | custom-call | tf_op jit(solution)/shard_map/pallas_call | solution.py:695
  27.1 2.2 %collective-permute-start.8 = (f32[128,128]{1,0:T(8,128)S(1)}, f32[128,128]{1,0:T(8,128)S(1)}, u32[]{:S(2)}, u32[]{:S(2)}) collective-permute-start(f32[128,128]{1,0:T(8,128)S(1)} %get-tuple-element.59.refs_0_), channel_id=1, source_target_pairs={{0,3},{1,2},{2,1},{3,0},{4,7},{5,6},{6,5},{7,4},{8,11},{9,10},{10,... | collective-permute-start | bytes 196616 | tf_op jit(solution)/shard_map/ppermute | solution.py:706
  29.6 1.9 %collective-permute-start.6 = (f32[128,128]{1,0:T(8,128)S(1)}, f32[128,128]{1,0:T(8,128)S(1)}, u32[]{:S(2)}, u32[]{:S(2)}) collective-permute-start(f32[128,128]{1,0:T(8,128)S(1)} %get-tuple-element.59.refs_0_), channel_id=1, source_target_pairs={{0,1},{1,0},{2,3},{3,2},{4,5},{5,4},{6,7},{7,6},{8,9},{9,8},{10,11... | collective-permute-start | bytes 196616 | tf_op jit(solution)/shard_map/ppermute | solution.py:706
  31.5 1.8 %collective-permute-done.8.refs_3_ = f32[128,128]{1,0:T(8,128)S(1)} collective-permute-done((f32[128,128]{1,0:T(8,128)S(1)}, f32[128,128]{1,0:T(8,128)S(1)}, u32[]{:S(2)}, u32[]{:S(2)}) %collective-permute-start.8) | collective-permute-done | bytes 65568 | tf_op jit(solution)/shard_map/ppermute | solution.py:706
  37.8 4.0 %collective-permute-done.10.refs_2_ = f32[256,128]{1,0:T(8,128)S(1)} collective-permute-done((f32[256,128]{1,0:T(8,128)S(1)}, f32[256,128]{1,0:T(8,128)S(1)}, u32[]{:S(2)}, u32[]{:S(2)}) %collective-permute-start.10) | collective-permute-done | bytes 131104 | tf_op jit(solution)/shard_map/ppermute | solution.py:706
  41.8 1.9 %collective-permute-done.11.refs_3_ = f32[256,128]{1,0:T(8,128)S(1)} collective-permute-done((f32[256,128]{1,0:T(8,128)S(1)}, f32[256,128]{1,0:T(8,128)S(1)}, u32[]{:S(2)}, u32[]{:S(2)}) %collective-permute-start.11) | collective-permute-done | bytes 131104 | tf_op jit(solution)/shard_map/ppermute | solution.py:706
  43.7 4.2 %shard_map.134 = (f32[256,128]{1,0:T(8,128)S(1)}, f32[256,128]{1,0:T(8,128)S(1)}, f32[256,128]{1,0:T(8,128)S(1)}, f32[256,128]{1,0:T(8,128)S(1)}, bf16[512,1024]{1,0:T(8,128)(2,1)S(1)}) custom-call(f32[512,1024]{1,0:T(8,128)S(1)} %shard_map.130.base_ref, bf16[512,1024]{1,0:T(8,128)(2,1)S(1)} %bitcast.8, bf16[64,64]{1,0:T(8,128)(2,1)S(1)} %get-tuple-element.46.table_ref, ...), custom_call_target="tpu_custom_call" | custom-call | tf_op jit(solution)/shard_map/pallas_call | solution.py:695
  50.9 3.7 %collective-permute-done.13.refs_2_ = f32[256,128]{1,0:T(8,128)S(1)} collective-permute-done((f32[256,128]{1,0:T(8,128)S(1)}, f32[256,128]{1,0:T(8,128)S(1)}, u32[]{:S(2)}, u32[]{:S(2)}) %collective-permute-start.13) | collective-permute-done | bytes 131104 | tf_op jit(solution)/shard_map/ppermute | solution.py:706
  57.1 1.8 %collective-permute-start.16 = (f32[144,128]{1,0:T(8,128)S(1)}, f32[144,128]{1,0:T(8,128)S(1)}, u32[]{:S(2)}, u32[]{:S(2)}) collective-permute-start(f32[144,128]{1,0:T(8,128)S(1)} %get-tuple-element.73), channel_id=1, source_target_pairs={{0,2},{1,3},{2,0},{3,1},{4,6},{5,7},{6,4},{7,5},{8,10},{9,11},{10,... | collective-permute-start | bytes 221192 | tf_op jit(solution)/shard_map/ppermute | solution.py:706
  58.9 1.8 %collective-permute-start.17 = (f32[144,128]{1,0:T(8,128)S(1)}, f32[144,128]{1,0:T(8,128)S(1)}, u32[]{:S(2)}, u32[]{:S(2)}) collective-permute-start(f32[144,128]{1,0:T(8,128)S(1)} %get-tuple-element.74), channel_id=1, source_target_pairs={{0,3},{1,2},{2,1},{3,0},{4,7},{5,6},{6,5},{7,4},{8,11},{9,10},{10,... | collective-permute-start | bytes 221192 | tf_op jit(solution)/shard_map/ppermute | solution.py:706
  61.9 4.4 %collective-permute-done.16.refs_2_ = f32[144,128]{1,0:T(8,128)S(1)} collective-permute-done((f32[144,128]{1,0:T(8,128)S(1)}, f32[144,128]{1,0:T(8,128)S(1)}, u32[]{:S(2)}, u32[]{:S(2)}) %collective-permute-start.16) | collective-permute-done | bytes 73760 | tf_op jit(solution)/shard_map/ppermute | solution.py:706
  66.3 2.5 %shard_map.137 = (f32[128,128]{1,0:T(8,128)S(1)}, f32[32,512]{1,0:T(8,128)S(1)}, f32[16,128]{1,0:T(8,128)S(1)}) custom-call(bf16[16,32768]{1,0:T(8,128)(2,1)S(1)} %copy-done.1, f32[144,128]{1,0:T(8,128)S(1)} %get-tuple-element.71.refs_0_, f32[144,128]{1,0:T(8,128)S(1)} %collective-permute-done.15.refs_1_, f32[144,128]{1,0:T(8,128)S(1)} %collective-permute-done.16.refs_2_, ...), custom_call_target="tpu_custom_call" | custom-call | tf_op jit(solution)/shard_map/pallas_call | solution.py:695
  68.8 2.1 %collective-permute-start.20 = (f32[128,128]{1,0:T(8,128)S(1)}, f32[128,128]{1,0:T(8,128)S(1)}, u32[]{:S(2)}, u32[]{:S(2)}) collective-permute-start(f32[128,128]{1,0:T(8,128)S(1)} %get-tuple-element.75.refs_0_), channel_id=1, source_target_pairs={{0,3},{1,2},{2,1},{3,0},{4,7},{5,6},{6,5},{7,4},{8,11},{9,10},{10,... | collective-permute-start | bytes 196616 | tf_op jit(solution)/shard_map/ppermute | solution.py:706
  73.2 2.3 %collective-permute-done.20.refs_3_ = f32[128,128]{1,0:T(8,128)S(1)} collective-permute-done((f32[128,128]{1,0:T(8,128)S(1)}, f32[128,128]{1,0:T(8,128)S(1)}, u32[]{:S(2)}, u32[]{:S(2)}) %collective-permute-start.20) | collective-permute-done | bytes 65568 | tf_op jit(solution)/shard_map/ppermute | solution.py:706
  79.6 2.8 %shard_map.140 = f32[16,32768]{1,0:T(8,128)} custom-call(f32[32,512]{1,0:T(8,128)S(1)} %get-tuple-element.82.field_ref, f32[32,512]{1,0:T(8,128)S(1)} %get-tuple-element.83.adjoint_ref), custom_call_target="tpu_custom_call" | custom-call | tf_op jit(solution)/shard_map/pallas_call | solution.py:695
  82.4 1.8 %collective-permute-done.22.refs_2_ = f32[272,128]{1,0:T(8,128)S(1)} collective-permute-done((f32[272,128]{1,0:T(8,128)S(1)}, f32[272,128]{1,0:T(8,128)S(1)}, u32[]{:S(2)}, u32[]{:S(2)}) %collective-permute-start.22) | collective-permute-done | bytes 139296 | tf_op jit(solution)/shard_map/ppermute | solution.py:706
  84.2 2.1 %collective-permute-done.23.refs_3_ = f32[272,128]{1,0:T(8,128)S(1)} collective-permute-done((f32[272,128]{1,0:T(8,128)S(1)}, f32[272,128]{1,0:T(8,128)S(1)}, u32[]{:S(2)}, u32[]{:S(2)}) %collective-permute-start.23) | collective-permute-done | bytes 139296 | tf_op jit(solution)/shard_map/ppermute | solution.py:706
  86.3 3.1 %shard_map.139 = (bf16[512,1024]{1,0:T(8,128)(2,1)}, f32[32,32]{1,0:T(8,128)}, f32[1,32]{1,0:T(1,128)}) custom-call(f32[512,1024]{1,0:T(8,128)S(1)} %get-tuple-element.65.mixed_ref, bf16[64,96]{1,0:T(8,128)(2,1)S(1)} %get-tuple-element.47.back_ref, bf16[1024,1024]{1,0:T(8,128)(2,1)S(1)} %get-tuple-element.48.depth_ref, ...), custom_call_target="tpu_custom_call" | custom-call | tf_op jit(solution)/shard_map/pallas_call | solution.py:695
  (44 shorter events, 21.6 us)
Async XLA Ops:
  4.0 3.2 %collective-permute-start = (f32[256,128]{1,0:T(8,128)S(1)}, f32[256,128]{1,0:T(8,128)S(1)}, u32[]{:S(2)}, u32[]{:S(2)}) collective-permute-start(f32[256,128]{1,0:T(8,128)S(1)} %get-tuple-element.52), channel_id=1, source_target_pairs={{0,4},{4,0},{8,12},{12,8},{1,5},{5,1},{9,13},{13,9},{2,6},{6,2},{1... | collective-permute-start | bytes 393224 | tf_op jit(solution)/shard_map/ppermute | solution.py:706
  4.5 6.9 %collective-permute-start.1 = (f32[256,128]{1,0:T(8,128)S(1)}, f32[256,128]{1,0:T(8,128)S(1)}, u32[]{:S(2)}, u32[]{:S(2)}) collective-permute-start(f32[256,128]{1,0:T(8,128)S(1)} %get-tuple-element.53), channel_id=1, source_target_pairs={{0,8},{4,12},{8,0},{12,4},{1,9},{5,13},{9,1},{13,5},{2,10},{6,14},... | collective-permute-start | bytes 393224 | tf_op jit(solution)/shard_map/ppermute | solution.py:706
  7.1 6.6 %collective-permute-start.2 = (f32[256,128]{1,0:T(8,128)S(1)}, f32[256,128]{1,0:T(8,128)S(1)}, u32[]{:S(2)}, u32[]{:S(2)}) collective-permute-start(f32[256,128]{1,0:T(8,128)S(1)} %get-tuple-element.54), channel_id=1, source_target_pairs={{0,12},{4,8},{8,4},{12,0},{1,13},{5,9},{9,5},{13,1},{2,14},{6,10},... | collective-permute-start | bytes 393224 | tf_op jit(solution)/shard_map/ppermute | solution.py:706
  14.1 4.5 %collective-permute-start.3 = (f32[128,128]{1,0:T(8,128)S(1)}, f32[128,128]{1,0:T(8,128)S(1)}, u32[]{:S(2)}, u32[]{:S(2)}) collective-permute-start(f32[128,128]{1,0:T(8,128)S(1)} %get-tuple-element.56), channel_id=1, source_target_pairs={{0,1},{1,0},{2,3},{3,2},{4,5},{5,4},{6,7},{7,6},{8,9},{9,8},{10,11... | collective-permute-start | bytes 196616 | tf_op jit(solution)/shard_map/ppermute | solution.py:706
  15.7 7.6 %collective-permute-start.4 = (f32[128,128]{1,0:T(8,128)S(1)}, f32[128,128]{1,0:T(8,128)S(1)}, u32[]{:S(2)}, u32[]{:S(2)}) collective-permute-start(f32[128,128]{1,0:T(8,128)S(1)} %get-tuple-element.57), channel_id=1, source_target_pairs={{0,2},{1,3},{2,0},{3,1},{4,6},{5,7},{6,4},{7,5},{8,10},{9,11},{10,... | collective-permute-start | bytes 196616 | tf_op jit(solution)/shard_map/ppermute | solution.py:706
  18.3 6.2 %collective-permute-start.5 = (f32[128,128]{1,0:T(8,128)S(1)}, f32[128,128]{1,0:T(8,128)S(1)}, u32[]{:S(2)}, u32[]{:S(2)}) collective-permute-start(f32[128,128]{1,0:T(8,128)S(1)} %get-tuple-element.58), channel_id=1, source_target_pairs={{0,3},{1,2},{2,1},{3,0},{4,7},{5,6},{6,5},{7,4},{8,11},{9,10},{10,... | collective-permute-start | bytes 196616 | tf_op jit(solution)/shard_map/ppermute | solution.py:706
  27.1 6.3 %collective-permute-start.8 = (f32[128,128]{1,0:T(8,128)S(1)}, f32[128,128]{1,0:T(8,128)S(1)}, u32[]{:S(2)}, u32[]{:S(2)}) collective-permute-start(f32[128,128]{1,0:T(8,128)S(1)} %get-tuple-element.59.refs_0_), channel_id=1, source_target_pairs={{0,3},{1,2},{2,1},{3,0},{4,7},{5,6},{6,5},{7,4},{8,11},{9,10},{10,... | collective-permute-start | bytes 196616 | tf_op jit(solution)/shard_map/ppermute | solution.py:706
  29.2 5.7 %collective-permute-start.7 = (f32[128,128]{1,0:T(8,128)S(1)}, f32[128,128]{1,0:T(8,128)S(1)}, u32[]{:S(2)}, u32[]{:S(2)}) collective-permute-start(f32[128,128]{1,0:T(8,128)S(1)} %get-tuple-element.59.refs_0_), channel_id=1, source_target_pairs={{0,2},{1,3},{2,0},{3,1},{4,6},{5,7},{6,4},{7,5},{8,10},{9,11},{10,... | collective-permute-start | bytes 196616 | tf_op jit(solution)/shard_map/ppermute | solution.py:706
  29.6 5.4 %collective-permute-start.6 = (f32[128,128]{1,0:T(8,128)S(1)}, f32[128,128]{1,0:T(8,128)S(1)}, u32[]{:S(2)}, u32[]{:S(2)}) collective-permute-start(f32[128,128]{1,0:T(8,128)S(1)} %get-tuple-element.59.refs_0_), channel_id=1, source_target_pairs={{0,1},{1,0},{2,3},{3,2},{4,5},{5,4},{6,7},{7,6},{8,9},{9,8},{10,11... | collective-permute-start | bytes 196616 | tf_op jit(solution)/shard_map/ppermute | solution.py:706
  35.4 2.4 %collective-permute-start.9 = (f32[256,128]{1,0:T(8,128)S(1)}, f32[256,128]{1,0:T(8,128)S(1)}, u32[]{:S(2)}, u32[]{:S(2)}) collective-permute-start(f32[256,128]{1,0:T(8,128)S(1)} %get-tuple-element.61), channel_id=1, source_target_pairs={{0,4},{4,0},{8,12},{12,8},{1,5},{5,1},{9,13},{13,9},{2,6},{6,2},{1... | collective-permute-start | bytes 393224 | tf_op jit(solution)/shard_map/ppermute | solution.py:706
  35.5 6.4 %collective-permute-start.10 = (f32[256,128]{1,0:T(8,128)S(1)}, f32[256,128]{1,0:T(8,128)S(1)}, u32[]{:S(2)}, u32[]{:S(2)}) collective-permute-start(f32[256,128]{1,0:T(8,128)S(1)} %get-tuple-element.62), channel_id=1, source_target_pairs={{0,8},{4,12},{8,0},{12,4},{1,9},{5,13},{9,1},{13,5},{2,10},{6,14},... | collective-permute-start | bytes 393224 | tf_op jit(solution)/shard_map/ppermute | solution.py:706
  37.1 6.7 %collective-permute-start.11 = (f32[256,128]{1,0:T(8,128)S(1)}, f32[256,128]{1,0:T(8,128)S(1)}, u32[]{:S(2)}, u32[]{:S(2)}) collective-permute-start(f32[256,128]{1,0:T(8,128)S(1)} %get-tuple-element.63), channel_id=1, source_target_pairs={{0,12},{4,8},{8,4},{12,0},{1,13},{5,9},{9,5},{13,1},{2,14},{6,10},... | collective-permute-start | bytes 393224 | tf_op jit(solution)/shard_map/ppermute | solution.py:706
  47.9 3.0 %collective-permute-start.12 = (f32[256,128]{1,0:T(8,128)S(1)}, f32[256,128]{1,0:T(8,128)S(1)}, u32[]{:S(2)}, u32[]{:S(2)}) collective-permute-start(f32[256,128]{1,0:T(8,128)S(1)} %get-tuple-element.67), channel_id=1, source_target_pairs={{0,4},{4,0},{8,12},{12,8},{1,5},{5,1},{9,13},{13,9},{2,6},{6,2},{1... | collective-permute-start | bytes 393224 | tf_op jit(solution)/shard_map/ppermute | solution.py:706
  48.2 6.3 %collective-permute-start.13 = (f32[256,128]{1,0:T(8,128)S(1)}, f32[256,128]{1,0:T(8,128)S(1)}, u32[]{:S(2)}, u32[]{:S(2)}) collective-permute-start(f32[256,128]{1,0:T(8,128)S(1)} %get-tuple-element.68), channel_id=1, source_target_pairs={{0,8},{4,12},{8,0},{12,4},{1,9},{5,13},{9,1},{13,5},{2,10},{6,14},... | collective-permute-start | bytes 393224 | tf_op jit(solution)/shard_map/ppermute | solution.py:706
  49.8 6.2 %collective-permute-start.14 = (f32[256,128]{1,0:T(8,128)S(1)}, f32[256,128]{1,0:T(8,128)S(1)}, u32[]{:S(2)}, u32[]{:S(2)}) collective-permute-start(f32[256,128]{1,0:T(8,128)S(1)} %get-tuple-element.69), channel_id=1, source_target_pairs={{0,12},{4,8},{8,4},{12,0},{1,13},{5,9},{9,5},{13,1},{2,14},{6,10},... | collective-permute-start | bytes 393224 | tf_op jit(solution)/shard_map/ppermute | solution.py:706
  56.3 5.6 %collective-permute-start.15 = (f32[144,128]{1,0:T(8,128)S(1)}, f32[144,128]{1,0:T(8,128)S(1)}, u32[]{:S(2)}, u32[]{:S(2)}) collective-permute-start(f32[144,128]{1,0:T(8,128)S(1)} %get-tuple-element.72), channel_id=1, source_target_pairs={{0,1},{1,0},{2,3},{3,2},{4,5},{5,4},{6,7},{7,6},{8,9},{9,8},{10,11... | collective-permute-start | bytes 221192 | tf_op jit(solution)/shard_map/ppermute | solution.py:706
  57.1 9.2 %collective-permute-start.16 = (f32[144,128]{1,0:T(8,128)S(1)}, f32[144,128]{1,0:T(8,128)S(1)}, u32[]{:S(2)}, u32[]{:S(2)}) collective-permute-start(f32[144,128]{1,0:T(8,128)S(1)} %get-tuple-element.73), channel_id=1, source_target_pairs={{0,2},{1,3},{2,0},{3,1},{4,6},{5,7},{6,4},{7,5},{8,10},{9,11},{10,... | collective-permute-start | bytes 221192 | tf_op jit(solution)/shard_map/ppermute | solution.py:706
  58.9 7.4 %collective-permute-start.17 = (f32[144,128]{1,0:T(8,128)S(1)}, f32[144,128]{1,0:T(8,128)S(1)}, u32[]{:S(2)}, u32[]{:S(2)}) collective-permute-start(f32[144,128]{1,0:T(8,128)S(1)} %get-tuple-element.74), channel_id=1, source_target_pairs={{0,3},{1,2},{2,1},{3,0},{4,7},{5,6},{6,5},{7,4},{8,11},{9,10},{10,... | collective-permute-start | bytes 221192 | tf_op jit(solution)/shard_map/ppermute | solution.py:706
  68.8 6.8 %collective-permute-start.20 = (f32[128,128]{1,0:T(8,128)S(1)}, f32[128,128]{1,0:T(8,128)S(1)}, u32[]{:S(2)}, u32[]{:S(2)}) collective-permute-start(f32[128,128]{1,0:T(8,128)S(1)} %get-tuple-element.75.refs_0_), channel_id=1, source_target_pairs={{0,3},{1,2},{2,1},{3,0},{4,7},{5,6},{6,5},{7,4},{8,11},{9,10},{10,... | collective-permute-start | bytes 196616 | tf_op jit(solution)/shard_map/ppermute | solution.py:706
  70.9 6.3 %collective-permute-start.19 = (f32[128,128]{1,0:T(8,128)S(1)}, f32[128,128]{1,0:T(8,128)S(1)}, u32[]{:S(2)}, u32[]{:S(2)}) collective-permute-start(f32[128,128]{1,0:T(8,128)S(1)} %get-tuple-element.75.refs_0_), channel_id=1, source_target_pairs={{0,2},{1,3},{2,0},{3,1},{4,6},{5,7},{6,4},{7,5},{8,10},{9,11},{10,... | collective-permute-start | bytes 196616 | tf_op jit(solution)/shard_map/ppermute | solution.py:706
  71.8 5.4 %collective-permute-start.18 = (f32[128,128]{1,0:T(8,128)S(1)}, f32[128,128]{1,0:T(8,128)S(1)}, u32[]{:S(2)}, u32[]{:S(2)}) collective-permute-start(f32[128,128]{1,0:T(8,128)S(1)} %get-tuple-element.75.refs_0_), channel_id=1, source_target_pairs={{0,1},{1,0},{2,3},{3,2},{4,5},{5,4},{6,7},{7,6},{8,9},{9,8},{10,11... | collective-permute-start | bytes 196616 | tf_op jit(solution)/shard_map/ppermute | solution.py:706
  77.6 4.8 %collective-permute-start.21 = (f32[272,128]{1,0:T(8,128)S(1)}, f32[272,128]{1,0:T(8,128)S(1)}, u32[]{:S(2)}, u32[]{:S(2)}) collective-permute-start(f32[272,128]{1,0:T(8,128)S(1)} %get-tuple-element.78), channel_id=1, source_target_pairs={{0,4},{4,0},{8,12},{12,8},{1,5},{5,1},{9,13},{13,9},{2,6},{6,2},{1... | collective-permute-start | bytes 417800 | tf_op jit(solution)/shard_map/ppermute | solution.py:706
  77.7 6.5 %collective-permute-start.22 = (f32[272,128]{1,0:T(8,128)S(1)}, f32[272,128]{1,0:T(8,128)S(1)}, u32[]{:S(2)}, u32[]{:S(2)}) collective-permute-start(f32[272,128]{1,0:T(8,128)S(1)} %get-tuple-element.79), channel_id=1, source_target_pairs={{0,8},{4,12},{8,0},{12,4},{1,9},{5,13},{9,1},{13,5},{2,10},{6,14},... | collective-permute-start | bytes 417800 | tf_op jit(solution)/shard_map/ppermute | solution.py:706
  79.3 7.0 %collective-permute-start.23 = (f32[272,128]{1,0:T(8,128)S(1)}, f32[272,128]{1,0:T(8,128)S(1)}, u32[]{:S(2)}, u32[]{:S(2)}) collective-permute-start(f32[272,128]{1,0:T(8,128)S(1)} %get-tuple-element.80), channel_id=1, source_target_pairs={{0,12},{4,8},{8,4},{12,0},{1,13},{5,9},{9,5},{13,1},{2,14},{6,10},... | collective-permute-start | bytes 417800 | tf_op jit(solution)/shard_map/ppermute | solution.py:706
  (4 other events, 114.0 us)

commit v3 on v2

--- a/solution.py
+++ b/solution.py
@@ -232,6 +232,11 @@
     return np.repeat(table.astype(np.float32).reshape(NZ, 2 * KZ), C, axis=1)
 
 
+def spread_table():
+    hit = np.repeat(np.eye(C, dtype=np.float32), C, axis=1)
+    return np.tile(hit, (LANES // C, 1)).astype(ml_dtypes.bfloat16)
+
+
 def y_tables(full_y, rows_y, x_parts, y_parts):
     angles = np_angles(np.arange(full_y), np_modes(KY, full_y), full_y)
     table = np.stack([np.cos(angles), -np.sin(angles)], axis=-1)
@@ -313,9 +318,8 @@
     return jnp.concatenate(planes, axis=0)
 
 
-def z_spectrum(planes, depth_ref, out_refs, rows_x):
-    both = halved(planes, depth_ref[...], (1, 0))
-    whole = both[:, :WIDE] + part_sign(planes.shape[0]) * turned(both[:, WIDE:])
+def z_spectrum(both, out_refs, rows_x):
+    whole = both[:, :WIDE] + part_sign(both.shape[0]) * turned(both[:, WIDE:])
     turns = len(out_refs)
     for x in range(rows_x):
         for turn in range(turns):
@@ -323,11 +327,14 @@
             write_lanes(out_refs[turn], block, rows_x * 8, x * 8)
 
 
-def z_synthesis(in_refs, depth_ref, rows_x):
+def z_synthesis(in_refs, depth_ref, rows_x, exact=True):
     blocks = [read_lanes(ref, rows_x * 8) for ref in in_refs]
     modes = jnp.concatenate(blocks, axis=0)
     other = -part_sign(modes.shape[0]) * turned(modes)
-    return halved(jnp.concatenate([modes, other], axis=1), depth_ref[...], (1, 1))
+    stacked = jnp.concatenate([modes, other], axis=1)
+    if exact:
+        return halved(stacked, depth_ref[...], (1, 1))
+    return dot(stacked.astype(BF), depth_ref[...], ((1,), (1,)))
 
 
 def y_synthesis(planes, table, x, rows_x):
@@ -422,10 +429,11 @@
     back_ref,
     modes_ref,
     cells_ref,
+    spread_ref,
     *refs,
 ):
-    out_refs, refs = refs[:-10], refs[-10:]
-    depth, mixing_ref, table, back, to_modes, to_cells, field, rows, point, gates = refs
+    out_refs, refs = refs[:-11], refs[-11:]
+    depth, mixing_ref, table, back, to_modes, to_cells, spread, field, rows, point, gates = refs
     device = device_index()
     half = field.shape[0] // 2
     pairs = [(rows_ref, rows), (point_ref, point), (table_ref.at[device], table)]
@@ -433,6 +441,7 @@
         block = pl.ds(part * half, half)
         pairs.append((field_ref.at[block], field.at[block]))
     pairs += [(back_ref.at[device], back), (modes_ref, to_modes), (cells_ref, to_cells)]
+    pairs += [(spread_ref, spread)]
     copies = [
         pltpu.make_async_copy(source, target, gates.at[turn])
         for turn, (source, target) in enumerate(pairs)
@@ -445,7 +454,8 @@
     mixing_ref[...] = mixing_matrix(point)
     for copy in copies[2:5]:
         copy.wait()
-    z_spectrum(y_spectrum(field[...], table[...], rows_x, rows_y), depth, out_refs, rows_x)
+    planes = y_spectrum(field[...], table[...], rows_x, rows_y)
+    z_spectrum(halved(planes, depth[...], (1, 0)), out_refs, rows_x)
     for copy in copies[5:]:
         copy.wait()
 
@@ -481,29 +491,47 @@
     return functools.reduce(jnp.add, [read_lanes(ref, 2 * KX) for ref in in_refs])
 
 
-def product_kernel(steps, weight_ref, *refs):
-    in_refs, (out_ref, spec_ref, scratch) = refs[:steps], refs[steps:]
+def stacked_modes(ref):
+    keep = own_group()
+    rows = [jnp.where(keep, mode_row(ref, row), 0.0) for row in range(2 * KX)]
+    return jnp.concatenate(rows, axis=0)
+
+
+def product_kernel(steps, weight_ref, spread_ref, *refs):
+    in_refs, (out_ref, spec_ref, scratch, wide) = refs[:steps], refs[steps:]
     spec_ref[...] = summed_modes(in_refs)
-    keep = own_group()
+    high, low = halves(stacked_modes(spec_ref))
+    spread = spread_ref[...]
+    wide[...] = dot(
+        jnp.concatenate([high, low], axis=1), jnp.concatenate([spread, spread], axis=0)
+    )
 
     def step(mode, carry):
-        real, imag = mode_row(spec_ref, 2 * mode), mode_row(spec_ref, 2 * mode + 1)
         real_w, imag_w = weight_parts(weight_ref, mode)
+        start = pl.multiple_of(2 * mode * KZ, 2 * KZ)
+        both = wide[pl.ds(start, 2 * KZ), :]
         real_sum = jnp.zeros((KZ, LANES), F32)
         imag_sum = jnp.zeros((KZ, LANES), F32)
         for part in range(C // 4):
-            index = in_index(part)
-            real_v, imag_v = lane_take(real, index), lane_take(imag, index)
+            real_v, imag_v = lanes_of(both[:KZ], part), lanes_of(both[KZ:], part)
             real_p, imag_p = lanes_of(real_w, part), lanes_of(imag_w, part)
             real_sum = real_sum + (real_v * real_p - imag_v * imag_p)
             imag_sum = imag_sum + (real_v * imag_p + imag_v * real_p)
-        for part, total in ((0, real_sum), (1, imag_sum)):
-            start = pl.multiple_of((2 * mode + part) * KZ, KZ)
-            scratch[pl.ds(start, KZ), :] = jnp.where(keep, folded(total), 0.0)
+        scratch[pl.ds(start, 2 * KZ), :] = jnp.concatenate([real_sum, imag_sum], axis=0)
         return carry
 
     lax.fori_loop(0, KX, step, 0, unroll=4)
+    shape = (LANES, LANES)
+    same = (iota(shape, 0) % C == iota(shape, 1) % C).astype(F32).astype(BF)
+    high, low = halves(scratch[...])
+    total = dot(jnp.concatenate([high, low], axis=1), jnp.concatenate([same, same], axis=0))
+    scratch[...] = own_rows(total)
     write_lanes(out_ref, gathered_rows(scratch) * depth_factor(), 2 * KX)
+
+
+def own_rows(values):
+    keep = iota(values.shape, 0) % 4 == iota(values.shape, 1) // C
+    return jnp.where(keep, values, 0.0)
 
 
 def point_kernel(field_ref, mixing_ref, bias_ref, out_ref):
@@ -536,7 +564,8 @@
     slope = (0.5 + 0.5 * bent) * (1.0 + (1.0 - bent) * tail)
     adjoint = (cotangent_ref[...].astype(F32) * slope).astype(BF)
     adjoint_ref[...] = adjoint
-    z_spectrum(y_spectrum(adjoint, table_ref[...], rows_x, rows_y), depth_ref, out_refs, rows_x)
+    modes = y_spectrum(adjoint, table_ref[...], rows_x, rows_y).astype(BF)
+    z_spectrum(dot(modes, depth_ref[...]), out_refs, rows_x)
 
 
 def sums_kernel(field_ref, adjoint_ref, mixing_ref, out_ref, sums_ref):
@@ -561,38 +590,13 @@
     sums_ref[8:, :] = folded(dot(jnp.ones((8, adjoint.shape[0]), BF), adjoint))
 
 
-def swapped(values, index, distance):
-    return lane_take(values, index ^ distance)
-
-
-def adjoint_kernel(steps, weight_ref, *refs):
-    in_refs, (out_ref, spec_ref, sums_ref, scratch) = refs[:steps], refs[steps:]
+def adjoint_kernel(steps, weight_ref, spread_ref, *refs):
+    in_refs, (out_ref, spec_ref, sums_ref, scratch, wide) = refs[:steps], refs[steps:]
     spec_ref[...] = summed_modes(in_refs) * depth_factor()
     sums_ref[...] = functools.reduce(jnp.add, [ref[CHUNKS * 2 * KX :, :] for ref in in_refs])
-    keep = own_group()
-    lane = iota((KZ, LANES), 1)
-    final = lane % C % 4 * C + lane % C // 4 * 4
-
-    def reduced(parts):
-        distance = 16
-        while len(parts) > 1:
-            bit = (lane & distance) != 0
-            half = len(parts) // 2
-            merged = []
-            for low, high in zip(parts[:half], parts[half:]):
-                kept = jnp.where(bit, high, low)
-                other = jnp.where(bit, low, high)
-                merged.append(kept + swapped(other, lane, distance))
-            parts = merged
-            distance //= 2
-        total = parts[0]
-        while distance:
-            total = total + swapped(total, lane, distance)
-            distance //= 2
-        return lane_take(total, final)
+    index = out_index()
 
     def step(mode, carry):
-        index = out_index()
         real = lane_take(mode_row(spec_ref, 2 * mode), index)
         imag = lane_take(mode_row(spec_ref, 2 * mode + 1), index)
         real_w, imag_w = weight_parts(weight_ref, mode)
@@ -601,12 +605,19 @@
             real_p, imag_p = lanes_of(real_w, part), lanes_of(imag_w, part)
             real_parts.append(real * real_p + imag * imag_p)
             imag_parts.append(imag * real_p - real * imag_p)
-        for part, parts in ((0, real_parts), (1, imag_parts)):
-            start = pl.multiple_of((2 * mode + part) * KZ, KZ)
-            scratch[pl.ds(start, KZ), :] = jnp.where(keep, reduced(parts), 0.0)
+        both = jnp.concatenate(
+            [jnp.concatenate(real_parts, axis=1), jnp.concatenate(imag_parts, axis=1)], axis=0
+        )
+        high, low = halves(both)
+        start = pl.multiple_of(2 * mode * KZ, 2 * KZ)
+        wide[0, pl.ds(start, 2 * KZ), :] = high
+        wide[1, pl.ds(start, 2 * KZ), :] = low
         return carry
 
     lax.fori_loop(0, KX, step, 0, unroll=4)
+    total = dot(wide[0], spread_ref[...], ((1,), (1,)))
+    total = total + dot(wide[1], spread_ref[...], ((1,), (1,)))
+    scratch[...] = own_rows(total)
     write_lanes(out_ref, gathered_rows(scratch), 2 * KX)
 
 
@@ -651,21 +662,15 @@
         piece = packed if part == 0 else pltpu.roll(packed, LANES - part * C, 1)
         point_ref[part * 8 : (part + 1) * 8, :] = piece[:, :C]
     bias_ref[...] = total[8:9, :C]
-    planes = z_synthesis(in_refs, depth_ref, rows_x)
+    planes = z_synthesis(in_refs, depth_ref, rows_x, exact=False)
     stores = []
-    parts = gates.shape[0]
     for x in range(rows_x):
         block = slice(x * rows_y, (x + 1) * rows_y)
         spectral = y_synthesis(planes, back_ref[...], x, rows_x)
         result[block, :] = (mixed_ref[block, :] + spectral).astype(BF)
-        if (x + 1) % (rows_x // parts) == 0:
-            part = (x + 1) // (rows_x // parts) - 1
-            rows = result.shape[0] // parts
-            span = pl.ds(part * rows, rows)
-            stores.append(
-                pltpu.make_async_copy(result.at[span], out_ref.at[span], gates.at[part])
-            )
-            stores[-1].start()
+        span = pl.ds(x * rows_y, rows_y)
+        stores.append(pltpu.make_async_copy(result.at[span], out_ref.at[span], gates.at[x]))
+        stores[-1].start()
     for store in stores:
         store.wait()
 
@@ -714,6 +719,7 @@
     scale = 1.0 / math.sqrt(full_x * full_y * NZ)
     cells = rows_x * rows_y
     z_rows = jnp.asarray(depth_rows())
+    spread_hits = jnp.asarray(spread_table())
     forward_y, inverse_y = map(jnp.asarray, y_tables(full_y, rows_y, x_parts, y_parts))
     forward_x, inverse_x = map(jnp.asarray, x_tables(full_x, rows_x, scale, y_parts))
     field = field_input.reshape(cells, depth)
@@ -746,27 +752,27 @@
         )(to_cells, *received, *extra)
         return exchange(sent, "gx")
 
-    *blocks, depth_table, mixing, table, back, to_modes, to_cells = call(
+    *blocks, depth_table, mixing, table, back, to_modes, to_cells, spread = call(
         functools.partial(first_kernel, rows_x, rows_y),
-        [False] * 7,
+        [False] * 8,
         [cell_block] * x_parts
         + [((depth, 2 * WIDE), BF, True), ((8 * C, 8 * C), BF, True)]
         + [(part.shape[1:], BF, True) for part in (forward_y, inverse_y)]
-        + [(part.shape, BF, True) for part in (forward_x, inverse_x)],
+        + [(part.shape, BF, True) for part in (forward_x, inverse_x, spread_hits)],
         [
             pltpu.VMEM((cells, depth), BF),
             pltpu.VMEM(z_rows.shape, F32),
             pltpu.VMEM((C, C), BF),
-            pltpu.SemaphoreType.DMA((8,)),
+            pltpu.SemaphoreType.DMA((9,)),
         ],
-    )(field, forward_y, z_rows, point_weight, inverse_y, forward_x, inverse_x)
+    )(field, forward_y, z_rows, point_weight, inverse_y, forward_x, inverse_x, spread_hits)
     (base,) = call(point_kernel, [True] * 3, [cell_shape])(field, mixing, bias)
     block, field_modes = call(
         functools.partial(product_kernel, y_parts),
-        [True] * (1 + y_parts),
+        [True] * (2 + y_parts),
         [mode_block, spectrum_shape],
-        [rows_scratch],
-    )(spectral_weight, *forward(blocks, [], mode_block))
+        [rows_scratch, pltpu.VMEM((2 * KX * KZ, C * C), F32)],
+    )(spectral_weight, spread, *forward(blocks, [], mode_block))
     *blocks, adjoint = call(
         functools.partial(middle_kernel, rows_x, rows_y, x_parts),
         [True] * (5 + x_parts),
@@ -785,10 +791,10 @@
     )
     block, adjoint_modes, sums = call(
         functools.partial(adjoint_kernel, y_parts),
-        [True] * (1 + y_parts),
+        [True] * (2 + y_parts),
         [mode_block, spectrum_shape, sums_shape],
-        [rows_scratch],
-    )(spectral_weight, *forward(blocks, [sums], mode_sums))
+        [rows_scratch, pltpu.VMEM((2, 2 * KX * KZ, C * C), BF)],
+    )(spectral_weight, spread, *forward(blocks, [sums], mode_sums))
     (grad_spectral,) = call(
         functools.partial(weight_kernel, scale),
         [True] * 2,
@@ -799,7 +805,7 @@
         functools.partial(last_kernel, rows_x, rows_y, x_parts, scale),
         [True] * (3 + x_parts),
         [((cells, depth), BF, False), ((C, C), F32, None), ((1, C), F32, None)],
-        [pltpu.VMEM((cells, depth), BF), pltpu.SemaphoreType.DMA((4,))],
+        [pltpu.VMEM((cells, depth), BF), pltpu.SemaphoreType.DMA((rows_x,))],
     )(mixed_adjoint, back, depth_table, *inverse(block, [sums], cell_sums))
     return (
         grad_field.reshape(field_input.shape),

time: 89.5 us -> 86.3 us (0.964)
  Pallas kernels: 21.2 us -> 18 us
    pallas_call x12, Pallas kernels: 21.2 us -> 18 us  [run(): return function(*map(pltpu.with_memory_space_constraint, arguments, spaces))]
where the time goes in v3:
time: 86.3 us; the launch traced here: 86.1 us
  waiting for transfers between devices  40.6 us (47%)
  starting transfers between devices  26.8 us (31%)
  Pallas kernels  18 us (21%)
    ppermute x24, waiting for transfers between devices, exchange(): received[turn] = lax.ppermute(blocks[turn], axis, pairs)  40.6 us
    ppermute x24, starting transfers between devices, exchange(): received[turn] = lax.ppermute(blocks[turn], axis, pairs)  26.8 us
    pallas_call x12, Pallas kernels, run(): return function(*map(pltpu.with_memory_space_constraint, arguments, spaces))  18 us
  transfers between devices with their start and end apart: 24, of which 16 were waited for; matrix products, arithmetic and copies ran while one was open for 0% of the time, Pallas kernels for 5%

profile of v3, /device:TPU:0, one launch (start us, length us, event | category | flops | bytes accessed | tf_op | source)
XLA Modules:
  0.0 86.1 jit_solution(16207203171794841560)
XLA Ops:
  0.7 3.4 %shard_map.138 = (f32[256,128]{1,0:T(8,128)S(1)}, f32[256,128]{1,0:T(8,128)S(1)}, f32[256,128]{1,0:T(8,128)S(1)}, f32[256,128]{1,0:T(8,128)S(1)}, bf16[1024,1024...) custom-call(bf16[512,1024]{1,0:T(8,128)(2,1)} %bitcast.5, ...), custom_call_target="tpu_custom_call" | custom-call | tf_op jit(solution)/shard_map/pallas_call | solution.py:700
  4.6 2.6 %collective-permute-start.1 = (f32[256,128]{1,0:T(8,128)S(1)}, f32[256,128]{1,0:T(8,128)S(1)}, u32[]{:S(2)}, u32[]{:S(2)}) collective-permute-start(f32[256,128]{1,0:T(8,128)S(1)} %get-tuple-element.55), channel_id=1, source_target_pairs={{0,8},{4,12},{8,0},{12,4},{1,9},{5,13},{9,1},{13,5},{2,10},{6,14},... | collective-permute-start | bytes 393224 | tf_op jit(solution)/shard_map/ppermute | solution.py:711
  7.2 4.3 %collective-permute-done.1.refs_2_ = f32[256,128]{1,0:T(8,128)S(1)} collective-permute-done((f32[256,128]{1,0:T(8,128)S(1)}, f32[256,128]{1,0:T(8,128)S(1)}, u32[]{:S(2)}, u32[]{:S(2)}) %collective-permute-start.1) | collective-permute-done | bytes 131104 | tf_op jit(solution)/shard_map/ppermute | solution.py:711
  11.5 2.3 %collective-permute-done.2.refs_3_ = f32[256,128]{1,0:T(8,128)S(1)} collective-permute-done((f32[256,128]{1,0:T(8,128)S(1)}, f32[256,128]{1,0:T(8,128)S(1)}, u32[]{:S(2)}, u32[]{:S(2)}) %collective-permute-start.2) | collective-permute-done | bytes 131104 | tf_op jit(solution)/shard_map/ppermute | solution.py:711
  14.1 1.7 %collective-permute-start.3 = (f32[128,128]{1,0:T(8,128)S(1)}, f32[128,128]{1,0:T(8,128)S(1)}, u32[]{:S(2)}, u32[]{:S(2)}) collective-permute-start(f32[128,128]{1,0:T(8,128)S(1)} %get-tuple-element.58), channel_id=1, source_target_pairs={{0,1},{1,0},{2,3},{3,2},{4,5},{5,4},{6,7},{7,6},{8,9},{9,8},{10,11... | collective-permute-start | bytes 196616 | tf_op jit(solution)/shard_map/ppermute | solution.py:711
  15.8 2.6 %collective-permute-start.4 = (f32[128,128]{1,0:T(8,128)S(1)}, f32[128,128]{1,0:T(8,128)S(1)}, u32[]{:S(2)}, u32[]{:S(2)}) collective-permute-start(f32[128,128]{1,0:T(8,128)S(1)} %get-tuple-element.59), channel_id=1, source_target_pairs={{0,2},{1,3},{2,0},{3,1},{4,6},{5,7},{6,4},{7,5},{8,10},{9,11},{10,... | collective-permute-start | bytes 196616 | tf_op jit(solution)/shard_map/ppermute | solution.py:711
  18.5 4.8 %collective-permute-done.4.refs_2_ = f32[128,128]{1,0:T(8,128)S(1)} collective-permute-done((f32[128,128]{1,0:T(8,128)S(1)}, f32[128,128]{1,0:T(8,128)S(1)}, u32[]{:S(2)}, u32[]{:S(2)}) %collective-permute-start.4) | collective-permute-done | bytes 65568 | tf_op jit(solution)/shard_map/ppermute | solution.py:711
  25.8 2.2 %collective-permute-start.8 = (f32[128,128]{1,0:T(8,128)S(1)}, f32[128,128]{1,0:T(8,128)S(1)}, u32[]{:S(2)}, u32[]{:S(2)}) collective-permute-start(f32[128,128]{1,0:T(8,128)S(1)} %get-tuple-element.61.refs_0_), channel_id=1, source_target_pairs={{0,3},{1,2},{2,1},{3,0},{4,7},{5,6},{6,5},{7,4},{8,11},{9,10},{10,... | collective-permute-start | bytes 196616 | tf_op jit(solution)/shard_map/ppermute | solution.py:711
  28.3 1.9 %collective-permute-start.6 = (f32[128,128]{1,0:T(8,128)S(1)}, f32[128,128]{1,0:T(8,128)S(1)}, u32[]{:S(2)}, u32[]{:S(2)}) collective-permute-start(f32[128,128]{1,0:T(8,128)S(1)} %get-tuple-element.61.refs_0_), channel_id=1, source_target_pairs={{0,1},{1,0},{2,3},{3,2},{4,5},{5,4},{6,7},{7,6},{8,9},{9,8},{10,11... | collective-permute-start | bytes 196616 | tf_op jit(solution)/shard_map/ppermute | solution.py:711
  30.2 1.8 %collective-permute-done.8.refs_3_ = f32[128,128]{1,0:T(8,128)S(1)} collective-permute-done((f32[128,128]{1,0:T(8,128)S(1)}, f32[128,128]{1,0:T(8,128)S(1)}, u32[]{:S(2)}, u32[]{:S(2)}) %collective-permute-start.8) | collective-permute-done | bytes 65568 | tf_op jit(solution)/shard_map/ppermute | solution.py:711
  32.0 1.7 %collective-permute-done.7.refs_2_ = f32[128,128]{1,0:T(8,128)S(1)} collective-permute-done((f32[128,128]{1,0:T(8,128)S(1)}, f32[128,128]{1,0:T(8,128)S(1)}, u32[]{:S(2)}, u32[]{:S(2)}) %collective-permute-start.7) | collective-permute-done | bytes 65568 | tf_op jit(solution)/shard_map/ppermute | solution.py:711
  36.5 4.0 %collective-permute-done.10.refs_2_ = f32[256,128]{1,0:T(8,128)S(1)} collective-permute-done((f32[256,128]{1,0:T(8,128)S(1)}, f32[256,128]{1,0:T(8,128)S(1)}, u32[]{:S(2)}, u32[]{:S(2)}) %collective-permute-start.10) | collective-permute-done | bytes 131104 | tf_op jit(solution)/shard_map/ppermute | solution.py:711
  40.5 1.9 %collective-permute-done.11.refs_3_ = f32[256,128]{1,0:T(8,128)S(1)} collective-permute-done((f32[256,128]{1,0:T(8,128)S(1)}, f32[256,128]{1,0:T(8,128)S(1)}, u32[]{:S(2)}, u32[]{:S(2)}) %collective-permute-start.11) | collective-permute-done | bytes 131104 | tf_op jit(solution)/shard_map/ppermute | solution.py:711
  42.4 3.6 %shard_map.143 = (f32[256,128]{1,0:T(8,128)S(1)}, f32[256,128]{1,0:T(8,128)S(1)}, f32[256,128]{1,0:T(8,128)S(1)}, f32[256,128]{1,0:T(8,128)S(1)}, bf16[512,1024]{1,0:T(8,128)(2,1)S(1)}) custom-call(f32[512,1024]{1,0:T(8,128)S(1)} %shard_map.139.base_ref, bf16[512,1024]{1,0:T(8,128)(2,1)S(1)} %bitcast.8, bf16[64,64]{1,0:T(8,128)(2,1)S(1)} %get-tuple-element.47.table_ref, ...), custom_call_target="tpu_custom_call" | custom-call | tf_op jit(solution)/shard_map/pallas_call | solution.py:700
  49.0 3.7 %collective-permute-done.13.refs_2_ = f32[256,128]{1,0:T(8,128)S(1)} collective-permute-done((f32[256,128]{1,0:T(8,128)S(1)}, f32[256,128]{1,0:T(8,128)S(1)}, u32[]{:S(2)}, u32[]{:S(2)}) %collective-permute-start.13) | collective-permute-done | bytes 131104 | tf_op jit(solution)/shard_map/ppermute | solution.py:711
  55.3 1.8 %collective-permute-start.16 = (f32[144,128]{1,0:T(8,128)S(1)}, f32[144,128]{1,0:T(8,128)S(1)}, u32[]{:S(2)}, u32[]{:S(2)}) collective-permute-start(f32[144,128]{1,0:T(8,128)S(1)} %get-tuple-element.75), channel_id=1, source_target_pairs={{0,2},{1,3},{2,0},{3,1},{4,6},{5,7},{6,4},{7,5},{8,10},{9,11},{10,... | collective-permute-start | bytes 221192 | tf_op jit(solution)/shard_map/ppermute | solution.py:711
  57.1 1.8 %collective-permute-start.17 = (f32[144,128]{1,0:T(8,128)S(1)}, f32[144,128]{1,0:T(8,128)S(1)}, u32[]{:S(2)}, u32[]{:S(2)}) collective-permute-start(f32[144,128]{1,0:T(8,128)S(1)} %get-tuple-element.76), channel_id=1, source_target_pairs={{0,3},{1,2},{2,1},{3,0},{4,7},{5,6},{6,5},{7,4},{8,11},{9,10},{10,... | collective-permute-start | bytes 221192 | tf_op jit(solution)/shard_map/ppermute | solution.py:711
  60.0 4.4 %collective-permute-done.16.refs_2_ = f32[144,128]{1,0:T(8,128)S(1)} collective-permute-done((f32[144,128]{1,0:T(8,128)S(1)}, f32[144,128]{1,0:T(8,128)S(1)}, u32[]{:S(2)}, u32[]{:S(2)}) %collective-permute-start.16) | collective-permute-done | bytes 73760 | tf_op jit(solution)/shard_map/ppermute | solution.py:711
  66.1 2.1 %collective-permute-start.20 = (f32[128,128]{1,0:T(8,128)S(1)}, f32[128,128]{1,0:T(8,128)S(1)}, u32[]{:S(2)}, u32[]{:S(2)}) collective-permute-start(f32[128,128]{1,0:T(8,128)S(1)} %get-tuple-element.77.refs_0_), channel_id=1, source_target_pairs={{0,3},{1,2},{2,1},{3,0},{4,7},{5,6},{6,5},{7,4},{8,11},{9,10},{10,... | collective-permute-start | bytes 196616 | tf_op jit(solution)/shard_map/ppermute | solution.py:711
  70.5 2.3 %collective-permute-done.20.refs_3_ = f32[128,128]{1,0:T(8,128)S(1)} collective-permute-done((f32[128,128]{1,0:T(8,128)S(1)}, f32[128,128]{1,0:T(8,128)S(1)}, u32[]{:S(2)}, u32[]{:S(2)}) %collective-permute-start.20) | collective-permute-done | bytes 65568 | tf_op jit(solution)/shard_map/ppermute | solution.py:711
  76.8 2.8 %shard_map.149 = f32[16,32768]{1,0:T(8,128)} custom-call(f32[32,512]{1,0:T(8,128)S(1)} %get-tuple-element.84.field_ref, f32[32,512]{1,0:T(8,128)S(1)} %get-tuple-element.85.adjoint_ref), custom_call_target="tpu_custom_call" | custom-call | tf_op jit(solution)/shard_map/pallas_call | solution.py:700
  79.6 1.8 %collective-permute-done.22.refs_2_ = f32[272,128]{1,0:T(8,128)S(1)} collective-permute-done((f32[272,128]{1,0:T(8,128)S(1)}, f32[272,128]{1,0:T(8,128)S(1)}, u32[]{:S(2)}, u32[]{:S(2)}) %collective-permute-start.22) | collective-permute-done | bytes 139296 | tf_op jit(solution)/shard_map/ppermute | solution.py:711
  81.5 2.1 %collective-permute-done.23.refs_3_ = f32[272,128]{1,0:T(8,128)S(1)} collective-permute-done((f32[272,128]{1,0:T(8,128)S(1)}, f32[272,128]{1,0:T(8,128)S(1)}, u32[]{:S(2)}, u32[]{:S(2)}) %collective-permute-start.23) | collective-permute-done | bytes 139296 | tf_op jit(solution)/shard_map/ppermute | solution.py:711
  83.6 2.5 %shard_map.148 = (bf16[512,1024]{1,0:T(8,128)(2,1)}, f32[32,32]{1,0:T(8,128)}, f32[1,32]{1,0:T(1,128)}) custom-call(f32[512,1024]{1,0:T(8,128)S(1)} %get-tuple-element.67.mixed_ref, bf16[64,96]{1,0:T(8,128)(2,1)S(1)} %get-tuple-element.48.back_ref, bf16[1024,1024]{1,0:T(8,128)(2,1)S(1)} %get-tuple-element.49.depth_ref, ...), custom_call_target="tpu_custom_call" | custom-call | tf_op jit(solution)/shard_map/pallas_call | solution.py:700
  (44 shorter events, 21.1 us)
Async XLA Ops:
  4.0 3.2 %collective-permute-start = (f32[256,128]{1,0:T(8,128)S(1)}, f32[256,128]{1,0:T(8,128)S(1)}, u32[]{:S(2)}, u32[]{:S(2)}) collective-permute-start(f32[256,128]{1,0:T(8,128)S(1)} %get-tuple-element.54), channel_id=1, source_target_pairs={{0,4},{4,0},{8,12},{12,8},{1,5},{5,1},{9,13},{13,9},{2,6},{6,2},{1... | collective-permute-start | bytes 393224 | tf_op jit(solution)/shard_map/ppermute | solution.py:711
  4.6 6.9 %collective-permute-start.1 = (f32[256,128]{1,0:T(8,128)S(1)}, f32[256,128]{1,0:T(8,128)S(1)}, u32[]{:S(2)}, u32[]{:S(2)}) collective-permute-start(f32[256,128]{1,0:T(8,128)S(1)} %get-tuple-element.55), channel_id=1, source_target_pairs={{0,8},{4,12},{8,0},{12,4},{1,9},{5,13},{9,1},{13,5},{2,10},{6,14},... | collective-permute-start | bytes 393224 | tf_op jit(solution)/shard_map/ppermute | solution.py:711
  7.1 6.6 %collective-permute-start.2 = (f32[256,128]{1,0:T(8,128)S(1)}, f32[256,128]{1,0:T(8,128)S(1)}, u32[]{:S(2)}, u32[]{:S(2)}) collective-permute-start(f32[256,128]{1,0:T(8,128)S(1)} %get-tuple-element.56), channel_id=1, source_target_pairs={{0,12},{4,8},{8,4},{12,0},{1,13},{5,9},{9,5},{13,1},{2,14},{6,10},... | collective-permute-start | bytes 393224 | tf_op jit(solution)/shard_map/ppermute | solution.py:711
  14.1 4.5 %collective-permute-start.3 = (f32[128,128]{1,0:T(8,128)S(1)}, f32[128,128]{1,0:T(8,128)S(1)}, u32[]{:S(2)}, u32[]{:S(2)}) collective-permute-start(f32[128,128]{1,0:T(8,128)S(1)} %get-tuple-element.58), channel_id=1, source_target_pairs={{0,1},{1,0},{2,3},{3,2},{4,5},{5,4},{6,7},{7,6},{8,9},{9,8},{10,11... | collective-permute-start | bytes 196616 | tf_op jit(solution)/shard_map/ppermute | solution.py:711
  15.8 7.6 %collective-permute-start.4 = (f32[128,128]{1,0:T(8,128)S(1)}, f32[128,128]{1,0:T(8,128)S(1)}, u32[]{:S(2)}, u32[]{:S(2)}) collective-permute-start(f32[128,128]{1,0:T(8,128)S(1)} %get-tuple-element.59), channel_id=1, source_target_pairs={{0,2},{1,3},{2,0},{3,1},{4,6},{5,7},{6,4},{7,5},{8,10},{9,11},{10,... | collective-permute-start | bytes 196616 | tf_op jit(solution)/shard_map/ppermute | solution.py:711
  18.4 6.2 %collective-permute-start.5 = (f32[128,128]{1,0:T(8,128)S(1)}, f32[128,128]{1,0:T(8,128)S(1)}, u32[]{:S(2)}, u32[]{:S(2)}) collective-permute-start(f32[128,128]{1,0:T(8,128)S(1)} %get-tuple-element.60), channel_id=1, source_target_pairs={{0,3},{1,2},{2,1},{3,0},{4,7},{5,6},{6,5},{7,4},{8,11},{9,10},{10,... | collective-permute-start | bytes 196616 | tf_op jit(solution)/shard_map/ppermute | solution.py:711
  25.8 6.3 %collective-permute-start.8 = (f32[128,128]{1,0:T(8,128)S(1)}, f32[128,128]{1,0:T(8,128)S(1)}, u32[]{:S(2)}, u32[]{:S(2)}) collective-permute-start(f32[128,128]{1,0:T(8,128)S(1)} %get-tuple-element.61.refs_0_), channel_id=1, source_target_pairs={{0,3},{1,2},{2,1},{3,0},{4,7},{5,6},{6,5},{7,4},{8,11},{9,10},{10,... | collective-permute-start | bytes 196616 | tf_op jit(solution)/shard_map/ppermute | solution.py:711
  27.9 5.8 %collective-permute-start.7 = (f32[128,128]{1,0:T(8,128)S(1)}, f32[128,128]{1,0:T(8,128)S(1)}, u32[]{:S(2)}, u32[]{:S(2)}) collective-permute-start(f32[128,128]{1,0:T(8,128)S(1)} %get-tuple-element.61.refs_0_), channel_id=1, source_target_pairs={{0,2},{1,3},{2,0},{3,1},{4,6},{5,7},{6,4},{7,5},{8,10},{9,11},{10,... | collective-permute-start | bytes 196616 | tf_op jit(solution)/shard_map/ppermute | solution.py:711
  28.3 5.4 %collective-permute-start.6 = (f32[128,128]{1,0:T(8,128)S(1)}, f32[128,128]{1,0:T(8,128)S(1)}, u32[]{:S(2)}, u32[]{:S(2)}) collective-permute-start(f32[128,128]{1,0:T(8,128)S(1)} %get-tuple-element.61.refs_0_), channel_id=1, source_target_pairs={{0,1},{1,0},{2,3},{3,2},{4,5},{5,4},{6,7},{7,6},{8,9},{9,8},{10,11... | collective-permute-start | bytes 196616 | tf_op jit(solution)/shard_map/ppermute | solution.py:711
  34.1 2.4 %collective-permute-start.9 = (f32[256,128]{1,0:T(8,128)S(1)}, f32[256,128]{1,0:T(8,128)S(1)}, u32[]{:S(2)}, u32[]{:S(2)}) collective-permute-start(f32[256,128]{1,0:T(8,128)S(1)} %get-tuple-element.63), channel_id=1, source_target_pairs={{0,4},{4,0},{8,12},{12,8},{1,5},{5,1},{9,13},{13,9},{2,6},{6,2},{1... | collective-permute-start | bytes 393224 | tf_op jit(solution)/shard_map/ppermute | solution.py:711
  34.2 6.4 %collective-permute-start.10 = (f32[256,128]{1,0:T(8,128)S(1)}, f32[256,128]{1,0:T(8,128)S(1)}, u32[]{:S(2)}, u32[]{:S(2)}) collective-permute-start(f32[256,128]{1,0:T(8,128)S(1)} %get-tuple-element.64), channel_id=1, source_target_pairs={{0,8},{4,12},{8,0},{12,4},{1,9},{5,13},{9,1},{13,5},{2,10},{6,14},... | collective-permute-start | bytes 393224 | tf_op jit(solution)/shard_map/ppermute | solution.py:711
  35.8 6.7 %collective-permute-start.11 = (f32[256,128]{1,0:T(8,128)S(1)}, f32[256,128]{1,0:T(8,128)S(1)}, u32[]{:S(2)}, u32[]{:S(2)}) collective-permute-start(f32[256,128]{1,0:T(8,128)S(1)} %get-tuple-element.65), channel_id=1, source_target_pairs={{0,12},{4,8},{8,4},{12,0},{1,13},{5,9},{9,5},{13,1},{2,14},{6,10},... | collective-permute-start | bytes 393224 | tf_op jit(solution)/shard_map/ppermute | solution.py:711
  46.0 3.0 %collective-permute-start.12 = (f32[256,128]{1,0:T(8,128)S(1)}, f32[256,128]{1,0:T(8,128)S(1)}, u32[]{:S(2)}, u32[]{:S(2)}) collective-permute-start(f32[256,128]{1,0:T(8,128)S(1)} %get-tuple-element.69), channel_id=1, source_target_pairs={{0,4},{4,0},{8,12},{12,8},{1,5},{5,1},{9,13},{13,9},{2,6},{6,2},{1... | collective-permute-start | bytes 393224 | tf_op jit(solution)/shard_map/ppermute | solution.py:711
  46.4 6.3 %collective-permute-start.13 = (f32[256,128]{1,0:T(8,128)S(1)}, f32[256,128]{1,0:T(8,128)S(1)}, u32[]{:S(2)}, u32[]{:S(2)}) collective-permute-start(f32[256,128]{1,0:T(8,128)S(1)} %get-tuple-element.70), channel_id=1, source_target_pairs={{0,8},{4,12},{8,0},{12,4},{1,9},{5,13},{9,1},{13,5},{2,10},{6,14},... | collective-permute-start | bytes 393224 | tf_op jit(solution)/shard_map/ppermute | solution.py:711
  47.9 6.2 %collective-permute-start.14 = (f32[256,128]{1,0:T(8,128)S(1)}, f32[256,128]{1,0:T(8,128)S(1)}, u32[]{:S(2)}, u32[]{:S(2)}) collective-permute-start(f32[256,128]{1,0:T(8,128)S(1)} %get-tuple-element.71), channel_id=1, source_target_pairs={{0,12},{4,8},{8,4},{12,0},{1,13},{5,9},{9,5},{13,1},{2,14},{6,10},... | collective-permute-start | bytes 393224 | tf_op jit(solution)/shard_map/ppermute | solution.py:711
  54.4 5.6 %collective-permute-start.15 = (f32[144,128]{1,0:T(8,128)S(1)}, f32[144,128]{1,0:T(8,128)S(1)}, u32[]{:S(2)}, u32[]{:S(2)}) collective-permute-start(f32[144,128]{1,0:T(8,128)S(1)} %get-tuple-element.74), channel_id=1, source_target_pairs={{0,1},{1,0},{2,3},{3,2},{4,5},{5,4},{6,7},{7,6},{8,9},{9,8},{10,11... | collective-permute-start | bytes 221192 | tf_op jit(solution)/shard_map/ppermute | solution.py:711
  55.3 9.1 %collective-permute-start.16 = (f32[144,128]{1,0:T(8,128)S(1)}, f32[144,128]{1,0:T(8,128)S(1)}, u32[]{:S(2)}, u32[]{:S(2)}) collective-permute-start(f32[144,128]{1,0:T(8,128)S(1)} %get-tuple-element.75), channel_id=1, source_target_pairs={{0,2},{1,3},{2,0},{3,1},{4,6},{5,7},{6,4},{7,5},{8,10},{9,11},{10,... | collective-permute-start | bytes 221192 | tf_op jit(solution)/shard_map/ppermute | solution.py:711
  57.1 7.4 %collective-permute-start.17 = (f32[144,128]{1,0:T(8,128)S(1)}, f32[144,128]{1,0:T(8,128)S(1)}, u32[]{:S(2)}, u32[]{:S(2)}) collective-permute-start(f32[144,128]{1,0:T(8,128)S(1)} %get-tuple-element.76), channel_id=1, source_target_pairs={{0,3},{1,2},{2,1},{3,0},{4,7},{5,6},{6,5},{7,4},{8,11},{9,10},{10,... | collective-permute-start | bytes 221192 | tf_op jit(solution)/shard_map/ppermute | solution.py:711
  66.1 6.8 %collective-permute-start.20 = (f32[128,128]{1,0:T(8,128)S(1)}, f32[128,128]{1,0:T(8,128)S(1)}, u32[]{:S(2)}, u32[]{:S(2)}) collective-permute-start(f32[128,128]{1,0:T(8,128)S(1)} %get-tuple-element.77.refs_0_), channel_id=1, source_target_pairs={{0,3},{1,2},{2,1},{3,0},{4,7},{5,6},{6,5},{7,4},{8,11},{9,10},{10,... | collective-permute-start | bytes 196616 | tf_op jit(solution)/shard_map/ppermute | solution.py:711
  68.2 6.3 %collective-permute-start.19 = (f32[128,128]{1,0:T(8,128)S(1)}, f32[128,128]{1,0:T(8,128)S(1)}, u32[]{:S(2)}, u32[]{:S(2)}) collective-permute-start(f32[128,128]{1,0:T(8,128)S(1)} %get-tuple-element.77.refs_0_), channel_id=1, source_target_pairs={{0,2},{1,3},{2,0},{3,1},{4,6},{5,7},{6,4},{7,5},{8,10},{9,11},{10,... | collective-permute-start | bytes 196616 | tf_op jit(solution)/shard_map/ppermute | solution.py:711
  69.0 5.4 %collective-permute-start.18 = (f32[128,128]{1,0:T(8,128)S(1)}, f32[128,128]{1,0:T(8,128)S(1)}, u32[]{:S(2)}, u32[]{:S(2)}) collective-permute-start(f32[128,128]{1,0:T(8,128)S(1)} %get-tuple-element.77.refs_0_), channel_id=1, source_target_pairs={{0,1},{1,0},{2,3},{3,2},{4,5},{5,4},{6,7},{7,6},{8,9},{9,8},{10,11... | collective-permute-start | bytes 196616 | tf_op jit(solution)/shard_map/ppermute | solution.py:711
  74.9 4.8 %collective-permute-start.21 = (f32[272,128]{1,0:T(8,128)S(1)}, f32[272,128]{1,0:T(8,128)S(1)}, u32[]{:S(2)}, u32[]{:S(2)}) collective-permute-start(f32[272,128]{1,0:T(8,128)S(1)} %get-tuple-element.80), channel_id=1, source_target_pairs={{0,4},{4,0},{8,12},{12,8},{1,5},{5,1},{9,13},{13,9},{2,6},{6,2},{1... | collective-permute-start | bytes 417800 | tf_op jit(solution)/shard_map/ppermute | solution.py:711
  75.0 6.5 %collective-permute-start.22 = (f32[272,128]{1,0:T(8,128)S(1)}, f32[272,128]{1,0:T(8,128)S(1)}, u32[]{:S(2)}, u32[]{:S(2)}) collective-permute-start(f32[272,128]{1,0:T(8,128)S(1)} %get-tuple-element.81), channel_id=1, source_target_pairs={{0,8},{4,12},{8,0},{12,4},{1,9},{5,13},{9,1},{13,5},{2,10},{6,14},... | collective-permute-start | bytes 417800 | tf_op jit(solution)/shard_map/ppermute | solution.py:711
  76.6 7.0 %collective-permute-start.23 = (f32[272,128]{1,0:T(8,128)S(1)}, f32[272,128]{1,0:T(8,128)S(1)}, u32[]{:S(2)}, u32[]{:S(2)}) collective-permute-start(f32[272,128]{1,0:T(8,128)S(1)} %get-tuple-element.82), channel_id=1, source_target_pairs={{0,12},{4,8},{8,4},{12,0},{1,13},{5,9},{9,5},{13,1},{2,14},{6,10},... | collective-permute-start | bytes 417800 | tf_op jit(solution)/shard_map/ppermute | solution.py:711
  (4 other events, 111.4 us)

commit v4 on v3

--- a/solution.py
+++ b/solution.py
@@ -461,7 +461,7 @@
 
 
 def x_forward_kernel(turns, table_ref, *refs):
-    in_refs, refs = refs[:turns], refs[turns:]
+    in_refs, refs = unqueued(refs[:turns], FORWARD_X), refs[turns:]
     rows = table_ref.shape[2] // 3
     own = lax.axis_index("gx")
     total = None
@@ -477,7 +477,7 @@
 
 
 def x_inverse_kernel(steps, turns, table_ref, *refs):
-    in_refs, refs = refs[:steps], refs[steps:]
+    in_refs, refs = unqueued(refs[:steps], INVERSE_Y), refs[steps:]
     values = tripled(jnp.concatenate([read_lanes(ref, 2 * KX) for ref in in_refs], axis=0))
     own = lax.axis_index("gx")
     rows = table_ref.shape[1]
@@ -485,6 +485,17 @@
         write_lanes(ref, dot(table_ref[own ^ turn], values), rows)
         if len(refs) > turns:
             ref[CHUNKS * rows :, :] = refs[0][...]
+
+
+FORWARD_X, FORWARD_Y, INVERSE_Y, INVERSE_X = ((2, 1, 3), (1, 2, 3), (1, 2, 3), (2, 3, 1))
+
+
+def queued(blocks, order):
+    return [blocks[0]] + [blocks[turn] for turn in order]
+
+
+def unqueued(refs, order):
+    return [refs[0]] + [refs[1 + order.index(turn)] for turn in range(1, len(refs))]
 
 
 def summed_modes(in_refs):
@@ -550,7 +561,8 @@
     depth_ref,
     *refs,
 ):
-    in_refs, out_refs, (adjoint_ref, value_ref) = refs[:turns], refs[turns:-2], refs[-2:]
+    in_refs = unqueued(refs[:turns], INVERSE_X)
+    out_refs, (adjoint_ref, value_ref) = refs[turns:-2], refs[-2:]
     planes = z_synthesis(in_refs, depth_ref, rows_x)
     for x in range(rows_x):
         block = slice(x * rows_y, (x + 1) * rows_y)
@@ -654,7 +666,8 @@
 
 
 def last_kernel(rows_x, rows_y, turns, scale, mixed_ref, back_ref, depth_ref, *refs):
-    in_refs, (out_ref, point_ref, bias_ref, result, gates) = refs[:turns], refs[turns:]
+    in_refs = unqueued(refs[:turns], INVERSE_X)
+    out_ref, point_ref, bias_ref, result, gates = refs[turns:]
     total = functools.reduce(jnp.add, [ref[ref.shape[0] - SUM_ROWS :, :] for ref in in_refs])
     total = total * scale
     packed = total[:8]
@@ -740,8 +753,8 @@
             functools.partial(x_forward_kernel, x_parts),
             [True] * (1 + x_parts + len(extra)),
             [mode_shape] * y_parts,
-        )(to_modes, *received, *extra)
-        return exchange(sent, "gy")
+        )(to_modes, *queued(received, FORWARD_X), *extra)
+        return queued(exchange(sent, "gy"), FORWARD_Y)
 
     def inverse(block, extra, cell_shape):
         received = exchange([block] * y_parts, "gy")
@@ -749,8 +762,8 @@
             functools.partial(x_inverse_kernel, y_parts, x_parts),
             [True] * (1 + y_parts + len(extra)),
             [cell_shape] * x_parts,
-        )(to_cells, *received, *extra)
-        return exchange(sent, "gx")
+        )(to_cells, *queued(received, INVERSE_Y), *extra)
+        return queued(exchange(sent, "gx"), INVERSE_X)
 
     *blocks, depth_table, mixing, table, back, to_modes, to_cells, spread = call(
         functools.partial(first_kernel, rows_x, rows_y),

time: 86.3 us -> 83.5 us (0.968)
  waiting for transfers between devices: 40.6 us -> 36.9 us
  starting transfers between devices: 26.8 us -> 27.7 us
    ppermute x24, waiting for transfers between devices: 40.6 us -> 36.9 us  [exchange(): received[turn] = lax.ppermute(blocks[turn], axis, pairs)]
    ppermute x24, starting transfers between devices: 26.8 us -> 27.7 us  [exchange(): received[turn] = lax.ppermute(blocks[turn], axis, pairs)]
where the time goes in v4:
time: 83.5 us; the launch traced here: 83.3 us
  waiting for transfers between devices  36.9 us (44%)
  starting transfers between devices  27.7 us (33%)
  Pallas kernels  18 us (22%)
    ppermute x24, waiting for transfers between devices, exchange(): received[turn] = lax.ppermute(blocks[turn], axis, pairs)  36.9 us
    ppermute x24, starting transfers between devices, exchange(): received[turn] = lax.ppermute(blocks[turn], axis, pairs)  27.7 us
    pallas_call x12, Pallas kernels, run(): return function(*map(pltpu.with_memory_space_constraint, arguments, spaces))  18 us
  transfers between devices with their start and end apart: 24, of which 16 were waited for; matrix products, arithmetic and copies ran while one was open for 0% of the time, Pallas kernels for 5%

profile of v4, /device:TPU:0, one launch (start us, length us, event | category | flops | bytes accessed | tf_op | source)
XLA Modules:
  0.0 83.3 jit_solution(6616334445275758085)
XLA Ops:
  0.7 3.4 %shard_map.138 = (f32[256,128]{1,0:T(8,128)S(1)}, f32[256,128]{1,0:T(8,128)S(1)}, f32[256,128]{1,0:T(8,128)S(1)}, f32[256,128]{1,0:T(8,128)S(1)}, bf16[1024,1024...) custom-call(bf16[512,1024]{1,0:T(8,128)(2,1)} %bitcast.5, ...), custom_call_target="tpu_custom_call" | custom-call | tf_op jit(solution)/shard_map/pallas_call | solution.py:713
  4.0 3.0 %collective-permute-start = (f32[256,128]{1,0:T(8,128)S(1)}, f32[256,128]{1,0:T(8,128)S(1)}, u32[]{:S(2)}, u32[]{:S(2)}) collective-permute-start(f32[256,128]{1,0:T(8,128)S(1)} %get-tuple-element.54), channel_id=1, source_target_pairs={{0,8},{4,12},{8,0},{12,4},{1,9},{5,13},{9,1},{13,5},{2,10},{6,14},... | collective-permute-start | bytes 393224 | tf_op jit(solution)/shard_map/ppermute | solution.py:724
  7.3 3.7 %collective-permute-done.refs_1_ = f32[256,128]{1,0:T(8,128)S(1)} collective-permute-done((f32[256,128]{1,0:T(8,128)S(1)}, f32[256,128]{1,0:T(8,128)S(1)}, u32[]{:S(2)}, u32[]{:S(2)}) %collective-permute-start) | collective-permute-done | bytes 131104 | tf_op jit(solution)/shard_map/ppermute | solution.py:724
  11.0 1.9 %collective-permute-done.2.refs_3_ = f32[256,128]{1,0:T(8,128)S(1)} collective-permute-done((f32[256,128]{1,0:T(8,128)S(1)}, f32[256,128]{1,0:T(8,128)S(1)}, u32[]{:S(2)}, u32[]{:S(2)}) %collective-permute-start.2) | collective-permute-done | bytes 131104 | tf_op jit(solution)/shard_map/ppermute | solution.py:724
  14.8 2.6 %collective-permute-start.4 = (f32[128,128]{1,0:T(8,128)S(1)}, f32[128,128]{1,0:T(8,128)S(1)}, u32[]{:S(2)}, u32[]{:S(2)}) collective-permute-start(f32[128,128]{1,0:T(8,128)S(1)} %get-tuple-element.59), channel_id=1, source_target_pairs={{0,2},{1,3},{2,0},{3,1},{4,6},{5,7},{6,4},{7,5},{8,10},{9,11},{10,... | collective-permute-start | bytes 196616 | tf_op jit(solution)/shard_map/ppermute | solution.py:724
  17.7 4.0 %collective-permute-done.4.refs_2_ = f32[128,128]{1,0:T(8,128)S(1)} collective-permute-done((f32[128,128]{1,0:T(8,128)S(1)}, f32[128,128]{1,0:T(8,128)S(1)}, u32[]{:S(2)}, u32[]{:S(2)}) %collective-permute-start.4) | collective-permute-done | bytes 65568 | tf_op jit(solution)/shard_map/ppermute | solution.py:724
  21.7 1.8 %collective-permute-done.5.refs_3_ = f32[128,128]{1,0:T(8,128)S(1)} collective-permute-done((f32[128,128]{1,0:T(8,128)S(1)}, f32[128,128]{1,0:T(8,128)S(1)}, u32[]{:S(2)}, u32[]{:S(2)}) %collective-permute-start.5) | collective-permute-done | bytes 65568 | tf_op jit(solution)/shard_map/ppermute | solution.py:724
  24.7 2.5 %collective-permute-start.8 = (f32[128,128]{1,0:T(8,128)S(1)}, f32[128,128]{1,0:T(8,128)S(1)}, u32[]{:S(2)}, u32[]{:S(2)}) collective-permute-start(f32[128,128]{1,0:T(8,128)S(1)} %get-tuple-element.61.refs_0_), channel_id=1, source_target_pairs={{0,3},{1,2},{2,1},{3,0},{4,7},{5,6},{6,5},{7,4},{8,11},{9,10},{10,... | collective-permute-start | bytes 196616 | tf_op jit(solution)/shard_map/ppermute | solution.py:724
  29.2 2.3 %collective-permute-done.8.refs_3_ = f32[128,128]{1,0:T(8,128)S(1)} collective-permute-done((f32[128,128]{1,0:T(8,128)S(1)}, f32[128,128]{1,0:T(8,128)S(1)}, u32[]{:S(2)}, u32[]{:S(2)}) %collective-permute-start.8) | collective-permute-done | bytes 65568 | tf_op jit(solution)/shard_map/ppermute | solution.py:724
  31.5 1.9 %collective-permute-done.7.refs_2_ = f32[128,128]{1,0:T(8,128)S(1)} collective-permute-done((f32[128,128]{1,0:T(8,128)S(1)}, f32[128,128]{1,0:T(8,128)S(1)}, u32[]{:S(2)}, u32[]{:S(2)}) %collective-permute-start.7) | collective-permute-done | bytes 65568 | tf_op jit(solution)/shard_map/ppermute | solution.py:724
  33.9 1.8 %collective-permute-start.9 = (f32[256,128]{1,0:T(8,128)S(1)}, f32[256,128]{1,0:T(8,128)S(1)}, u32[]{:S(2)}, u32[]{:S(2)}) collective-permute-start(f32[256,128]{1,0:T(8,128)S(1)} %get-tuple-element.63), channel_id=1, source_target_pairs={{0,8},{4,12},{8,0},{12,4},{1,9},{5,13},{9,1},{13,5},{2,10},{6,14},... | collective-permute-start | bytes 393224 | tf_op jit(solution)/shard_map/ppermute | solution.py:724
  36.5 3.1 %collective-permute-done.9.refs_1_ = f32[256,128]{1,0:T(8,128)S(1)} collective-permute-done((f32[256,128]{1,0:T(8,128)S(1)}, f32[256,128]{1,0:T(8,128)S(1)}, u32[]{:S(2)}, u32[]{:S(2)}) %collective-permute-start.9) | collective-permute-done | bytes 131104 | tf_op jit(solution)/shard_map/ppermute | solution.py:724
  39.6 1.9 %collective-permute-done.10.refs_2_ = f32[256,128]{1,0:T(8,128)S(1)} collective-permute-done((f32[256,128]{1,0:T(8,128)S(1)}, f32[256,128]{1,0:T(8,128)S(1)}, u32[]{:S(2)}, u32[]{:S(2)}) %collective-permute-start.10) | collective-permute-done | bytes 131104 | tf_op jit(solution)/shard_map/ppermute | solution.py:724
  41.5 3.6 %shard_map.143 = (f32[256,128]{1,0:T(8,128)S(1)}, f32[256,128]{1,0:T(8,128)S(1)}, f32[256,128]{1,0:T(8,128)S(1)}, f32[256,128]{1,0:T(8,128)S(1)}, bf16[512,1024]{1,0:T(8,128)(2,1)S(1)}) custom-call(f32[512,1024]{1,0:T(8,128)S(1)} %shard_map.139.base_ref, bf16[512,1024]{1,0:T(8,128)(2,1)S(1)} %bitcast.8, bf16[64,64]{1,0:T(8,128)(2,1)S(1)} %get-tuple-element.47.table_ref, ...), custom_call_target="tpu_custom_call" | custom-call | tf_op jit(solution)/shard_map/pallas_call | solution.py:713
  48.4 3.2 %collective-permute-done.12.refs_1_ = f32[256,128]{1,0:T(8,128)S(1)} collective-permute-done((f32[256,128]{1,0:T(8,128)S(1)}, f32[256,128]{1,0:T(8,128)S(1)}, u32[]{:S(2)}, u32[]{:S(2)}) %collective-permute-start.12) | collective-permute-done | bytes 131104 | tf_op jit(solution)/shard_map/ppermute | solution.py:724
  53.2 2.8 %collective-permute-start.16 = (f32[144,128]{1,0:T(8,128)S(1)}, f32[144,128]{1,0:T(8,128)S(1)}, u32[]{:S(2)}, u32[]{:S(2)}) collective-permute-start(f32[144,128]{1,0:T(8,128)S(1)} %get-tuple-element.75), channel_id=1, source_target_pairs={{0,2},{1,3},{2,0},{3,1},{4,6},{5,7},{6,4},{7,5},{8,10},{9,11},{10,... | collective-permute-start | bytes 221192 | tf_op jit(solution)/shard_map/ppermute | solution.py:724
  57.4 1.7 %collective-permute-done.15.refs_1_ = f32[144,128]{1,0:T(8,128)S(1)} collective-permute-done((f32[144,128]{1,0:T(8,128)S(1)}, f32[144,128]{1,0:T(8,128)S(1)}, u32[]{:S(2)}, u32[]{:S(2)}) %collective-permute-start.15) | collective-permute-done | bytes 73760 | tf_op jit(solution)/shard_map/ppermute | solution.py:724
  59.1 3.2 %collective-permute-done.16.refs_2_ = f32[144,128]{1,0:T(8,128)S(1)} collective-permute-done((f32[144,128]{1,0:T(8,128)S(1)}, f32[144,128]{1,0:T(8,128)S(1)}, u32[]{:S(2)}, u32[]{:S(2)}) %collective-permute-start.16) | collective-permute-done | bytes 73760 | tf_op jit(solution)/shard_map/ppermute | solution.py:724
  64.0 2.6 %collective-permute-start.20 = (f32[128,128]{1,0:T(8,128)S(1)}, f32[128,128]{1,0:T(8,128)S(1)}, u32[]{:S(2)}, u32[]{:S(2)}) collective-permute-start(f32[128,128]{1,0:T(8,128)S(1)} %get-tuple-element.77.refs_0_), channel_id=1, source_target_pairs={{0,3},{1,2},{2,1},{3,0},{4,7},{5,6},{6,5},{7,4},{8,11},{9,10},{10,... | collective-permute-start | bytes 196616 | tf_op jit(solution)/shard_map/ppermute | solution.py:724
  68.4 2.2 %collective-permute-done.20.refs_3_ = f32[128,128]{1,0:T(8,128)S(1)} collective-permute-done((f32[128,128]{1,0:T(8,128)S(1)}, f32[128,128]{1,0:T(8,128)S(1)}, u32[]{:S(2)}, u32[]{:S(2)}) %collective-permute-start.20) | collective-permute-done | bytes 65568 | tf_op jit(solution)/shard_map/ppermute | solution.py:724
  70.6 2.1 %collective-permute-done.19.refs_2_ = f32[128,128]{1,0:T(8,128)S(1)} collective-permute-done((f32[128,128]{1,0:T(8,128)S(1)}, f32[128,128]{1,0:T(8,128)S(1)}, u32[]{:S(2)}, u32[]{:S(2)}) %collective-permute-start.19) | collective-permute-done | bytes 65568 | tf_op jit(solution)/shard_map/ppermute | solution.py:724
  75.4 2.8 %shard_map.149 = f32[16,32768]{1,0:T(8,128)} custom-call(f32[32,512]{1,0:T(8,128)S(1)} %get-tuple-element.84.field_ref, f32[32,512]{1,0:T(8,128)S(1)} %get-tuple-element.85.adjoint_ref), custom_call_target="tpu_custom_call" | custom-call | tf_op jit(solution)/shard_map/pallas_call | solution.py:713
  78.8 2.0 %collective-permute-done.22.refs_2_ = f32[272,128]{1,0:T(8,128)S(1)} collective-permute-done((f32[272,128]{1,0:T(8,128)S(1)}, f32[272,128]{1,0:T(8,128)S(1)}, u32[]{:S(2)}, u32[]{:S(2)}) %collective-permute-start.22) | collective-permute-done | bytes 139296 | tf_op jit(solution)/shard_map/ppermute | solution.py:724
  80.8 2.5 %shard_map.148 = (bf16[512,1024]{1,0:T(8,128)(2,1)}, f32[32,32]{1,0:T(8,128)}, f32[1,32]{1,0:T(1,128)}) custom-call(f32[512,1024]{1,0:T(8,128)S(1)} %get-tuple-element.67.mixed_ref, bf16[64,96]{1,0:T(8,128)(2,1)S(1)} %get-tuple-element.48.back_ref, bf16[1024,1024]{1,0:T(8,128)(2,1)S(1)} %get-tuple-element.49.depth_ref, ...), custom_call_target="tpu_custom_call" | custom-call | tf_op jit(solution)/shard_map/pallas_call | solution.py:713
  (44 shorter events, 19.9 us)
Async XLA Ops:
  4.0 7.0 %collective-permute-start = (f32[256,128]{1,0:T(8,128)S(1)}, f32[256,128]{1,0:T(8,128)S(1)}, u32[]{:S(2)}, u32[]{:S(2)}) collective-permute-start(f32[256,128]{1,0:T(8,128)S(1)} %get-tuple-element.54), channel_id=1, source_target_pairs={{0,8},{4,12},{8,0},{12,4},{1,9},{5,13},{9,1},{13,5},{2,10},{6,14},... | collective-permute-start | bytes 393224 | tf_op jit(solution)/shard_map/ppermute | solution.py:724
  7.1 4.0 %collective-permute-start.1 = (f32[256,128]{1,0:T(8,128)S(1)}, f32[256,128]{1,0:T(8,128)S(1)}, u32[]{:S(2)}, u32[]{:S(2)}) collective-permute-start(f32[256,128]{1,0:T(8,128)S(1)} %get-tuple-element.55), channel_id=1, source_target_pairs={{0,4},{4,0},{8,12},{12,8},{1,5},{5,1},{9,13},{13,9},{2,6},{6,2},{1... | collective-permute-start | bytes 393224 | tf_op jit(solution)/shard_map/ppermute | solution.py:724
  7.1 5.9 %collective-permute-start.2 = (f32[256,128]{1,0:T(8,128)S(1)}, f32[256,128]{1,0:T(8,128)S(1)}, u32[]{:S(2)}, u32[]{:S(2)}) collective-permute-start(f32[256,128]{1,0:T(8,128)S(1)} %get-tuple-element.56), channel_id=1, source_target_pairs={{0,12},{4,8},{8,4},{12,0},{1,13},{5,9},{9,5},{13,1},{2,14},{6,10},... | collective-permute-start | bytes 393224 | tf_op jit(solution)/shard_map/ppermute | solution.py:724
  13.2 4.5 %collective-permute-start.3 = (f32[128,128]{1,0:T(8,128)S(1)}, f32[128,128]{1,0:T(8,128)S(1)}, u32[]{:S(2)}, u32[]{:S(2)}) collective-permute-start(f32[128,128]{1,0:T(8,128)S(1)} %get-tuple-element.58), channel_id=1, source_target_pairs={{0,1},{1,0},{2,3},{3,2},{4,5},{5,4},{6,7},{7,6},{8,9},{9,8},{10,11... | collective-permute-start | bytes 196616 | tf_op jit(solution)/shard_map/ppermute | solution.py:724
  14.8 6.9 %collective-permute-start.4 = (f32[128,128]{1,0:T(8,128)S(1)}, f32[128,128]{1,0:T(8,128)S(1)}, u32[]{:S(2)}, u32[]{:S(2)}) collective-permute-start(f32[128,128]{1,0:T(8,128)S(1)} %get-tuple-element.59), channel_id=1, source_target_pairs={{0,2},{1,3},{2,0},{3,1},{4,6},{5,7},{6,4},{7,5},{8,10},{9,11},{10,... | collective-permute-start | bytes 196616 | tf_op jit(solution)/shard_map/ppermute | solution.py:724
  17.4 6.1 %collective-permute-start.5 = (f32[128,128]{1,0:T(8,128)S(1)}, f32[128,128]{1,0:T(8,128)S(1)}, u32[]{:S(2)}, u32[]{:S(2)}) collective-permute-start(f32[128,128]{1,0:T(8,128)S(1)} %get-tuple-element.60), channel_id=1, source_target_pairs={{0,3},{1,2},{2,1},{3,0},{4,7},{5,6},{6,5},{7,4},{8,11},{9,10},{10,... | collective-permute-start | bytes 196616 | tf_op jit(solution)/shard_map/ppermute | solution.py:724
  24.7 6.8 %collective-permute-start.8 = (f32[128,128]{1,0:T(8,128)S(1)}, f32[128,128]{1,0:T(8,128)S(1)}, u32[]{:S(2)}, u32[]{:S(2)}) collective-permute-start(f32[128,128]{1,0:T(8,128)S(1)} %get-tuple-element.61.refs_0_), channel_id=1, source_target_pairs={{0,3},{1,2},{2,1},{3,0},{4,7},{5,6},{6,5},{7,4},{8,11},{9,10},{10,... | collective-permute-start | bytes 196616 | tf_op jit(solution)/shard_map/ppermute | solution.py:724
  27.2 6.3 %collective-permute-start.7 = (f32[128,128]{1,0:T(8,128)S(1)}, f32[128,128]{1,0:T(8,128)S(1)}, u32[]{:S(2)}, u32[]{:S(2)}) collective-permute-start(f32[128,128]{1,0:T(8,128)S(1)} %get-tuple-element.61.refs_0_), channel_id=1, source_target_pairs={{0,2},{1,3},{2,0},{3,1},{4,6},{5,7},{6,4},{7,5},{8,10},{9,11},{10,... | collective-permute-start | bytes 196616 | tf_op jit(solution)/shard_map/ppermute | solution.py:724
  27.5 6.0 %collective-permute-start.6 = (f32[128,128]{1,0:T(8,128)S(1)}, f32[128,128]{1,0:T(8,128)S(1)}, u32[]{:S(2)}, u32[]{:S(2)}) collective-permute-start(f32[128,128]{1,0:T(8,128)S(1)} %get-tuple-element.61.refs_0_), channel_id=1, source_target_pairs={{0,1},{1,0},{2,3},{3,2},{4,5},{5,4},{6,7},{7,6},{8,9},{9,8},{10,11... | collective-permute-start | bytes 196616 | tf_op jit(solution)/shard_map/ppermute | solution.py:724
  33.9 5.8 %collective-permute-start.9 = (f32[256,128]{1,0:T(8,128)S(1)}, f32[256,128]{1,0:T(8,128)S(1)}, u32[]{:S(2)}, u32[]{:S(2)}) collective-permute-start(f32[256,128]{1,0:T(8,128)S(1)} %get-tuple-element.63), channel_id=1, source_target_pairs={{0,8},{4,12},{8,0},{12,4},{1,9},{5,13},{9,1},{13,5},{2,10},{6,14},... | collective-permute-start | bytes 393224 | tf_op jit(solution)/shard_map/ppermute | solution.py:724
  35.7 5.8 %collective-permute-start.10 = (f32[256,128]{1,0:T(8,128)S(1)}, f32[256,128]{1,0:T(8,128)S(1)}, u32[]{:S(2)}, u32[]{:S(2)}) collective-permute-start(f32[256,128]{1,0:T(8,128)S(1)} %get-tuple-element.64), channel_id=1, source_target_pairs={{0,12},{4,8},{8,4},{12,0},{1,13},{5,9},{9,5},{13,1},{2,14},{6,10},... | collective-permute-start | bytes 393224 | tf_op jit(solution)/shard_map/ppermute | solution.py:724
  35.7 5.8 %collective-permute-start.11 = (f32[256,128]{1,0:T(8,128)S(1)}, f32[256,128]{1,0:T(8,128)S(1)}, u32[]{:S(2)}, u32[]{:S(2)}) collective-permute-start(f32[256,128]{1,0:T(8,128)S(1)} %get-tuple-element.65), channel_id=1, source_target_pairs={{0,4},{4,0},{8,12},{12,8},{1,5},{5,1},{9,13},{13,9},{2,6},{6,2},{1... | collective-permute-start | bytes 393224 | tf_op jit(solution)/shard_map/ppermute | solution.py:724
  45.1 6.4 %collective-permute-start.12 = (f32[256,128]{1,0:T(8,128)S(1)}, f32[256,128]{1,0:T(8,128)S(1)}, u32[]{:S(2)}, u32[]{:S(2)}) collective-permute-start(f32[256,128]{1,0:T(8,128)S(1)} %get-tuple-element.69), channel_id=1, source_target_pairs={{0,8},{4,12},{8,0},{12,4},{1,9},{5,13},{9,1},{13,5},{2,10},{6,14},... | collective-permute-start | bytes 393224 | tf_op jit(solution)/shard_map/ppermute | solution.py:724
  45.8 5.8 %collective-permute-start.13 = (f32[256,128]{1,0:T(8,128)S(1)}, f32[256,128]{1,0:T(8,128)S(1)}, u32[]{:S(2)}, u32[]{:S(2)}) collective-permute-start(f32[256,128]{1,0:T(8,128)S(1)} %get-tuple-element.70), channel_id=1, source_target_pairs={{0,4},{4,0},{8,12},{12,8},{1,5},{5,1},{9,13},{13,9},{2,6},{6,2},{1... | collective-permute-start | bytes 393224 | tf_op jit(solution)/shard_map/ppermute | solution.py:724
  46.7 6.0 %collective-permute-start.14 = (f32[256,128]{1,0:T(8,128)S(1)}, f32[256,128]{1,0:T(8,128)S(1)}, u32[]{:S(2)}, u32[]{:S(2)}) collective-permute-start(f32[256,128]{1,0:T(8,128)S(1)} %get-tuple-element.71), channel_id=1, source_target_pairs={{0,12},{4,8},{8,4},{12,0},{1,13},{5,9},{9,5},{13,1},{2,14},{6,10},... | collective-permute-start | bytes 393224 | tf_op jit(solution)/shard_map/ppermute | solution.py:724
  53.0 6.2 %collective-permute-start.15 = (f32[144,128]{1,0:T(8,128)S(1)}, f32[144,128]{1,0:T(8,128)S(1)}, u32[]{:S(2)}, u32[]{:S(2)}) collective-permute-start(f32[144,128]{1,0:T(8,128)S(1)} %get-tuple-element.74), channel_id=1, source_target_pairs={{0,1},{1,0},{2,3},{3,2},{4,5},{5,4},{6,7},{7,6},{8,9},{9,8},{10,11... | collective-permute-start | bytes 221192 | tf_op jit(solution)/shard_map/ppermute | solution.py:724
  53.2 9.2 %collective-permute-start.16 = (f32[144,128]{1,0:T(8,128)S(1)}, f32[144,128]{1,0:T(8,128)S(1)}, u32[]{:S(2)}, u32[]{:S(2)}) collective-permute-start(f32[144,128]{1,0:T(8,128)S(1)} %get-tuple-element.75), channel_id=1, source_target_pairs={{0,2},{1,3},{2,0},{3,1},{4,6},{5,7},{6,4},{7,5},{8,10},{9,11},{10,... | collective-permute-start | bytes 221192 | tf_op jit(solution)/shard_map/ppermute | solution.py:724
  56.0 6.4 %collective-permute-start.17 = (f32[144,128]{1,0:T(8,128)S(1)}, f32[144,128]{1,0:T(8,128)S(1)}, u32[]{:S(2)}, u32[]{:S(2)}) collective-permute-start(f32[144,128]{1,0:T(8,128)S(1)} %get-tuple-element.76), channel_id=1, source_target_pairs={{0,3},{1,2},{2,1},{3,0},{4,7},{5,6},{6,5},{7,4},{8,11},{9,10},{10,... | collective-permute-start | bytes 221192 | tf_op jit(solution)/shard_map/ppermute | solution.py:724
  64.0 6.7 %collective-permute-start.20 = (f32[128,128]{1,0:T(8,128)S(1)}, f32[128,128]{1,0:T(8,128)S(1)}, u32[]{:S(2)}, u32[]{:S(2)}) collective-permute-start(f32[128,128]{1,0:T(8,128)S(1)} %get-tuple-element.77.refs_0_), channel_id=1, source_target_pairs={{0,3},{1,2},{2,1},{3,0},{4,7},{5,6},{6,5},{7,4},{8,11},{9,10},{10,... | collective-permute-start | bytes 196616 | tf_op jit(solution)/shard_map/ppermute | solution.py:724
  66.5 6.2 %collective-permute-start.19 = (f32[128,128]{1,0:T(8,128)S(1)}, f32[128,128]{1,0:T(8,128)S(1)}, u32[]{:S(2)}, u32[]{:S(2)}) collective-permute-start(f32[128,128]{1,0:T(8,128)S(1)} %get-tuple-element.77.refs_0_), channel_id=1, source_target_pairs={{0,2},{1,3},{2,0},{3,1},{4,6},{5,7},{6,4},{7,5},{8,10},{9,11},{10,... | collective-permute-start | bytes 196616 | tf_op jit(solution)/shard_map/ppermute | solution.py:724
  67.3 5.4 %collective-permute-start.18 = (f32[128,128]{1,0:T(8,128)S(1)}, f32[128,128]{1,0:T(8,128)S(1)}, u32[]{:S(2)}, u32[]{:S(2)}) collective-permute-start(f32[128,128]{1,0:T(8,128)S(1)} %get-tuple-element.77.refs_0_), channel_id=1, source_target_pairs={{0,1},{1,0},{2,3},{3,2},{4,5},{5,4},{6,7},{7,6},{8,9},{9,8},{10,11... | collective-permute-start | bytes 196616 | tf_op jit(solution)/shard_map/ppermute | solution.py:724
  73.2 5.6 %collective-permute-start.21 = (f32[272,128]{1,0:T(8,128)S(1)}, f32[272,128]{1,0:T(8,128)S(1)}, u32[]{:S(2)}, u32[]{:S(2)}) collective-permute-start(f32[272,128]{1,0:T(8,128)S(1)} %get-tuple-element.80), channel_id=1, source_target_pairs={{0,8},{4,12},{8,0},{12,4},{1,9},{5,13},{9,1},{13,5},{2,10},{6,14},... | collective-permute-start | bytes 417800 | tf_op jit(solution)/shard_map/ppermute | solution.py:724
  74.8 6.0 %collective-permute-start.22 = (f32[272,128]{1,0:T(8,128)S(1)}, f32[272,128]{1,0:T(8,128)S(1)}, u32[]{:S(2)}, u32[]{:S(2)}) collective-permute-start(f32[272,128]{1,0:T(8,128)S(1)} %get-tuple-element.81), channel_id=1, source_target_pairs={{0,12},{4,8},{8,4},{12,0},{1,13},{5,9},{9,5},{13,1},{2,14},{6,10},... | collective-permute-start | bytes 417800 | tf_op jit(solution)/shard_map/ppermute | solution.py:724
  74.8 6.0 %collective-permute-start.23 = (f32[272,128]{1,0:T(8,128)S(1)}, f32[272,128]{1,0:T(8,128)S(1)}, u32[]{:S(2)}, u32[]{:S(2)}) collective-permute-start(f32[272,128]{1,0:T(8,128)S(1)} %get-tuple-element.82), channel_id=1, source_target_pairs={{0,4},{4,0},{8,12},{12,8},{1,5},{5,1},{9,13},{13,9},{2,6},{6,2},{1... | collective-permute-start | bytes 417800 | tf_op jit(solution)/shard_map/ppermute | solution.py:724
  (4 other events, 110.5 us)

commit v5 on v4

--- a/solution.py
+++ b/solution.py
@@ -481,8 +481,10 @@
     values = tripled(jnp.concatenate([read_lanes(ref, 2 * KX) for ref in in_refs], axis=0))
     own = lax.axis_index("gx")
     rows = table_ref.shape[1]
+    table = jnp.concatenate([table_ref[own ^ turn] for turn in range(turns)], axis=0)
+    cells = dot(table, values)
     for turn, ref in enumerate(refs[-turns:]):
-        write_lanes(ref, dot(table_ref[own ^ turn], values), rows)
+        write_lanes(ref, cells[turn * rows : (turn + 1) * rows], rows)
         if len(refs) > turns:
             ref[CHUNKS * rows :, :] = refs[0][...]
 
@@ -531,7 +533,7 @@
         scratch[pl.ds(start, 2 * KZ), :] = jnp.concatenate([real_sum, imag_sum], axis=0)
         return carry
 
-    lax.fori_loop(0, KX, step, 0, unroll=4)
+    lax.fori_loop(0, KX, step, 0, unroll=KX)
     shape = (LANES, LANES)
     same = (iota(shape, 0) % C == iota(shape, 1) % C).astype(F32).astype(BF)
     high, low = halves(scratch[...])
@@ -626,7 +628,7 @@
         wide[1, pl.ds(start, 2 * KZ), :] = low
         return carry
 
-    lax.fori_loop(0, KX, step, 0, unroll=4)
+    lax.fori_loop(0, KX, step, 0, unroll=KX)
     total = dot(wide[0], spread_ref[...], ((1,), (1,)))
     total = total + dot(wide[1], spread_ref[...], ((1,), (1,)))
     scratch[...] = own_rows(total)

time: 83.5 us -> 82.1 us (0.983)
  Pallas kernels: 18 us -> 16.5 us
    pallas_call x12, Pallas kernels: 18 us -> 16.5 us  [run(): return function(*map(pltpu.with_memory_space_constraint, arguments, spaces))]
where the time goes in v5:
time: 82.1 us; the launch traced here: 82 us
  waiting for transfers between devices  37 us (45%)
  starting transfers between devices  27.7 us (34%)
  Pallas kernels  16.5 us (20%)
    ppermute x24, waiting for transfers between devices, exchange(): received[turn] = lax.ppermute(blocks[turn], axis, pairs)  37 us
    ppermute x24, starting transfers between devices, exchange(): received[turn] = lax.ppermute(blocks[turn], axis, pairs)  27.7 us
    pallas_call x12, Pallas kernels, run(): return function(*map(pltpu.with_memory_space_constraint, arguments, spaces))  16.5 us
  transfers between devices with their start and end apart: 24, of which 16 were waited for; matrix products, arithmetic and copies ran while one was open for 0% of the time, Pallas kernels for 5%

profile of v5, /device:TPU:0, one launch (start us, length us, event | category | flops | bytes accessed | tf_op | source)
XLA Modules:
  0.0 82.0 jit_solution(2803679296304579681)
XLA Ops:
  0.7 3.4 %shard_map.138 = (f32[256,128]{1,0:T(8,128)S(1)}, f32[256,128]{1,0:T(8,128)S(1)}, f32[256,128]{1,0:T(8,128)S(1)}, f32[256,128]{1,0:T(8,128)S(1)}, bf16[1024,1024...) custom-call(bf16[512,1024]{1,0:T(8,128)(2,1)} %bitcast.5, ...), custom_call_target="tpu_custom_call" | custom-call | tf_op jit(solution)/shard_map/pallas_call | solution.py:715
  4.0 3.0 %collective-permute-start = (f32[256,128]{1,0:T(8,128)S(1)}, f32[256,128]{1,0:T(8,128)S(1)}, u32[]{:S(2)}, u32[]{:S(2)}) collective-permute-start(f32[256,128]{1,0:T(8,128)S(1)} %get-tuple-element.54), channel_id=1, source_target_pairs={{0,8},{4,12},{8,0},{12,4},{1,9},{5,13},{9,1},{13,5},{2,10},{6,14},... | collective-permute-start | bytes 393224 | tf_op jit(solution)/shard_map/ppermute | solution.py:726
  7.3 3.7 %collective-permute-done.refs_1_ = f32[256,128]{1,0:T(8,128)S(1)} collective-permute-done((f32[256,128]{1,0:T(8,128)S(1)}, f32[256,128]{1,0:T(8,128)S(1)}, u32[]{:S(2)}, u32[]{:S(2)}) %collective-permute-start) | collective-permute-done | bytes 131104 | tf_op jit(solution)/shard_map/ppermute | solution.py:726
  11.0 1.9 %collective-permute-done.2.refs_3_ = f32[256,128]{1,0:T(8,128)S(1)} collective-permute-done((f32[256,128]{1,0:T(8,128)S(1)}, f32[256,128]{1,0:T(8,128)S(1)}, u32[]{:S(2)}, u32[]{:S(2)}) %collective-permute-start.2) | collective-permute-done | bytes 131104 | tf_op jit(solution)/shard_map/ppermute | solution.py:726
  14.8 2.6 %collective-permute-start.4 = (f32[128,128]{1,0:T(8,128)S(1)}, f32[128,128]{1,0:T(8,128)S(1)}, u32[]{:S(2)}, u32[]{:S(2)}) collective-permute-start(f32[128,128]{1,0:T(8,128)S(1)} %get-tuple-element.59), channel_id=1, source_target_pairs={{0,2},{1,3},{2,0},{3,1},{4,6},{5,7},{6,4},{7,5},{8,10},{9,11},{10,... | collective-permute-start | bytes 196616 | tf_op jit(solution)/shard_map/ppermute | solution.py:726
  17.7 4.0 %collective-permute-done.4.refs_2_ = f32[128,128]{1,0:T(8,128)S(1)} collective-permute-done((f32[128,128]{1,0:T(8,128)S(1)}, f32[128,128]{1,0:T(8,128)S(1)}, u32[]{:S(2)}, u32[]{:S(2)}) %collective-permute-start.4) | collective-permute-done | bytes 65568 | tf_op jit(solution)/shard_map/ppermute | solution.py:726
  21.7 1.8 %collective-permute-done.5.refs_3_ = f32[128,128]{1,0:T(8,128)S(1)} collective-permute-done((f32[128,128]{1,0:T(8,128)S(1)}, f32[128,128]{1,0:T(8,128)S(1)}, u32[]{:S(2)}, u32[]{:S(2)}) %collective-permute-start.5) | collective-permute-done | bytes 65568 | tf_op jit(solution)/shard_map/ppermute | solution.py:726
  24.3 2.5 %collective-permute-start.8 = (f32[128,128]{1,0:T(8,128)S(1)}, f32[128,128]{1,0:T(8,128)S(1)}, u32[]{:S(2)}, u32[]{:S(2)}) collective-permute-start(f32[128,128]{1,0:T(8,128)S(1)} %get-tuple-element.61.refs_0_), channel_id=1, source_target_pairs={{0,3},{1,2},{2,1},{3,0},{4,7},{5,6},{6,5},{7,4},{8,11},{9,10},{10,... | collective-permute-start | bytes 196616 | tf_op jit(solution)/shard_map/ppermute | solution.py:726
  28.7 2.3 %collective-permute-done.8.refs_3_ = f32[128,128]{1,0:T(8,128)S(1)} collective-permute-done((f32[128,128]{1,0:T(8,128)S(1)}, f32[128,128]{1,0:T(8,128)S(1)}, u32[]{:S(2)}, u32[]{:S(2)}) %collective-permute-start.8) | collective-permute-done | bytes 65568 | tf_op jit(solution)/shard_map/ppermute | solution.py:726
  31.1 1.9 %collective-permute-done.7.refs_2_ = f32[128,128]{1,0:T(8,128)S(1)} collective-permute-done((f32[128,128]{1,0:T(8,128)S(1)}, f32[128,128]{1,0:T(8,128)S(1)}, u32[]{:S(2)}, u32[]{:S(2)}) %collective-permute-start.7) | collective-permute-done | bytes 65568 | tf_op jit(solution)/shard_map/ppermute | solution.py:726
  33.3 1.8 %collective-permute-start.9 = (f32[256,128]{1,0:T(8,128)S(1)}, f32[256,128]{1,0:T(8,128)S(1)}, u32[]{:S(2)}, u32[]{:S(2)}) collective-permute-start(f32[256,128]{1,0:T(8,128)S(1)} %get-tuple-element.63), channel_id=1, source_target_pairs={{0,8},{4,12},{8,0},{12,4},{1,9},{5,13},{9,1},{13,5},{2,10},{6,14},... | collective-permute-start | bytes 393224 | tf_op jit(solution)/shard_map/ppermute | solution.py:726
  36.0 3.1 %collective-permute-done.9.refs_1_ = f32[256,128]{1,0:T(8,128)S(1)} collective-permute-done((f32[256,128]{1,0:T(8,128)S(1)}, f32[256,128]{1,0:T(8,128)S(1)}, u32[]{:S(2)}, u32[]{:S(2)}) %collective-permute-start.9) | collective-permute-done | bytes 131104 | tf_op jit(solution)/shard_map/ppermute | solution.py:726
  39.1 1.9 %collective-permute-done.10.refs_2_ = f32[256,128]{1,0:T(8,128)S(1)} collective-permute-done((f32[256,128]{1,0:T(8,128)S(1)}, f32[256,128]{1,0:T(8,128)S(1)}, u32[]{:S(2)}, u32[]{:S(2)}) %collective-permute-start.10) | collective-permute-done | bytes 131104 | tf_op jit(solution)/shard_map/ppermute | solution.py:726
  41.0 3.6 %shard_map.143 = (f32[256,128]{1,0:T(8,128)S(1)}, f32[256,128]{1,0:T(8,128)S(1)}, f32[256,128]{1,0:T(8,128)S(1)}, f32[256,128]{1,0:T(8,128)S(1)}, bf16[512,1024]{1,0:T(8,128)(2,1)S(1)}) custom-call(f32[512,1024]{1,0:T(8,128)S(1)} %shard_map.139.base_ref, bf16[512,1024]{1,0:T(8,128)(2,1)S(1)} %bitcast.8, bf16[64,64]{1,0:T(8,128)(2,1)S(1)} %get-tuple-element.47.table_ref, ...), custom_call_target="tpu_custom_call" | custom-call | tf_op jit(solution)/shard_map/pallas_call | solution.py:715
  47.8 3.2 %collective-permute-done.12.refs_1_ = f32[256,128]{1,0:T(8,128)S(1)} collective-permute-done((f32[256,128]{1,0:T(8,128)S(1)}, f32[256,128]{1,0:T(8,128)S(1)}, u32[]{:S(2)}, u32[]{:S(2)}) %collective-permute-start.12) | collective-permute-done | bytes 131104 | tf_op jit(solution)/shard_map/ppermute | solution.py:726
  52.7 2.8 %collective-permute-start.16 = (f32[144,128]{1,0:T(8,128)S(1)}, f32[144,128]{1,0:T(8,128)S(1)}, u32[]{:S(2)}, u32[]{:S(2)}) collective-permute-start(f32[144,128]{1,0:T(8,128)S(1)} %get-tuple-element.75), channel_id=1, source_target_pairs={{0,2},{1,3},{2,0},{3,1},{4,6},{5,7},{6,4},{7,5},{8,10},{9,11},{10,... | collective-permute-start | bytes 221192 | tf_op jit(solution)/shard_map/ppermute | solution.py:726
  58.6 3.3 %collective-permute-done.16.refs_2_ = f32[144,128]{1,0:T(8,128)S(1)} collective-permute-done((f32[144,128]{1,0:T(8,128)S(1)}, f32[144,128]{1,0:T(8,128)S(1)}, u32[]{:S(2)}, u32[]{:S(2)}) %collective-permute-start.16) | collective-permute-done | bytes 73760 | tf_op jit(solution)/shard_map/ppermute | solution.py:726
  62.6 2.6 %collective-permute-start.20 = (f32[128,128]{1,0:T(8,128)S(1)}, f32[128,128]{1,0:T(8,128)S(1)}, u32[]{:S(2)}, u32[]{:S(2)}) collective-permute-start(f32[128,128]{1,0:T(8,128)S(1)} %get-tuple-element.77.refs_0_), channel_id=1, source_target_pairs={{0,3},{1,2},{2,1},{3,0},{4,7},{5,6},{6,5},{7,4},{8,11},{9,10},{10,... | collective-permute-start | bytes 196616 | tf_op jit(solution)/shard_map/ppermute | solution.py:726
  67.1 2.2 %collective-permute-done.20.refs_3_ = f32[128,128]{1,0:T(8,128)S(1)} collective-permute-done((f32[128,128]{1,0:T(8,128)S(1)}, f32[128,128]{1,0:T(8,128)S(1)}, u32[]{:S(2)}, u32[]{:S(2)}) %collective-permute-start.20) | collective-permute-done | bytes 65568 | tf_op jit(solution)/shard_map/ppermute | solution.py:726
  69.3 2.1 %collective-permute-done.19.refs_2_ = f32[128,128]{1,0:T(8,128)S(1)} collective-permute-done((f32[128,128]{1,0:T(8,128)S(1)}, f32[128,128]{1,0:T(8,128)S(1)}, u32[]{:S(2)}, u32[]{:S(2)}) %collective-permute-start.19) | collective-permute-done | bytes 65568 | tf_op jit(solution)/shard_map/ppermute | solution.py:726
  71.7 1.7 %collective-permute-start.21 = (f32[272,128]{1,0:T(8,128)S(1)}, f32[272,128]{1,0:T(8,128)S(1)}, u32[]{:S(2)}, u32[]{:S(2)}) collective-permute-start(f32[272,128]{1,0:T(8,128)S(1)} %get-tuple-element.80), channel_id=1, source_target_pairs={{0,8},{4,12},{8,0},{12,4},{1,9},{5,13},{9,1},{13,5},{2,10},{6,14},... | collective-permute-start | bytes 417800 | tf_op jit(solution)/shard_map/ppermute | solution.py:726
  73.9 2.8 %shard_map.149 = f32[16,32768]{1,0:T(8,128)} custom-call(f32[32,512]{1,0:T(8,128)S(1)} %get-tuple-element.84.field_ref, f32[32,512]{1,0:T(8,128)S(1)} %get-tuple-element.85.adjoint_ref), custom_call_target="tpu_custom_call" | custom-call | tf_op jit(solution)/shard_map/pallas_call | solution.py:715
  77.3 2.1 %collective-permute-done.22.refs_2_ = f32[272,128]{1,0:T(8,128)S(1)} collective-permute-done((f32[272,128]{1,0:T(8,128)S(1)}, f32[272,128]{1,0:T(8,128)S(1)}, u32[]{:S(2)}, u32[]{:S(2)}) %collective-permute-start.22) | collective-permute-done | bytes 139296 | tf_op jit(solution)/shard_map/ppermute | solution.py:726
  79.4 2.5 %shard_map.148 = (bf16[512,1024]{1,0:T(8,128)(2,1)}, f32[32,32]{1,0:T(8,128)}, f32[1,32]{1,0:T(1,128)}) custom-call(f32[512,1024]{1,0:T(8,128)S(1)} %get-tuple-element.67.mixed_ref, bf16[64,96]{1,0:T(8,128)(2,1)S(1)} %get-tuple-element.48.back_ref, bf16[1024,1024]{1,0:T(8,128)(2,1)S(1)} %get-tuple-element.49.depth_ref, ...), custom_call_target="tpu_custom_call" | custom-call | tf_op jit(solution)/shard_map/pallas_call | solution.py:715
  (44 shorter events, 18.4 us)
Async XLA Ops:
  4.0 7.0 %collective-permute-start = (f32[256,128]{1,0:T(8,128)S(1)}, f32[256,128]{1,0:T(8,128)S(1)}, u32[]{:S(2)}, u32[]{:S(2)}) collective-permute-start(f32[256,128]{1,0:T(8,128)S(1)} %get-tuple-element.54), channel_id=1, source_target_pairs={{0,8},{4,12},{8,0},{12,4},{1,9},{5,13},{9,1},{13,5},{2,10},{6,14},... | collective-permute-start | bytes 393224 | tf_op jit(solution)/shard_map/ppermute | solution.py:726
  7.1 4.0 %collective-permute-start.1 = (f32[256,128]{1,0:T(8,128)S(1)}, f32[256,128]{1,0:T(8,128)S(1)}, u32[]{:S(2)}, u32[]{:S(2)}) collective-permute-start(f32[256,128]{1,0:T(8,128)S(1)} %get-tuple-element.55), channel_id=1, source_target_pairs={{0,4},{4,0},{8,12},{12,8},{1,5},{5,1},{9,13},{13,9},{2,6},{6,2},{1... | collective-permute-start | bytes 393224 | tf_op jit(solution)/shard_map/ppermute | solution.py:726
  7.1 5.9 %collective-permute-start.2 = (f32[256,128]{1,0:T(8,128)S(1)}, f32[256,128]{1,0:T(8,128)S(1)}, u32[]{:S(2)}, u32[]{:S(2)}) collective-permute-start(f32[256,128]{1,0:T(8,128)S(1)} %get-tuple-element.56), channel_id=1, source_target_pairs={{0,12},{4,8},{8,4},{12,0},{1,13},{5,9},{9,5},{13,1},{2,14},{6,10},... | collective-permute-start | bytes 393224 | tf_op jit(solution)/shard_map/ppermute | solution.py:726
  13.2 4.5 %collective-permute-start.3 = (f32[128,128]{1,0:T(8,128)S(1)}, f32[128,128]{1,0:T(8,128)S(1)}, u32[]{:S(2)}, u32[]{:S(2)}) collective-permute-start(f32[128,128]{1,0:T(8,128)S(1)} %get-tuple-element.58), channel_id=1, source_target_pairs={{0,1},{1,0},{2,3},{3,2},{4,5},{5,4},{6,7},{7,6},{8,9},{9,8},{10,11... | collective-permute-start | bytes 196616 | tf_op jit(solution)/shard_map/ppermute | solution.py:726
  14.8 6.9 %collective-permute-start.4 = (f32[128,128]{1,0:T(8,128)S(1)}, f32[128,128]{1,0:T(8,128)S(1)}, u32[]{:S(2)}, u32[]{:S(2)}) collective-permute-start(f32[128,128]{1,0:T(8,128)S(1)} %get-tuple-element.59), channel_id=1, source_target_pairs={{0,2},{1,3},{2,0},{3,1},{4,6},{5,7},{6,4},{7,5},{8,10},{9,11},{10,... | collective-permute-start | bytes 196616 | tf_op jit(solution)/shard_map/ppermute | solution.py:726
  17.4 6.1 %collective-permute-start.5 = (f32[128,128]{1,0:T(8,128)S(1)}, f32[128,128]{1,0:T(8,128)S(1)}, u32[]{:S(2)}, u32[]{:S(2)}) collective-permute-start(f32[128,128]{1,0:T(8,128)S(1)} %get-tuple-element.60), channel_id=1, source_target_pairs={{0,3},{1,2},{2,1},{3,0},{4,7},{5,6},{6,5},{7,4},{8,11},{9,10},{10,... | collective-permute-start | bytes 196616 | tf_op jit(solution)/shard_map/ppermute | solution.py:726
  24.3 6.8 %collective-permute-start.8 = (f32[128,128]{1,0:T(8,128)S(1)}, f32[128,128]{1,0:T(8,128)S(1)}, u32[]{:S(2)}, u32[]{:S(2)}) collective-permute-start(f32[128,128]{1,0:T(8,128)S(1)} %get-tuple-element.61.refs_0_), channel_id=1, source_target_pairs={{0,3},{1,2},{2,1},{3,0},{4,7},{5,6},{6,5},{7,4},{8,11},{9,10},{10,... | collective-permute-start | bytes 196616 | tf_op jit(solution)/shard_map/ppermute | solution.py:726
  26.8 6.3 %collective-permute-start.7 = (f32[128,128]{1,0:T(8,128)S(1)}, f32[128,128]{1,0:T(8,128)S(1)}, u32[]{:S(2)}, u32[]{:S(2)}) collective-permute-start(f32[128,128]{1,0:T(8,128)S(1)} %get-tuple-element.61.refs_0_), channel_id=1, source_target_pairs={{0,2},{1,3},{2,0},{3,1},{4,6},{5,7},{6,4},{7,5},{8,10},{9,11},{10,... | collective-permute-start | bytes 196616 | tf_op jit(solution)/shard_map/ppermute | solution.py:726
  27.1 6.0 %collective-permute-start.6 = (f32[128,128]{1,0:T(8,128)S(1)}, f32[128,128]{1,0:T(8,128)S(1)}, u32[]{:S(2)}, u32[]{:S(2)}) collective-permute-start(f32[128,128]{1,0:T(8,128)S(1)} %get-tuple-element.61.refs_0_), channel_id=1, source_target_pairs={{0,1},{1,0},{2,3},{3,2},{4,5},{5,4},{6,7},{7,6},{8,9},{9,8},{10,11... | collective-permute-start | bytes 196616 | tf_op jit(solution)/shard_map/ppermute | solution.py:726
  33.3 5.8 %collective-permute-start.9 = (f32[256,128]{1,0:T(8,128)S(1)}, f32[256,128]{1,0:T(8,128)S(1)}, u32[]{:S(2)}, u32[]{:S(2)}) collective-permute-start(f32[256,128]{1,0:T(8,128)S(1)} %get-tuple-element.63), channel_id=1, source_target_pairs={{0,8},{4,12},{8,0},{12,4},{1,9},{5,13},{9,1},{13,5},{2,10},{6,14},... | collective-permute-start | bytes 393224 | tf_op jit(solution)/shard_map/ppermute | solution.py:726
  35.1 5.8 %collective-permute-start.10 = (f32[256,128]{1,0:T(8,128)S(1)}, f32[256,128]{1,0:T(8,128)S(1)}, u32[]{:S(2)}, u32[]{:S(2)}) collective-permute-start(f32[256,128]{1,0:T(8,128)S(1)} %get-tuple-element.64), channel_id=1, source_target_pairs={{0,12},{4,8},{8,4},{12,0},{1,13},{5,9},{9,5},{13,1},{2,14},{6,10},... | collective-permute-start | bytes 393224 | tf_op jit(solution)/shard_map/ppermute | solution.py:726
  35.2 5.8 %collective-permute-start.11 = (f32[256,128]{1,0:T(8,128)S(1)}, f32[256,128]{1,0:T(8,128)S(1)}, u32[]{:S(2)}, u32[]{:S(2)}) collective-permute-start(f32[256,128]{1,0:T(8,128)S(1)} %get-tuple-element.65), channel_id=1, source_target_pairs={{0,4},{4,0},{8,12},{12,8},{1,5},{5,1},{9,13},{13,9},{2,6},{6,2},{1... | collective-permute-start | bytes 393224 | tf_op jit(solution)/shard_map/ppermute | solution.py:726
  44.6 6.4 %collective-permute-start.12 = (f32[256,128]{1,0:T(8,128)S(1)}, f32[256,128]{1,0:T(8,128)S(1)}, u32[]{:S(2)}, u32[]{:S(2)}) collective-permute-start(f32[256,128]{1,0:T(8,128)S(1)} %get-tuple-element.69), channel_id=1, source_target_pairs={{0,8},{4,12},{8,0},{12,4},{1,9},{5,13},{9,1},{13,5},{2,10},{6,14},... | collective-permute-start | bytes 393224 | tf_op jit(solution)/shard_map/ppermute | solution.py:726
  45.2 5.8 %collective-permute-start.13 = (f32[256,128]{1,0:T(8,128)S(1)}, f32[256,128]{1,0:T(8,128)S(1)}, u32[]{:S(2)}, u32[]{:S(2)}) collective-permute-start(f32[256,128]{1,0:T(8,128)S(1)} %get-tuple-element.70), channel_id=1, source_target_pairs={{0,4},{4,0},{8,12},{12,8},{1,5},{5,1},{9,13},{13,9},{2,6},{6,2},{1... | collective-permute-start | bytes 393224 | tf_op jit(solution)/shard_map/ppermute | solution.py:726
  46.2 6.0 %collective-permute-start.14 = (f32[256,128]{1,0:T(8,128)S(1)}, f32[256,128]{1,0:T(8,128)S(1)}, u32[]{:S(2)}, u32[]{:S(2)}) collective-permute-start(f32[256,128]{1,0:T(8,128)S(1)} %get-tuple-element.71), channel_id=1, source_target_pairs={{0,12},{4,8},{8,4},{12,0},{1,13},{5,9},{9,5},{13,1},{2,14},{6,10},... | collective-permute-start | bytes 393224 | tf_op jit(solution)/shard_map/ppermute | solution.py:726
  52.4 6.2 %collective-permute-start.15 = (f32[144,128]{1,0:T(8,128)S(1)}, f32[144,128]{1,0:T(8,128)S(1)}, u32[]{:S(2)}, u32[]{:S(2)}) collective-permute-start(f32[144,128]{1,0:T(8,128)S(1)} %get-tuple-element.74), channel_id=1, source_target_pairs={{0,1},{1,0},{2,3},{3,2},{4,5},{5,4},{6,7},{7,6},{8,9},{9,8},{10,11... | collective-permute-start | bytes 221192 | tf_op jit(solution)/shard_map/ppermute | solution.py:726
  52.7 9.2 %collective-permute-start.16 = (f32[144,128]{1,0:T(8,128)S(1)}, f32[144,128]{1,0:T(8,128)S(1)}, u32[]{:S(2)}, u32[]{:S(2)}) collective-permute-start(f32[144,128]{1,0:T(8,128)S(1)} %get-tuple-element.75), channel_id=1, source_target_pairs={{0,2},{1,3},{2,0},{3,1},{4,6},{5,7},{6,4},{7,5},{8,10},{9,11},{10,... | collective-permute-start | bytes 221192 | tf_op jit(solution)/shard_map/ppermute | solution.py:726
  55.4 6.4 %collective-permute-start.17 = (f32[144,128]{1,0:T(8,128)S(1)}, f32[144,128]{1,0:T(8,128)S(1)}, u32[]{:S(2)}, u32[]{:S(2)}) collective-permute-start(f32[144,128]{1,0:T(8,128)S(1)} %get-tuple-element.76), channel_id=1, source_target_pairs={{0,3},{1,2},{2,1},{3,0},{4,7},{5,6},{6,5},{7,4},{8,11},{9,10},{10,... | collective-permute-start | bytes 221192 | tf_op jit(solution)/shard_map/ppermute | solution.py:726
  62.6 6.7 %collective-permute-start.20 = (f32[128,128]{1,0:T(8,128)S(1)}, f32[128,128]{1,0:T(8,128)S(1)}, u32[]{:S(2)}, u32[]{:S(2)}) collective-permute-start(f32[128,128]{1,0:T(8,128)S(1)} %get-tuple-element.77.refs_0_), channel_id=1, source_target_pairs={{0,3},{1,2},{2,1},{3,0},{4,7},{5,6},{6,5},{7,4},{8,11},{9,10},{10,... | collective-permute-start | bytes 196616 | tf_op jit(solution)/shard_map/ppermute | solution.py:726
  65.2 6.2 %collective-permute-start.19 = (f32[128,128]{1,0:T(8,128)S(1)}, f32[128,128]{1,0:T(8,128)S(1)}, u32[]{:S(2)}, u32[]{:S(2)}) collective-permute-start(f32[128,128]{1,0:T(8,128)S(1)} %get-tuple-element.77.refs_0_), channel_id=1, source_target_pairs={{0,2},{1,3},{2,0},{3,1},{4,6},{5,7},{6,4},{7,5},{8,10},{9,11},{10,... | collective-permute-start | bytes 196616 | tf_op jit(solution)/shard_map/ppermute | solution.py:726
  66.0 5.4 %collective-permute-start.18 = (f32[128,128]{1,0:T(8,128)S(1)}, f32[128,128]{1,0:T(8,128)S(1)}, u32[]{:S(2)}, u32[]{:S(2)}) collective-permute-start(f32[128,128]{1,0:T(8,128)S(1)} %get-tuple-element.77.refs_0_), channel_id=1, source_target_pairs={{0,1},{1,0},{2,3},{3,2},{4,5},{5,4},{6,7},{7,6},{8,9},{9,8},{10,11... | collective-permute-start | bytes 196616 | tf_op jit(solution)/shard_map/ppermute | solution.py:726
  71.7 5.6 %collective-permute-start.21 = (f32[272,128]{1,0:T(8,128)S(1)}, f32[272,128]{1,0:T(8,128)S(1)}, u32[]{:S(2)}, u32[]{:S(2)}) collective-permute-start(f32[272,128]{1,0:T(8,128)S(1)} %get-tuple-element.80), channel_id=1, source_target_pairs={{0,8},{4,12},{8,0},{12,4},{1,9},{5,13},{9,1},{13,5},{2,10},{6,14},... | collective-permute-start | bytes 417800 | tf_op jit(solution)/shard_map/ppermute | solution.py:726
  73.4 6.0 %collective-permute-start.22 = (f32[272,128]{1,0:T(8,128)S(1)}, f32[272,128]{1,0:T(8,128)S(1)}, u32[]{:S(2)}, u32[]{:S(2)}) collective-permute-start(f32[272,128]{1,0:T(8,128)S(1)} %get-tuple-element.81), channel_id=1, source_target_pairs={{0,12},{4,8},{8,4},{12,0},{1,13},{5,9},{9,5},{13,1},{2,14},{6,10},... | collective-permute-start | bytes 417800 | tf_op jit(solution)/shard_map/ppermute | solution.py:726
  73.4 6.0 %collective-permute-start.23 = (f32[272,128]{1,0:T(8,128)S(1)}, f32[272,128]{1,0:T(8,128)S(1)}, u32[]{:S(2)}, u32[]{:S(2)}) collective-permute-start(f32[272,128]{1,0:T(8,128)S(1)} %get-tuple-element.82), channel_id=1, source_target_pairs={{0,4},{4,0},{8,12},{12,8},{1,5},{5,1},{9,13},{13,9},{2,6},{6,2},{1... | collective-permute-start | bytes 417800 | tf_op jit(solution)/shard_map/ppermute | solution.py:726
  (4 other events, 109.3 us)

commit v6 on v5

--- a/solution.py
+++ b/solution.py
@@ -425,38 +425,38 @@
     field_ref,
     table_ref,
     rows_ref,
-    point_ref,
     back_ref,
     modes_ref,
     cells_ref,
     spread_ref,
     *refs,
 ):
-    out_refs, refs = refs[:-11], refs[-11:]
-    depth, mixing_ref, table, back, to_modes, to_cells, spread, field, rows, point, gates = refs
+    out_refs, refs = refs[:-9], refs[-9:]
+    depth, table, back, to_modes, to_cells, spread, field, rows, gates = refs
     device = device_index()
     half = field.shape[0] // 2
-    pairs = [(rows_ref, rows), (point_ref, point), (table_ref.at[device], table)]
+    pairs = [(rows_ref, rows), (table_ref.at[device], table)]
     for part in range(2):
         block = pl.ds(part * half, half)
         pairs.append((field_ref.at[block], field.at[block]))
+    needed = len(pairs)
     pairs += [(back_ref.at[device], back), (modes_ref, to_modes), (cells_ref, to_cells)]
     pairs += [(spread_ref, spread)]
     copies = [
         pltpu.make_async_copy(source, target, gates.at[turn])
         for turn, (source, target) in enumerate(pairs)
     ]
-    for copy in copies:
+    for copy in copies[:needed]:
         copy.start()
     copies[0].wait()
     fill_depth(rows, depth)
-    copies[1].wait()
-    mixing_ref[...] = mixing_matrix(point)
-    for copy in copies[2:5]:
+    for copy in copies[1:needed]:
         copy.wait()
+    for copy in copies[needed:]:
+        copy.start()
     planes = y_spectrum(field[...], table[...], rows_x, rows_y)
     z_spectrum(halved(planes, depth[...], (1, 0)), out_refs, rows_x)
-    for copy in copies[5:]:
+    for copy in copies[needed:]:
         copy.wait()
 
 
@@ -547,7 +547,8 @@
     return jnp.where(keep, values, 0.0)
 
 
-def point_kernel(field_ref, mixing_ref, bias_ref, out_ref):
+def point_kernel(field_ref, point_ref, bias_ref, out_ref, mixing_ref):
+    mixing_ref[...] = mixing_matrix(point_ref)
     bias = jnp.concatenate([bias_ref[...]] * NZ, axis=1)
     out_ref[...] = mixed(field_ref[...], mixing_ref[...], ((1,), (0,))) + bias
 
@@ -669,16 +670,21 @@
 
 def last_kernel(rows_x, rows_y, turns, scale, mixed_ref, back_ref, depth_ref, *refs):
     in_refs = unqueued(refs[:turns], INVERSE_X)
-    out_ref, point_ref, bias_ref, result, gates = refs[turns:]
+    out_ref, point_ref, bias_ref, result, point, columns, gates, sum_gates = refs[turns:]
     total = functools.reduce(jnp.add, [ref[ref.shape[0] - SUM_ROWS :, :] for ref in in_refs])
     total = total * scale
     packed = total[:8]
     for part in range(4):
         piece = packed if part == 0 else pltpu.roll(packed, LANES - part * C, 1)
-        point_ref[part * 8 : (part + 1) * 8, :] = piece[:, :C]
-    bias_ref[...] = total[8:9, :C]
+        point[part * 8 : (part + 1) * 8, :] = piece[:, :C]
+    columns[...] = total[8:9, :C]
+    stores = [
+        pltpu.make_async_copy(point, point_ref, sum_gates.at[0]),
+        pltpu.make_async_copy(columns, bias_ref, sum_gates.at[1]),
+    ]
+    for store in stores:
+        store.start()
     planes = z_synthesis(in_refs, depth_ref, rows_x, exact=False)
-    stores = []
     for x in range(rows_x):
         block = slice(x * rows_y, (x + 1) * rows_y)
         spectral = y_synthesis(planes, back_ref[...], x, rows_x)
@@ -767,21 +773,22 @@
         )(to_cells, *queued(received, INVERSE_Y), *extra)
         return queued(exchange(sent, "gx"), INVERSE_X)
 
-    *blocks, depth_table, mixing, table, back, to_modes, to_cells, spread = call(
+    *blocks, depth_table, table, back, to_modes, to_cells, spread = call(
         functools.partial(first_kernel, rows_x, rows_y),
-        [False] * 8,
+        [False] * 7,
         [cell_block] * x_parts
-        + [((depth, 2 * WIDE), BF, True), ((8 * C, 8 * C), BF, True)]
+        + [((depth, 2 * WIDE), BF, True)]
         + [(part.shape[1:], BF, True) for part in (forward_y, inverse_y)]
         + [(part.shape, BF, True) for part in (forward_x, inverse_x, spread_hits)],
         [
             pltpu.VMEM((cells, depth), BF),
             pltpu.VMEM(z_rows.shape, F32),
-            pltpu.VMEM((C, C), BF),
-            pltpu.SemaphoreType.DMA((9,)),
+            pltpu.SemaphoreType.DMA((8,)),
         ],
-    )(field, forward_y, z_rows, point_weight, inverse_y, forward_x, inverse_x, spread_hits)
-    (base,) = call(point_kernel, [True] * 3, [cell_shape])(field, mixing, bias)
+    )(field, forward_y, z_rows, inverse_y, forward_x, inverse_x, spread_hits)
+    base, mixing = call(point_kernel, [True] * 3, [cell_shape, ((8 * C, 8 * C), BF, True)])(
+        field, point_weight, bias
+    )
     block, field_modes = call(
         functools.partial(product_kernel, y_parts),
         [True] * (2 + y_parts),
@@ -819,8 +826,14 @@
     grad_field, grad_point, grad_bias = call(
         functools.partial(last_kernel, rows_x, rows_y, x_parts, scale),
         [True] * (3 + x_parts),
-        [((cells, depth), BF, False), ((C, C), F32, None), ((1, C), F32, None)],
-        [pltpu.VMEM((cells, depth), BF), pltpu.SemaphoreType.DMA((rows_x,))],
+        [((cells, depth), BF, False), ((C, C), F32, False), ((1, C), F32, False)],
+        [
+            pltpu.VMEM((cells, depth), BF),
+            pltpu.VMEM((C, C), F32),
+            pltpu.VMEM((1, C), F32),
+            pltpu.SemaphoreType.DMA((rows_x,)),
+            pltpu.SemaphoreType.DMA((2,)),
+        ],
     )(mixed_adjoint, back, depth_table, *inverse(block, [sums], cell_sums))
     return (
         grad_field.reshape(field_input.shape),

time: 82.1 us -> 81.2 us (0.989)
  transfers between devices with their start and end apart: 24 -> 24, of which waited for: 16 -> 16; matrix products, arithmetic and copies ran while one was open for 0% -> 0% of each run, Pallas kernels for 5% -> 6%
where the time goes in v6:
time: 81.2 us; the launch traced here: 81 us
  waiting for transfers between devices  36.6 us (45%)
  starting transfers between devices  27.7 us (34%)
  Pallas kernels  16 us (20%)
    ppermute x24, waiting for transfers between devices, exchange(): received[turn] = lax.ppermute(blocks[turn], axis, pairs)  36.6 us
    ppermute x24, starting transfers between devices, exchange(): received[turn] = lax.ppermute(blocks[turn], axis, pairs)  27.7 us
    pallas_call x12, Pallas kernels, run(): return function(*map(pltpu.with_memory_space_constraint, arguments, spaces))  16 us
  transfers between devices with their start and end apart: 24, of which 16 were waited for; matrix products, arithmetic and copies ran while one was open for 0% of the time, Pallas kernels for 6%

profile of v6, /device:TPU:0, one launch (start us, length us, event | category | flops | bytes accessed | tf_op | source)
XLA Modules:
  0.0 81.0 jit_solution(15382912519953593446)
XLA Ops:
  0.7 3.1 %shard_map.139 = (f32[256,128]{1,0:T(8,128)S(1)}, f32[256,128]{1,0:T(8,128)S(1)}, f32[256,128]{1,0:T(8,128)S(1)}, f32[256,128]{1,0:T(8,128)S(1)}, bf16[1024,1024...) custom-call(bf16[512,1024]{1,0:T(8,128)(2,1)} %bitcast.5, ...), custom_call_target="tpu_custom_call" | custom-call | tf_op jit(solution)/shard_map/pallas_call | solution.py:721
  3.8 3.0 %collective-permute-start = (f32[256,128]{1,0:T(8,128)S(1)}, f32[256,128]{1,0:T(8,128)S(1)}, u32[]{:S(2)}, u32[]{:S(2)}) collective-permute-start(f32[256,128]{1,0:T(8,128)S(1)} %get-tuple-element.55), channel_id=1, source_target_pairs={{0,8},{4,12},{8,0},{12,4},{1,9},{5,13},{9,1},{13,5},{2,10},{6,14},... | collective-permute-start | bytes 393224 | tf_op jit(solution)/shard_map/ppermute | solution.py:732
  7.0 3.7 %collective-permute-done.refs_1_ = f32[256,128]{1,0:T(8,128)S(1)} collective-permute-done((f32[256,128]{1,0:T(8,128)S(1)}, f32[256,128]{1,0:T(8,128)S(1)}, u32[]{:S(2)}, u32[]{:S(2)}) %collective-permute-start) | collective-permute-done | bytes 131104 | tf_op jit(solution)/shard_map/ppermute | solution.py:732
  10.7 1.9 %collective-permute-done.2.refs_3_ = f32[256,128]{1,0:T(8,128)S(1)} collective-permute-done((f32[256,128]{1,0:T(8,128)S(1)}, f32[256,128]{1,0:T(8,128)S(1)}, u32[]{:S(2)}, u32[]{:S(2)}) %collective-permute-start.2) | collective-permute-done | bytes 131104 | tf_op jit(solution)/shard_map/ppermute | solution.py:732
  14.5 2.6 %collective-permute-start.4 = (f32[128,128]{1,0:T(8,128)S(1)}, f32[128,128]{1,0:T(8,128)S(1)}, u32[]{:S(2)}, u32[]{:S(2)}) collective-permute-start(f32[128,128]{1,0:T(8,128)S(1)} %get-tuple-element.60), channel_id=1, source_target_pairs={{0,2},{1,3},{2,0},{3,1},{4,6},{5,7},{6,4},{7,5},{8,10},{9,11},{10,... | collective-permute-start | bytes 196616 | tf_op jit(solution)/shard_map/ppermute | solution.py:732
  17.4 4.1 %collective-permute-done.4.refs_2_ = f32[128,128]{1,0:T(8,128)S(1)} collective-permute-done((f32[128,128]{1,0:T(8,128)S(1)}, f32[128,128]{1,0:T(8,128)S(1)}, u32[]{:S(2)}, u32[]{:S(2)}) %collective-permute-start.4) | collective-permute-done | bytes 65568 | tf_op jit(solution)/shard_map/ppermute | solution.py:732
  21.5 1.8 %collective-permute-done.5.refs_3_ = f32[128,128]{1,0:T(8,128)S(1)} collective-permute-done((f32[128,128]{1,0:T(8,128)S(1)}, f32[128,128]{1,0:T(8,128)S(1)}, u32[]{:S(2)}, u32[]{:S(2)}) %collective-permute-start.5) | collective-permute-done | bytes 65568 | tf_op jit(solution)/shard_map/ppermute | solution.py:732
  24.0 2.5 %collective-permute-start.8 = (f32[128,128]{1,0:T(8,128)S(1)}, f32[128,128]{1,0:T(8,128)S(1)}, u32[]{:S(2)}, u32[]{:S(2)}) collective-permute-start(f32[128,128]{1,0:T(8,128)S(1)} %get-tuple-element.62.refs_0_), channel_id=1, source_target_pairs={{0,3},{1,2},{2,1},{3,0},{4,7},{5,6},{6,5},{7,4},{8,11},{9,10},{10,... | collective-permute-start | bytes 196616 | tf_op jit(solution)/shard_map/ppermute | solution.py:732
  28.5 2.4 %collective-permute-done.8.refs_3_ = f32[128,128]{1,0:T(8,128)S(1)} collective-permute-done((f32[128,128]{1,0:T(8,128)S(1)}, f32[128,128]{1,0:T(8,128)S(1)}, u32[]{:S(2)}, u32[]{:S(2)}) %collective-permute-start.8) | collective-permute-done | bytes 65568 | tf_op jit(solution)/shard_map/ppermute | solution.py:732
  30.8 1.9 %collective-permute-done.7.refs_2_ = f32[128,128]{1,0:T(8,128)S(1)} collective-permute-done((f32[128,128]{1,0:T(8,128)S(1)}, f32[128,128]{1,0:T(8,128)S(1)}, u32[]{:S(2)}, u32[]{:S(2)}) %collective-permute-start.7) | collective-permute-done | bytes 65568 | tf_op jit(solution)/shard_map/ppermute | solution.py:732
  33.0 1.8 %collective-permute-start.9 = (f32[256,128]{1,0:T(8,128)S(1)}, f32[256,128]{1,0:T(8,128)S(1)}, u32[]{:S(2)}, u32[]{:S(2)}) collective-permute-start(f32[256,128]{1,0:T(8,128)S(1)} %get-tuple-element.64), channel_id=1, source_target_pairs={{0,8},{4,12},{8,0},{12,4},{1,9},{5,13},{9,1},{13,5},{2,10},{6,14},... | collective-permute-start | bytes 393224 | tf_op jit(solution)/shard_map/ppermute | solution.py:732
  35.9 2.9 %collective-permute-done.9.refs_1_ = f32[256,128]{1,0:T(8,128)S(1)} collective-permute-done((f32[256,128]{1,0:T(8,128)S(1)}, f32[256,128]{1,0:T(8,128)S(1)}, u32[]{:S(2)}, u32[]{:S(2)}) %collective-permute-start.9) | collective-permute-done | bytes 131104 | tf_op jit(solution)/shard_map/ppermute | solution.py:732
  38.8 1.9 %collective-permute-done.10.refs_2_ = f32[256,128]{1,0:T(8,128)S(1)} collective-permute-done((f32[256,128]{1,0:T(8,128)S(1)}, f32[256,128]{1,0:T(8,128)S(1)}, u32[]{:S(2)}, u32[]{:S(2)}) %collective-permute-start.10) | collective-permute-done | bytes 131104 | tf_op jit(solution)/shard_map/ppermute | solution.py:732
  40.7 3.6 %shard_map.143 = (f32[256,128]{1,0:T(8,128)S(1)}, f32[256,128]{1,0:T(8,128)S(1)}, f32[256,128]{1,0:T(8,128)S(1)}, f32[256,128]{1,0:T(8,128)S(1)}, bf16[512,1024]{1,0:T(8,128)(2,1)S(1)}) custom-call(f32[512,1024]{1,0:T(8,128)S(1)} %get-tuple-element.47.base_ref, bf16[512,1024]{1,0:T(8,128)(2,1)S(1)} %bitcast.8, ...), custom_call_target="tpu_custom_call" | custom-call | tf_op jit(solution)/shard_map/pallas_call | solution.py:721
  47.6 3.2 %collective-permute-done.12.refs_1_ = f32[256,128]{1,0:T(8,128)S(1)} collective-permute-done((f32[256,128]{1,0:T(8,128)S(1)}, f32[256,128]{1,0:T(8,128)S(1)}, u32[]{:S(2)}, u32[]{:S(2)}) %collective-permute-start.12) | collective-permute-done | bytes 131104 | tf_op jit(solution)/shard_map/ppermute | solution.py:732
  52.4 2.8 %collective-permute-start.16 = (f32[144,128]{1,0:T(8,128)S(1)}, f32[144,128]{1,0:T(8,128)S(1)}, u32[]{:S(2)}, u32[]{:S(2)}) collective-permute-start(f32[144,128]{1,0:T(8,128)S(1)} %get-tuple-element.77), channel_id=1, source_target_pairs={{0,2},{1,3},{2,0},{3,1},{4,6},{5,7},{6,4},{7,5},{8,10},{9,11},{10,... | collective-permute-start | bytes 221192 | tf_op jit(solution)/shard_map/ppermute | solution.py:732
  56.7 1.7 %collective-permute-done.15.refs_1_ = f32[144,128]{1,0:T(8,128)S(1)} collective-permute-done((f32[144,128]{1,0:T(8,128)S(1)}, f32[144,128]{1,0:T(8,128)S(1)}, u32[]{:S(2)}, u32[]{:S(2)}) %collective-permute-start.15) | collective-permute-done | bytes 73760 | tf_op jit(solution)/shard_map/ppermute | solution.py:732
  58.3 3.3 %collective-permute-done.16.refs_2_ = f32[144,128]{1,0:T(8,128)S(1)} collective-permute-done((f32[144,128]{1,0:T(8,128)S(1)}, f32[144,128]{1,0:T(8,128)S(1)}, u32[]{:S(2)}, u32[]{:S(2)}) %collective-permute-start.16) | collective-permute-done | bytes 73760 | tf_op jit(solution)/shard_map/ppermute | solution.py:732
  62.4 2.6 %collective-permute-start.20 = (f32[128,128]{1,0:T(8,128)S(1)}, f32[128,128]{1,0:T(8,128)S(1)}, u32[]{:S(2)}, u32[]{:S(2)}) collective-permute-start(f32[128,128]{1,0:T(8,128)S(1)} %get-tuple-element.79.refs_0_), channel_id=1, source_target_pairs={{0,3},{1,2},{2,1},{3,0},{4,7},{5,6},{6,5},{7,4},{8,11},{9,10},{10,... | collective-permute-start | bytes 196616 | tf_op jit(solution)/shard_map/ppermute | solution.py:732
  66.9 2.2 %collective-permute-done.20.refs_3_ = f32[128,128]{1,0:T(8,128)S(1)} collective-permute-done((f32[128,128]{1,0:T(8,128)S(1)}, f32[128,128]{1,0:T(8,128)S(1)}, u32[]{:S(2)}, u32[]{:S(2)}) %collective-permute-start.20) | collective-permute-done | bytes 65568 | tf_op jit(solution)/shard_map/ppermute | solution.py:732
  69.1 2.1 %collective-permute-done.19.refs_2_ = f32[128,128]{1,0:T(8,128)S(1)} collective-permute-done((f32[128,128]{1,0:T(8,128)S(1)}, f32[128,128]{1,0:T(8,128)S(1)}, u32[]{:S(2)}, u32[]{:S(2)}) %collective-permute-start.19) | collective-permute-done | bytes 65568 | tf_op jit(solution)/shard_map/ppermute | solution.py:732
  73.7 2.8 %shard_map.149 = f32[16,32768]{1,0:T(8,128)} custom-call(f32[32,512]{1,0:T(8,128)S(1)} %get-tuple-element.86.field_ref, f32[32,512]{1,0:T(8,128)S(1)} %get-tuple-element.87.adjoint_ref), custom_call_target="tpu_custom_call" | custom-call | tf_op jit(solution)/shard_map/pallas_call | solution.py:721
  77.1 1.9 %collective-permute-done.22.refs_2_ = f32[272,128]{1,0:T(8,128)S(1)} collective-permute-done((f32[272,128]{1,0:T(8,128)S(1)}, f32[272,128]{1,0:T(8,128)S(1)}, u32[]{:S(2)}, u32[]{:S(2)}) %collective-permute-start.22) | collective-permute-done | bytes 139296 | tf_op jit(solution)/shard_map/ppermute | solution.py:732
  79.1 2.0 %shard_map.148 = (bf16[512,1024]{1,0:T(8,128)(2,1)}, f32[32,32]{1,0:T(8,128)}, f32[1,32]{1,0:T(1,128)}) custom-call(f32[512,1024]{1,0:T(8,128)S(1)} %get-tuple-element.69.mixed_ref, bf16[64,96]{1,0:T(8,128)(2,1)S(1)} %get-tuple-element.49.back_ref, bf16[1024,1024]{1,0:T(8,128)(2,1)S(1)} %get-tuple-element.50.depth_ref, ...), custom_call_target="tpu_custom_call" | custom-call | tf_op jit(solution)/shard_map/pallas_call | solution.py:721
  (46 shorter events, 18.7 us)
Async XLA Ops:
  3.8 7.0 %collective-permute-start = (f32[256,128]{1,0:T(8,128)S(1)}, f32[256,128]{1,0:T(8,128)S(1)}, u32[]{:S(2)}, u32[]{:S(2)}) collective-permute-start(f32[256,128]{1,0:T(8,128)S(1)} %get-tuple-element.55), channel_id=1, source_target_pairs={{0,8},{4,12},{8,0},{12,4},{1,9},{5,13},{9,1},{13,5},{2,10},{6,14},... | collective-permute-start | bytes 393224 | tf_op jit(solution)/shard_map/ppermute | solution.py:732
  6.8 3.9 %collective-permute-start.1 = (f32[256,128]{1,0:T(8,128)S(1)}, f32[256,128]{1,0:T(8,128)S(1)}, u32[]{:S(2)}, u32[]{:S(2)}) collective-permute-start(f32[256,128]{1,0:T(8,128)S(1)} %get-tuple-element.56), channel_id=1, source_target_pairs={{0,4},{4,0},{8,12},{12,8},{1,5},{5,1},{9,13},{13,9},{2,6},{6,2},{1... | collective-permute-start | bytes 393224 | tf_op jit(solution)/shard_map/ppermute | solution.py:732
  6.8 5.9 %collective-permute-start.2 = (f32[256,128]{1,0:T(8,128)S(1)}, f32[256,128]{1,0:T(8,128)S(1)}, u32[]{:S(2)}, u32[]{:S(2)}) collective-permute-start(f32[256,128]{1,0:T(8,128)S(1)} %get-tuple-element.57), channel_id=1, source_target_pairs={{0,12},{4,8},{8,4},{12,0},{1,13},{5,9},{9,5},{13,1},{2,14},{6,10},... | collective-permute-start | bytes 393224 | tf_op jit(solution)/shard_map/ppermute | solution.py:732
  13.0 4.5 %collective-permute-start.3 = (f32[128,128]{1,0:T(8,128)S(1)}, f32[128,128]{1,0:T(8,128)S(1)}, u32[]{:S(2)}, u32[]{:S(2)}) collective-permute-start(f32[128,128]{1,0:T(8,128)S(1)} %get-tuple-element.59), channel_id=1, source_target_pairs={{0,1},{1,0},{2,3},{3,2},{4,5},{5,4},{6,7},{7,6},{8,9},{9,8},{10,11... | collective-permute-start | bytes 196616 | tf_op jit(solution)/shard_map/ppermute | solution.py:732
  14.5 6.9 %collective-permute-start.4 = (f32[128,128]{1,0:T(8,128)S(1)}, f32[128,128]{1,0:T(8,128)S(1)}, u32[]{:S(2)}, u32[]{:S(2)}) collective-permute-start(f32[128,128]{1,0:T(8,128)S(1)} %get-tuple-element.60), channel_id=1, source_target_pairs={{0,2},{1,3},{2,0},{3,1},{4,6},{5,7},{6,4},{7,5},{8,10},{9,11},{10,... | collective-permute-start | bytes 196616 | tf_op jit(solution)/shard_map/ppermute | solution.py:732
  17.1 6.1 %collective-permute-start.5 = (f32[128,128]{1,0:T(8,128)S(1)}, f32[128,128]{1,0:T(8,128)S(1)}, u32[]{:S(2)}, u32[]{:S(2)}) collective-permute-start(f32[128,128]{1,0:T(8,128)S(1)} %get-tuple-element.61), channel_id=1, source_target_pairs={{0,3},{1,2},{2,1},{3,0},{4,7},{5,6},{6,5},{7,4},{8,11},{9,10},{10,... | collective-permute-start | bytes 196616 | tf_op jit(solution)/shard_map/ppermute | solution.py:732
  24.0 6.8 %collective-permute-start.8 = (f32[128,128]{1,0:T(8,128)S(1)}, f32[128,128]{1,0:T(8,128)S(1)}, u32[]{:S(2)}, u32[]{:S(2)}) collective-permute-start(f32[128,128]{1,0:T(8,128)S(1)} %get-tuple-element.62.refs_0_), channel_id=1, source_target_pairs={{0,3},{1,2},{2,1},{3,0},{4,7},{5,6},{6,5},{7,4},{8,11},{9,10},{10,... | collective-permute-start | bytes 196616 | tf_op jit(solution)/shard_map/ppermute | solution.py:732
  26.5 6.2 %collective-permute-start.7 = (f32[128,128]{1,0:T(8,128)S(1)}, f32[128,128]{1,0:T(8,128)S(1)}, u32[]{:S(2)}, u32[]{:S(2)}) collective-permute-start(f32[128,128]{1,0:T(8,128)S(1)} %get-tuple-element.62.refs_0_), channel_id=1, source_target_pairs={{0,2},{1,3},{2,0},{3,1},{4,6},{5,7},{6,4},{7,5},{8,10},{9,11},{10,... | collective-permute-start | bytes 196616 | tf_op jit(solution)/shard_map/ppermute | solution.py:732
  26.8 5.9 %collective-permute-start.6 = (f32[128,128]{1,0:T(8,128)S(1)}, f32[128,128]{1,0:T(8,128)S(1)}, u32[]{:S(2)}, u32[]{:S(2)}) collective-permute-start(f32[128,128]{1,0:T(8,128)S(1)} %get-tuple-element.62.refs_0_), channel_id=1, source_target_pairs={{0,1},{1,0},{2,3},{3,2},{4,5},{5,4},{6,7},{7,6},{8,9},{9,8},{10,11... | collective-permute-start | bytes 196616 | tf_op jit(solution)/shard_map/ppermute | solution.py:732
  33.0 5.8 %collective-permute-start.9 = (f32[256,128]{1,0:T(8,128)S(1)}, f32[256,128]{1,0:T(8,128)S(1)}, u32[]{:S(2)}, u32[]{:S(2)}) collective-permute-start(f32[256,128]{1,0:T(8,128)S(1)} %get-tuple-element.64), channel_id=1, source_target_pairs={{0,8},{4,12},{8,0},{12,4},{1,9},{5,13},{9,1},{13,5},{2,10},{6,14},... | collective-permute-start | bytes 393224 | tf_op jit(solution)/shard_map/ppermute | solution.py:732
  34.9 5.8 %collective-permute-start.10 = (f32[256,128]{1,0:T(8,128)S(1)}, f32[256,128]{1,0:T(8,128)S(1)}, u32[]{:S(2)}, u32[]{:S(2)}) collective-permute-start(f32[256,128]{1,0:T(8,128)S(1)} %get-tuple-element.65), channel_id=1, source_target_pairs={{0,12},{4,8},{8,4},{12,0},{1,13},{5,9},{9,5},{13,1},{2,14},{6,10},... | collective-permute-start | bytes 393224 | tf_op jit(solution)/shard_map/ppermute | solution.py:732
  34.9 5.8 %collective-permute-start.11 = (f32[256,128]{1,0:T(8,128)S(1)}, f32[256,128]{1,0:T(8,128)S(1)}, u32[]{:S(2)}, u32[]{:S(2)}) collective-permute-start(f32[256,128]{1,0:T(8,128)S(1)} %get-tuple-element.66), channel_id=1, source_target_pairs={{0,4},{4,0},{8,12},{12,8},{1,5},{5,1},{9,13},{13,9},{2,6},{6,2},{1... | collective-permute-start | bytes 393224 | tf_op jit(solution)/shard_map/ppermute | solution.py:732
  44.3 6.4 %collective-permute-start.12 = (f32[256,128]{1,0:T(8,128)S(1)}, f32[256,128]{1,0:T(8,128)S(1)}, u32[]{:S(2)}, u32[]{:S(2)}) collective-permute-start(f32[256,128]{1,0:T(8,128)S(1)} %get-tuple-element.71), channel_id=1, source_target_pairs={{0,8},{4,12},{8,0},{12,4},{1,9},{5,13},{9,1},{13,5},{2,10},{6,14},... | collective-permute-start | bytes 393224 | tf_op jit(solution)/shard_map/ppermute | solution.py:732
  45.0 5.8 %collective-permute-start.13 = (f32[256,128]{1,0:T(8,128)S(1)}, f32[256,128]{1,0:T(8,128)S(1)}, u32[]{:S(2)}, u32[]{:S(2)}) collective-permute-start(f32[256,128]{1,0:T(8,128)S(1)} %get-tuple-element.72), channel_id=1, source_target_pairs={{0,4},{4,0},{8,12},{12,8},{1,5},{5,1},{9,13},{13,9},{2,6},{6,2},{1... | collective-permute-start | bytes 393224 | tf_op jit(solution)/shard_map/ppermute | solution.py:732
  45.9 6.0 %collective-permute-start.14 = (f32[256,128]{1,0:T(8,128)S(1)}, f32[256,128]{1,0:T(8,128)S(1)}, u32[]{:S(2)}, u32[]{:S(2)}) collective-permute-start(f32[256,128]{1,0:T(8,128)S(1)} %get-tuple-element.73), channel_id=1, source_target_pairs={{0,12},{4,8},{8,4},{12,0},{1,13},{5,9},{9,5},{13,1},{2,14},{6,10},... | collective-permute-start | bytes 393224 | tf_op jit(solution)/shard_map/ppermute | solution.py:732
  52.2 6.2 %collective-permute-start.15 = (f32[144,128]{1,0:T(8,128)S(1)}, f32[144,128]{1,0:T(8,128)S(1)}, u32[]{:S(2)}, u32[]{:S(2)}) collective-permute-start(f32[144,128]{1,0:T(8,128)S(1)} %get-tuple-element.76), channel_id=1, source_target_pairs={{0,1},{1,0},{2,3},{3,2},{4,5},{5,4},{6,7},{7,6},{8,9},{9,8},{10,11... | collective-permute-start | bytes 221192 | tf_op jit(solution)/shard_map/ppermute | solution.py:732
  52.4 9.2 %collective-permute-start.16 = (f32[144,128]{1,0:T(8,128)S(1)}, f32[144,128]{1,0:T(8,128)S(1)}, u32[]{:S(2)}, u32[]{:S(2)}) collective-permute-start(f32[144,128]{1,0:T(8,128)S(1)} %get-tuple-element.77), channel_id=1, source_target_pairs={{0,2},{1,3},{2,0},{3,1},{4,6},{5,7},{6,4},{7,5},{8,10},{9,11},{10,... | collective-permute-start | bytes 221192 | tf_op jit(solution)/shard_map/ppermute | solution.py:732
  55.2 6.4 %collective-permute-start.17 = (f32[144,128]{1,0:T(8,128)S(1)}, f32[144,128]{1,0:T(8,128)S(1)}, u32[]{:S(2)}, u32[]{:S(2)}) collective-permute-start(f32[144,128]{1,0:T(8,128)S(1)} %get-tuple-element.78), channel_id=1, source_target_pairs={{0,3},{1,2},{2,1},{3,0},{4,7},{5,6},{6,5},{7,4},{8,11},{9,10},{10,... | collective-permute-start | bytes 221192 | tf_op jit(solution)/shard_map/ppermute | solution.py:732
  62.4 6.7 %collective-permute-start.20 = (f32[128,128]{1,0:T(8,128)S(1)}, f32[128,128]{1,0:T(8,128)S(1)}, u32[]{:S(2)}, u32[]{:S(2)}) collective-permute-start(f32[128,128]{1,0:T(8,128)S(1)} %get-tuple-element.79.refs_0_), channel_id=1, source_target_pairs={{0,3},{1,2},{2,1},{3,0},{4,7},{5,6},{6,5},{7,4},{8,11},{9,10},{10,... | collective-permute-start | bytes 196616 | tf_op jit(solution)/shard_map/ppermute | solution.py:732
  65.0 6.2 %collective-permute-start.19 = (f32[128,128]{1,0:T(8,128)S(1)}, f32[128,128]{1,0:T(8,128)S(1)}, u32[]{:S(2)}, u32[]{:S(2)}) collective-permute-start(f32[128,128]{1,0:T(8,128)S(1)} %get-tuple-element.79.refs_0_), channel_id=1, source_target_pairs={{0,2},{1,3},{2,0},{3,1},{4,6},{5,7},{6,4},{7,5},{8,10},{9,11},{10,... | collective-permute-start | bytes 196616 | tf_op jit(solution)/shard_map/ppermute | solution.py:732
  65.7 5.4 %collective-permute-start.18 = (f32[128,128]{1,0:T(8,128)S(1)}, f32[128,128]{1,0:T(8,128)S(1)}, u32[]{:S(2)}, u32[]{:S(2)}) collective-permute-start(f32[128,128]{1,0:T(8,128)S(1)} %get-tuple-element.79.refs_0_), channel_id=1, source_target_pairs={{0,1},{1,0},{2,3},{3,2},{4,5},{5,4},{6,7},{7,6},{8,9},{9,8},{10,11... | collective-permute-start | bytes 196616 | tf_op jit(solution)/shard_map/ppermute | solution.py:732
  71.5 5.7 %collective-permute-start.21 = (f32[272,128]{1,0:T(8,128)S(1)}, f32[272,128]{1,0:T(8,128)S(1)}, u32[]{:S(2)}, u32[]{:S(2)}) collective-permute-start(f32[272,128]{1,0:T(8,128)S(1)} %get-tuple-element.82), channel_id=1, source_target_pairs={{0,8},{4,12},{8,0},{12,4},{1,9},{5,13},{9,1},{13,5},{2,10},{6,14},... | collective-permute-start | bytes 417800 | tf_op jit(solution)/shard_map/ppermute | solution.py:732
  73.1 6.0 %collective-permute-start.22 = (f32[272,128]{1,0:T(8,128)S(1)}, f32[272,128]{1,0:T(8,128)S(1)}, u32[]{:S(2)}, u32[]{:S(2)}) collective-permute-start(f32[272,128]{1,0:T(8,128)S(1)} %get-tuple-element.83), channel_id=1, source_target_pairs={{0,12},{4,8},{8,4},{12,0},{1,13},{5,9},{9,5},{13,1},{2,14},{6,10},... | collective-permute-start | bytes 417800 | tf_op jit(solution)/shard_map/ppermute | solution.py:732
  73.1 6.0 %collective-permute-start.23 = (f32[272,128]{1,0:T(8,128)S(1)}, f32[272,128]{1,0:T(8,128)S(1)}, u32[]{:S(2)}, u32[]{:S(2)}) collective-permute-start(f32[272,128]{1,0:T(8,128)S(1)} %get-tuple-element.84), channel_id=1, source_target_pairs={{0,4},{4,0},{8,12},{12,8},{1,5},{5,1},{9,13},{13,9},{2,6},{6,2},{1... | collective-permute-start | bytes 417800 | tf_op jit(solution)/shard_map/ppermute | solution.py:732
  (5 other events, 163.3 us)
